TPU v7x, 32 devices: a whole 2x2x4 slice. The times are simulated.
32 devices in a mesh: grp: 8 (over y, x, core), tile: 4 (over z).
Axes of the slice: x: 2, y: 2, z: 4, core: 2. Of those that a mesh axis runs over, the one named last changes fastest.
Arguments:
- coeff: bfloat16 [32, 256, 4096], P('grp', None, 'tile'), may hold values from -0.09375 to 0.09375
- energy: float32 [32, 4096], P('grp', 'tile'), may hold values from 1 to 3
- ranks: int32 [32, 32], replicated, may hold values from 32 to 256, as said below
- assign: int32 [1024], P(('grp', 'tile')), may hold values from 0 to 1023, each once
- screen: bfloat16 [1024, 256, 256], P(('grp', 'tile')), may hold values from -0.375 to 0.375
- initial: float32 [32, 8, 4096], P('grp', None, 'tile'), may hold values from -6 to 6
Outputs:
- rayleigh: float32 [2, 8, 8], replicated
- basis: float32 [32, 8, 4096], P('grp', None, 'tile')
- residual: float32 [32, 8, 4096], P('grp', None, 'tile')
Inputs may be any that keep to these rules, and one draw needn't show every extreme that they name: ranks is symmetric and its diagonal equals 256. `assign`: every pair index appears exactly once.
All inputs are finite; a program needn't handle non-finite values.
Results may differ from a plain program's by a relative error of at most 0.0075.
Values may be sent and summed in bfloat16 or wider, within the bound.
No kernel may reach another device: no remote copies, remote signals or barrier semaphores. Data moves between devices by JAX's collectives and lax.ppermute only.
A program may use at most 64 MiB of HBM per device.

v0:
```python
import jax
import jax.numpy as jnp
from jax import lax
from jax.sharding import PartitionSpec as P

ITERS = 2


def inner_sum(left, right):
    return jnp.einsum("knp,kmp->nm", left, right, precision=lax.Precision.HIGHEST)


def combine_rows(weights, block):
    return jnp.einsum("mn,kmp->knp", weights, block, precision=lax.Precision.HIGHEST)


def orthonormal(block, count):
    gram = lax.psum(inner_sum(block, block), ("grp", "tile")) / count
    lower = jnp.linalg.cholesky(gram)
    vectors = block.shape[1]
    inverse = lax.linalg.triangular_solve(
        lower, jnp.eye(vectors, dtype=jnp.float32), left_side=True, lower=True
    )
    return combine_rows(inverse.T, block)


def apply_kernel(block, coeff, energy, ranks, assign, screen):
    local_k, vectors, _ = block.shape
    levels_count = coeff.shape[1]
    block_b = block.astype(jnp.bfloat16)
    dens_part = jnp.einsum("knp,kgp->kng", block_b, coeff, preferred_element_type=jnp.float32)
    dens_local = lax.psum(dens_part, "tile")
    dens_b = lax.all_gather(dens_local.astype(jnp.bfloat16), "grp", axis=0, tiled=True)
    total_k = dens_b.shape[0]
    task_row = assign // total_k
    task_col = assign % total_k
    task_rank = ranks[task_row, task_col]
    levels = jnp.arange(levels_count, dtype=jnp.int32)
    keep = (levels[None, :] < task_rank[:, None]).astype(jnp.float32)
    task_dens = dens_b[task_col] * keep.astype(jnp.bfloat16)[:, None, :]
    task_out = jnp.einsum("tnh,tgh->tng", task_dens, screen, preferred_element_type=jnp.float32)
    task_out = task_out * keep[:, None, :]
    onehot = (task_row[None, :] == jnp.arange(total_k, dtype=jnp.int32)[:, None]).astype(
        jnp.float32
    )
    partial_rows = jnp.dot(
        onehot,
        task_out.reshape(task_out.shape[0], vectors * levels_count),
        precision=lax.Precision.HIGHEST,
    )
    summed_tile = lax.psum(partial_rows, "tile")
    owned = lax.psum_scatter(summed_tile, "grp", scatter_dimension=0, tiled=True)
    rows_b = owned.reshape(local_k, vectors, levels_count).astype(jnp.bfloat16)
    coupled = jnp.einsum("kng,kgp->knp", rows_b, coeff, preferred_element_type=jnp.float32)
    return energy[:, None, :] * block + coupled


def per_device(coeff, energy, ranks, assign, screen, initial):
    count = initial.shape[0] * lax.axis_size("grp") * initial.shape[2] * lax.axis_size("tile")
    basis = orthonormal(initial, count)
    collected = []
    residual = initial
    for step in range(ITERS):
        sigma = apply_kernel(basis, coeff, energy, ranks, assign, screen)
        scaled_energy = energy[:, None, :]
        first, second, third = lax.psum(
            (
                inner_sum(basis, sigma),
                inner_sum(basis, sigma / scaled_energy),
                inner_sum(basis, basis / scaled_energy),
            ),
            ("grp", "tile"),
        )
        projected = first / count
        correlation = second / count - jnp.dot(
            third / count, projected, precision=lax.Precision.HIGHEST
        )
        residual = sigma - combine_rows(projected, basis)
        precond = residual / scaled_energy
        collected.append(projected)
        direction = precond - combine_rows(correlation, basis)
        basis = orthonormal(direction, count)
    return (jnp.stack(collected), basis, residual)


def solution(mesh):
    placed = (
        P("grp", None, "tile"),
        P("grp", "tile"),
        P(),
        P(("grp", "tile")),
        P(("grp", "tile"), None, None),
        P("grp", None, "tile"),
    )
    return jax.shard_map(
        per_device,
        mesh=mesh,
        in_specs=placed,
        out_specs=(P(), P("grp", None, "tile"), P("grp", None, "tile")),
        check_vma=False,
    )
```

profile of v0, /device:TPU:0, one launch (start us, length us, event | category | flops | bytes accessed | tf_op | source)
XLA Modules:
  0.0 440.9 jit_solution(4244520324346047489)
XLA Ops:
  7.2 1.5 convolution_bitcast_fusion.18
  8.7 41.9 %psum.91 = f32[8,8]{0,1:T(8,128)S(1)} all-reduce(f32[8,8]{0,1:T(8,128)S(1)} %convolution_bitcast_fusion.18), channel_id=1, replica_groups=mesh['grp'=8,'tile'=4] {'grp','tile'}, use_global_device_ids=true, to_apply=%region_0.0 | all-reduce | flops 64 | bytes 512 | tf_op jit(solution)/shard_map/psum | solution.py:18
  50.7 0.7 cholesky.59
  51.5 0.6 compare_reduce_fusion.2
  52.1 0.6 fusion.36
  52.8 0.6 custom-call.9
  53.6 1.2 convolution_bitcast_fusion.6
  54.8 0.6 fusion.17
  55.4 17.9 %psum.92 = bf16[4,8,256]{2,1,0:T(8,128)(2,1)S(1)} all-reduce(f32[4,8,256]{2,1,0:T(8,128)S(1)} %fusion.17), channel_id=1, replica_groups=mesh['grp'=8,'tile'=4] {'tile'}, use_global_device_ids=true, to_apply=%region_3.6 | all-reduce | flops 8192 | bytes 49152 | tf_op jit(solution)/shard_map/psum | solution.py:32
  73.3 10.0 %all_gather.6 = bf16[32,8,256]{2,1,0:T(8,128)(2,1)S(1)} all-gather(bf16[4,8,256]{2,1,0:T(8,128)(2,1)S(1)} %psum.92), channel_id=1, replica_groups=mesh['grp'=8,'tile'=4] {'grp'}, dimensions={0}, use_global_device_ids=true | all-gather | bytes 147456 | tf_op jit(solution)/shard_map/all_gather | solution.py:33
  83.3 0.7 gather_fusion.1
  84.1 0.6 gather_fusion
  84.7 3.4 convolution_multiply_fusion.1
  88.2 1.0 fusion.29
  89.2 0.6 dynamic-slice
  90.5 0.4 convolution_bitcast_fusion.14
  90.8 49.6 %all-reduce.7.cloned.1.call-done = f32[32,2048]{1,0:T(8,128)} async-done(((f32[32,2048]{1,0:T(8,128)}), f32[32,2048]{1,0:T(8,128)}) %all-reduce.7.cloned.1.call-update) | async-done | bytes 262160
  140.4 0.8 constant_dynamic-slice_fusion.1
  141.3 19.0 %psum.104 = bf16[4,2048]{1,0:T(4,128)(2,1)S(1)} all-reduce(f32[4,2048]{1,0:T(4,128)S(1)} %constant_dynamic-slice_fusion.1), channel_id=1, replica_groups=mesh['grp'=8,'tile'=4] {'tile'}, use_global_device_ids=true, to_apply=%region_4.7 | all-reduce | flops 8192 | bytes 49152 | tf_op jit(solution)/shard_map/psum | solution.py:51
  160.3 0.4 convolution_add_fusion.1
  160.7 0.4 convolution_bitcast_fusion.15
  161.0 0.4 convolution_bitcast_fusion.16
  161.4 37.6 %all-reduce.3 = (f32[8,8]{0,1:T(8,128)S(1)}, f32[8,8]{0,1:T(8,128)S(1)}, f32[8,8]{0,1:T(8,128)S(1)}) all-reduce(f32[8,8]{0,1:T(8,128)S(1)} %convolution_bitcast_fusion.16, f32[8,8]{0,1:T(8,128)S(1)} %convolution_bitcast_fusion.14, f32[8,8]{0,1:T(8,128)S(1)} %convolution_bitcast_fusion.15), channel_id=1, replica_groups=mesh['grp'=8,'tile'=4] {'grp','tile'}, use_global_device_ids=true, to_apply=%region_6.9 | all-reduce | flops 192 | bytes 1536 | tf_op jit(solution)/shard_map/psum | solution.py:66
  200.1 41.1 %psum.97 = f32[8,8]{0,1:T(8,128)S(1)} all-reduce(f32[8,8]{0,1:T(8,128)S(1)} %convolution_bitcast_fusion.13), channel_id=1, replica_groups=mesh['grp'=8,'tile'=4] {'grp','tile'}, use_global_device_ids=true, to_apply=%region_9.12 | all-reduce | flops 64 | bytes 512 | tf_op jit(solution)/shard_map/psum | solution.py:18
  241.3 0.7 cholesky.70
  242.0 0.6 compare_reduce_fusion.1
  242.6 0.6 fusion.37
  243.3 0.6 custom-call.10
  244.4 0.6 fusion.13
  245.0 17.2 %psum.98 = bf16[4,8,256]{2,1,0:T(8,128)(2,1)S(1)} all-reduce(f32[4,8,256]{2,1,0:T(8,128)S(1)} %fusion.13), channel_id=1, replica_groups=mesh['grp'=8,'tile'=4] {'tile'}, use_global_device_ids=true, to_apply=%region_10.13 | all-reduce | flops 8192 | bytes 49152 | tf_op jit(solution)/shard_map/psum | solution.py:32
  262.3 10.0 %all_gather.7 = bf16[32,8,256]{2,1,0:T(8,128)(2,1)S(1)} all-gather(bf16[4,8,256]{2,1,0:T(8,128)(2,1)S(1)} %psum.98), channel_id=1, replica_groups=mesh['grp'=8,'tile'=4] {'grp'}, dimensions={0}, use_global_device_ids=true | all-gather | bytes 147456 | tf_op jit(solution)/shard_map/all_gather | solution.py:33
  272.2 0.6 gather_fusion.2
  272.8 3.4 convolution_multiply_fusion
  276.3 1.0 fusion.28
  277.7 50.8 %all-reduce.9.cloned.1.call-done = f32[32,2048]{1,0:T(8,128)} async-done(((f32[32,2048]{1,0:T(8,128)}), f32[32,2048]{1,0:T(8,128)}) %all-reduce.9.cloned.1.call-update) | async-done | bytes 262160
  328.5 0.8 constant_dynamic-slice_fusion
  329.4 19.0 %psum.105 = bf16[4,2048]{1,0:T(4,128)(2,1)S(1)} all-reduce(f32[4,2048]{1,0:T(4,128)S(1)} %constant_dynamic-slice_fusion), channel_id=1, replica_groups=mesh['grp'=8,'tile'=4] {'tile'}, use_global_device_ids=true, to_apply=%region_11.14 | all-reduce | flops 8192 | bytes 49152 | tf_op jit(solution)/shard_map/psum | solution.py:51
  348.4 0.4 convolution_add_fusion
  348.8 0.4 convolution_bitcast_fusion.10
  349.1 0.4 convolution_bitcast_fusion.11
  349.5 37.8 %all-reduce.2 = (f32[8,8]{0,1:T(8,128)S(1)}, f32[8,8]{0,1:T(8,128)S(1)}, f32[8,8]{0,1:T(8,128)S(1)}) all-reduce(f32[8,8]{0,1:T(8,128)S(1)} %convolution_bitcast_fusion.11, f32[8,8]{0,1:T(8,128)S(1)} %convolution_bitcast_fusion.9, f32[8,8]{0,1:T(8,128)S(1)} %convolution_bitcast_fusion.10), channel_id=1, replica_groups=mesh['grp'=8,'tile'=4] {'grp','tile'}, use_global_device_ids=true, to_apply=%region_13.16 | all-reduce | flops 192 | bytes 1536 | tf_op jit(solution)/shard_map/psum | solution.py:66
  388.4 41.1 %psum.103 = f32[8,8]{0,1:T(8,128)S(1)} all-reduce(f32[8,8]{0,1:T(8,128)S(1)} %convolution_bitcast_fusion.8), channel_id=1, replica_groups=mesh['grp'=8,'tile'=4] {'grp','tile'}, use_global_device_ids=true, to_apply=%region_16.19 | all-reduce | flops 64 | bytes 512 | tf_op jit(solution)/shard_map/psum | solution.py:18
  429.5 0.7 cholesky.81
  430.3 0.6 compare_reduce_fusion
  430.9 0.6 fusion.38
  431.6 0.6 custom-call.11
  432.4 0.9 convolution_bitcast_fusion
  433.4 0.6 pad_maximum_fusion
  (50 shorter events, 4.1 us)
Async XLA Ops:
  7.2 47.6 %copy-start = (bf16[4,256,1024]{2,1,0:T(8,128)(2,1)S(1)}, bf16[4,256,1024]{2,1,0:T(8,128)(2,1)}, u32[]{:S(2)}) copy-start(bf16[4,256,1024]{2,1,0:T(8,128)(2,1)} %param.9) | copy-start | bytes 6291460
  7.2 76.1 %copy-start.4 = (s32[32]{0:T(128)S(1)}, s32[32]{0:T(128)}, u32[]{:S(2)}) copy-start(s32[32]{0:T(128)} %param.12) | copy-start | bytes 388
  7.2 76.1 %copy-start.1 = (s32[32,32]{1,0:T(8,128)S(1)}, s32[32,32]{1,0:T(8,128)}, u32[]{:S(2)}) copy-start(s32[32,32]{1,0:T(8,128)} %param.11) | copy-start | bytes 12292
  7.2 133.2 %all-reduce.7.cloned.1.call-start = ((), (), s32[]{:S(2)}) async-start(), calls=%async_computation | async-start | bytes 524288
  84.7 4.5 %copy-start.5 = (u32[32]{0:T(128)S(1)}, u32[32]{0:T(128)}, u32[]{:S(2)}) copy-start(u32[32]{0:T(128)} %constant.93) | copy-start | bytes 388
  84.7 5.8 %copy-start.3 = (f32[4,1024]{1,0:T(4,128)S(1)}, f32[4,1024]{1,0:T(4,128)}, u32[]{:S(2)}) copy-start(f32[4,1024]{1,0:T(4,128)} %param.10) | copy-start | bytes 49156
  89.2 239.4 %all-reduce.9.cloned.1.call-start = ((), (), s32[]{:S(2)}) async-start(), calls=%async_computation.1 | async-start | bytes 524288
  387.6 46.4 %copy-start.2 = (f32[4,8,1024]{2,1,0:T(8,128)}, f32[4,8,1024]{2,1,0:T(8,128)S(1)}, u32[]{:S(2)}) copy-start(f32[4,8,1024]{2,1,0:T(8,128)S(1)} %fusion.1) | copy-start | bytes 393220
Sparse Core Ops, SparseCore 0:
  89.3 51.1 all-reduce.6
  277.4 51.1 all-reduce.8
where the time goes:
time: 442 us; the launch traced here: 441 us
  blocking collectives  293 us (66%)
  waiting for transfers between devices  100 us (23%)
  matrix products  19.4 us (4%)
  between operations  14.9 us (3%)
  other arithmetic  8.74 us (2%)
  local copies, waits for them, and re-layouts  4.71 us (1%)
    psum x3, blocking collectives, orthonormal(): gram = lax.psum(inner_sum(block, block), ('grp', 'tile')) / count  124 us
    unnamed x4, waiting for transfers between devices  100 us
    psum x2, blocking collectives, per_device(): lax.psum((inner_sum(basis, sigma), inner_sum(basis, sigma / scaled_energy...  75.4 us
    psum x2, blocking collectives, apply_kernel(): summed_tile = lax.psum(partial_rows, 'tile')  38 us
    psum x2, blocking collectives, apply_kernel(): dens_local = lax.psum(dens_part, 'tile')  35.1 us
    all_gather x2, blocking collectives, apply_kernel(): lax.all_gather(dens_local.astype(jnp.bfloat16), 'grp', axis=0, tiled=True)  19.9 us
  transfers between devices with their start and end apart: 2, of which 2 were waited for; matrix products, arithmetic and copies ran while one was open for 0% of the time, Pallas kernels for 0%

commit v1 on v0

v1 whole, which is shorter than its diff:
```python
import functools

import jax
import jax.numpy as jnp
from jax import lax
from jax.experimental import pallas as pl
from jax.experimental.pallas import tpu as pltpu
from jax.sharding import PartitionSpec as P

ITERS = 2
LANES = 128
BF = jnp.bfloat16
F4 = jnp.float32
NT = (((1,), (1,)), ((), ()))
NN = (((1,), (0,)), ((), ()))


def split2(x):
    high = x.astype(BF)
    return high, (x - high.astype(F4)).astype(BF)


def mm(left, right, dims):
    return lax.dot_general(left, right, dims, preferred_element_type=F4)


def exact(left, right, dims):
    return lax.dot_general(
        left, right, dims, preferred_element_type=F4, precision=lax.Precision.HIGHEST
    )


def apply_small(weights, block):
    total = weights[:, 0:1] * block[0:1, :]
    for m in range(1, weights.shape[1]):
        total = total + weights[:, m : m + 1] * block[m : m + 1, :]
    return total


def inverse_cholesky(gram):
    v = gram.shape[0]
    row_id = lax.broadcasted_iota(jnp.int32, (v, v), 0)
    col_id = lax.broadcasted_iota(jnp.int32, (v, v), 1)
    inverse = (row_id == col_id).astype(F4)
    rest = gram
    for j in range(v):
        scale = 1.0 / jnp.sqrt(rest[j : j + 1, j : j + 1])
        col = rest[:, j : j + 1] * scale
        row = rest[j : j + 1, :] * scale
        inv_row = inverse[j : j + 1, :] * scale
        below = jnp.where(row_id[:, 0:1] > j, col, 0.0)
        inverse = jnp.where(row_id == j, inv_row, inverse - below * inv_row)
        if j + 1 < v:
            rest = rest - col * row
    return inverse


def pack_moments(scratch, parts):
    total = None
    for i, part in enumerate(parts):
        width = part.shape[1]
        scratch[...] = jnp.zeros(scratch.shape, F4)
        scratch[:, 0:width] = part
        placed = scratch[...]
        if i:
            placed = pltpu.roll(placed, i * width, 1)
        total = placed if total is None else total + placed
    used = sum(part.shape[1] for part in parts)
    first = total.astype(BF).astype(F4)
    left = total - first
    second = left.astype(BF).astype(F4)
    third = (left - second).astype(BF).astype(F4)
    packed = first + pltpu.roll(second, used, 1) + pltpu.roll(third, 2 * used, 1)
    return packed.astype(BF)


def unpack_moments(total, used):
    width = total.shape[1]
    return total + pltpu.roll(total, width - used, 1) + pltpu.roll(total, width - 2 * used, 1)


def store_for_all(out_ref, dens_halves, moments):
    pairs, _, tiles, blocks = out_ref.shape[:4]

    def one(g, carry):
        for h in range(2):
            for t in range(tiles):
                for k in range(blocks - 1):
                    out_ref[g, h, t, k] = dens_halves[k][h]
                out_ref[g, h, t, blocks - 1] = moments
        return carry

    lax.fori_loop(0, pairs, one, 0, unroll=True)


def project(block, coeff):
    high, low = split2(block)
    both = mm(jnp.concatenate([high, low], 0), coeff, NT)
    v = block.shape[0]
    total = both[:v] + both[v:]
    half = total.shape[1] // 2
    return [total[:, :half].astype(BF), total[:, half:].astype(BF)]


def start_kernel(x_ref, e_ref, c_ref, out_ref, scratch):
    local_k, v, _ = x_ref.shape
    halves = []
    moments = None
    for k in range(local_k):
        x = x_ref[k]
        halves.append(project(x, c_ref[k]))
        xh, xl = split2(x)
        eh, el = split2(x * e_ref[k : k + 1, :])
        big = mm(jnp.concatenate([xh, xl], 0), jnp.concatenate([xh, eh], 0), NT)
        small = mm(xh, jnp.concatenate([xl, el], 0), NT)
        part = big[:v] + big[v:] + small
        moments = part if moments is None else moments + part
    store_for_all(out_ref, halves, pack_moments(scratch, [moments]))


def gather_dens(core_ref, mine_ref, other_ref, dens_ref):
    groups, tiles, blocks = mine_ref.shape[:3]
    local_k = blocks - 1
    core = core_ref[0]
    moments = None
    for g in range(groups):
        for k in range(local_k):
            for ref, slot in ((mine_ref, core), (other_ref, 1 - core)):
                total = ref[g, 0, k].astype(F4)
                for t in range(1, tiles):
                    total = total + ref[g, t, k].astype(F4)
                dens_ref[slot, g * local_k + k] = total
        for t in range(tiles):
            block = mine_ref[g, t, local_k].astype(F4)
            moments = block if moments is None else moments + block
    return moments


def run_tasks(assign_ref, ranks_ref, screen_ref, core_ref, dens_ref, dens_b, acc, keep_ref, send_ref, scratch, local_k):
    total_k, v = dens_b.shape[1:3]
    half = dens_b.shape[3]
    slots = acc.shape[1]
    core = core_ref[0]
    for which in range(2):
        for slot in range(slots):
            acc[which, slot] = jnp.zeros((v, 2 * half), F4)
    lane = lax.broadcasted_iota(jnp.int32, (v, 2 * half), 1)

    def one(t, carry):
        pair = assign_ref[t]
        row = pair // total_k
        col = pair - row * total_k
        keep = lane < ranks_ref[row, col]
        vec = jnp.concatenate([dens_b[0, col], dens_b[1, col]], 1)
        vec = jnp.where(keep, vec, 0.0).astype(BF)
        term = jnp.where(keep, mm(vec, screen_ref[t], NT), 0.0)
        owner = row // local_k
        slot = (owner // 2) * local_k + row - owner * local_k
        which = (owner + core) % 2
        acc[which, slot] = acc[which, slot] + term
        return carry

    lax.fori_loop(0, assign_ref.shape[0], one, 0, unroll=8)
    total = None
    for which in range(2):
        for slot in range(slots):
            owner_pair = slot // local_k
            k = (owner_pair * 2 + (core + which) % 2) * local_k + slot % local_k
            rows = acc[which, slot]
            rh, rl = split2(rows)
            dens = jnp.concatenate([dens_ref[0, k], dens_ref[1, k]], 1)
            dh, dl = split2(dens)
            big = mm(jnp.concatenate([rh, rl], 0), dh, NT)
            part = big[:v] + big[v:] + mm(rh, dl, NT)
            total = part if total is None else total + part
            (send_ref if which else keep_ref)[slot] = rows
    scratch[...] = jnp.zeros(scratch.shape, F4)
    scratch[:, 0:v] = total
    for ref, value in ((keep_ref, scratch[...]), (send_ref, scratch[...])):
        ref[slots] = jnp.concatenate([value, jnp.zeros_like(value)], 1)


def pad_small(scratch, small):
    scratch[...] = jnp.zeros(scratch.shape, F4)
    scratch[:, 0 : small.shape[1]] = small
    return scratch[...]


def first_tasks_kernel(core_ref, assign_ref, ranks_ref, mine_ref, other_ref, screen_ref,
                       keep_ref, send_ref, dens_ref, small_ref, dens_b, acc, scratch, *, count):
    v = mine_ref.shape[3]
    local_k = mine_ref.shape[2] - 1
    moments = unpack_moments(gather_dens(core_ref, mine_ref, other_ref, dens_ref), 2 * v)
    inverse = inverse_cholesky(moments[:, 0:v] / count)
    weighted = moments[:, v : 2 * v] / count
    diag = exact(exact(inverse, weighted, NN), inverse, NT)
    for h in range(2):
        for k in range(dens_ref.shape[1]):
            dens = apply_small(inverse, dens_ref[h, k])
            dens_ref[h, k] = dens
            dens_b[h, k] = dens.astype(BF)
    small_ref[0] = pad_small(scratch, inverse)
    small_ref[1] = pad_small(scratch, diag)
    run_tasks(assign_ref, ranks_ref, screen_ref, core_ref, dens_ref, dens_b, acc,
              keep_ref, send_ref, scratch, local_k)


def next_tasks_kernel(core_ref, assign_ref, ranks_ref, mine_ref, other_ref, prev_dens_ref,
                      prev_small_ref, screen_ref, keep_ref, send_ref, dens_ref, small_ref,
                      dens_b, acc, scratch, *, count):
    v = mine_ref.shape[3]
    local_k = mine_ref.shape[2] - 1
    moments = unpack_moments(gather_dens(core_ref, mine_ref, other_ref, dens_ref), 4 * v) / count
    pp = moments[:, 0:v]
    mix = moments[:, v : 2 * v]
    rp = moments[:, 2 * v : 3 * v]
    rv = moments[:, 3 * v : 4 * v]
    prev_diag = prev_small_ref[1][:, 0:v]
    inverse = inverse_cholesky(pp - exact(mix, mix, NT))
    cross = exact(rv, mix, NT)
    cross_t = exact(mix, rv, NT)
    weighted = rp - cross - cross_t + exact(exact(mix, prev_diag, NN), mix, NT)
    diag = exact(exact(inverse, weighted, NN), inverse, NT)
    both = exact(inverse, mix, NN)
    for h in range(2):
        for k in range(dens_ref.shape[1]):
            dens = apply_small(inverse, dens_ref[h, k]) - apply_small(both, prev_dens_ref[h, k])
            dens_ref[h, k] = dens
            dens_b[h, k] = dens.astype(BF)
    small_ref[0] = pad_small(scratch, inverse)
    small_ref[1] = pad_small(scratch, diag)
    small_ref[2] = pad_small(scratch, both)
    run_tasks(assign_ref, ranks_ref, screen_ref, core_ref, dens_ref, dens_b, acc,
              keep_ref, send_ref, scratch, local_k)


def rows_kernel(keep_ref, recv_ref, out_ref):
    pairs, tiles, blocks, v, half = out_ref.shape
    local_k = (blocks - 1) // 2
    slots = pairs * local_k
    diag = (keep_ref[slots] + recv_ref[slots])[:, :half]
    first = diag.astype(BF).astype(F4)
    left = diag - first
    second = left.astype(BF).astype(F4)
    third = (left - second).astype(BF).astype(F4)
    packed = (first + pltpu.roll(second, v, 1) + pltpu.roll(third, 2 * v, 1)).astype(BF)
    for g in range(pairs):
        for k in range(local_k):
            rows = (keep_ref[g * local_k + k] + recv_ref[g * local_k + k]).astype(BF)
            for t in range(tiles):
                out_ref[g, t, 2 * k] = rows[:, :half]
                out_ref[g, t, 2 * k + 1] = rows[:, half:]
        for t in range(tiles):
            out_ref[g, t, blocks - 1] = packed


def sum_rows(recv_ref):
    sources, blocks, v, half = recv_ref.shape
    sums = []
    for b in range(blocks):
        total = recv_ref[0, b].astype(F4)
        for s in range(1, sources):
            total = total + recv_ref[s, b].astype(F4)
        sums.append(total)
    local_k = (blocks - 1) // 2
    rows = [jnp.concatenate([sums[2 * k], sums[2 * k + 1]], 1).astype(BF) for k in range(local_k)]
    return rows, unpack_moments(sums[-1], v)[:, 0:v]


def after_first_kernel(recv_ref, x_ref, e_ref, c_ref, small_ref, out_ref, v_ref, p_ref, ray_ref, scratch, *, count):
    local_k, v, _ = x_ref.shape
    rows, coupled_part = sum_rows(recv_ref)
    inverse = small_ref[0][:, 0:v]
    ray = small_ref[1][:, 0:v] + coupled_part / count
    ray_ref[...] = pad_small(scratch, ray)
    halves = []
    moments = None
    for k in range(local_k):
        basis = apply_small(inverse, x_ref[k])
        energy = e_ref[k : k + 1, :]
        sigma = energy * basis + mm(rows[k], c_ref[k], NN)
        residual = sigma - apply_small(ray, basis)
        precond = residual / energy
        v_ref[k] = basis
        p_ref[k] = precond
        halves.append(project(precond, c_ref[k]))
        bh, bl = split2(basis)
        rh, rl = split2(residual)
        ph, pw = split2(precond)
        big = mm(jnp.concatenate([ph, rh, pw, rl], 0), jnp.concatenate([ph, bh], 0), NT)
        small = mm(jnp.concatenate([ph, rh], 0), jnp.concatenate([pw, bl], 0), NT)
        part = big[: 2 * v] + big[2 * v :] + small
        moments = part if moments is None else moments + part
    store_for_all(out_ref, halves, pack_moments(scratch, [moments[:v], moments[v:]]))


def last_rows_kernel(recv_ref, v_ref, p_ref, e_ref, c_ref, small_ref, out_ref, res_ref, basis_ref, q_ref, ray_ref, scratch, *, count):
    local_k, v, _ = v_ref.shape
    rows, coupled_part = sum_rows(recv_ref)
    inverse = small_ref[0][:, 0:v]
    both = small_ref[2][:, 0:v]
    ray = small_ref[1][:, 0:v] + coupled_part / count
    ray_ref[...] = pad_small(scratch, ray)
    moments = None
    for k in range(local_k):
        basis = apply_small(inverse, p_ref[k]) - apply_small(both, v_ref[k])
        energy = e_ref[k : k + 1, :]
        sigma = energy * basis + mm(rows[k], c_ref[k], NN)
        residual = sigma - apply_small(ray, basis)
        precond = residual / energy
        res_ref[k] = residual
        basis_ref[k] = basis
        q_ref[k] = precond
        bh, bl = split2(basis)
        ph, pw = split2(precond)
        big = mm(jnp.concatenate([ph, pw], 0), jnp.concatenate([ph, bh], 0), NT)
        part = big[:v] + big[v:] + mm(ph, jnp.concatenate([pw, bl], 0), NT)
        moments = part if moments is None else moments + part
    packed = pack_moments(scratch, [moments])
    for d in range(out_ref.shape[0]):
        out_ref[d] = packed


def finish_kernel(recv_ref, q_ref, b_ref, out_ref, *, count):
    local_k, v, _ = q_ref.shape
    total = recv_ref[0].astype(F4)
    for d in range(1, recv_ref.shape[0]):
        total = total + recv_ref[d].astype(F4)
    moments = unpack_moments(total, 2 * v) / count
    mix = moments[:, v : 2 * v]
    inverse = inverse_cholesky(moments[:, 0:v] - exact(mix, mix, NT))
    both = exact(inverse, mix, NN)
    for k in range(local_k):
        out_ref[k] = apply_small(inverse, q_ref[k]) - apply_small(both, b_ref[k])


VM = pl.BlockSpec(memory_space=pltpu.VMEM)
SM = pl.BlockSpec(memory_space=pltpu.SMEM)


def call(body, outs, ins, args, scratch=()):
    return pl.pallas_call(
        body,
        out_shape=outs,
        in_specs=ins,
        out_specs=jax.tree.map(lambda _: VM, outs),
        scratch_shapes=scratch,
    )(*args)


def per_device(coeff, energy, ranks, assign, screen, initial):
    groups = lax.axis_size("grp")
    tiles = lax.axis_size("tile")
    devices = groups * tiles
    pairs = groups // 2
    local_k, v, width = initial.shape
    levels = coeff.shape[1]
    half = levels // 2
    total_k = local_k * groups
    count = float(total_k * width * tiles)
    core = (lax.axis_index("grp") % 2).reshape(1)
    axes = ("grp", "tile")
    same_core = [[g * tiles + t for g in range(c, groups, 2) for t in range(tiles)] for c in range(2)]
    swap = [(g, g ^ 1) for g in range(groups)]
    sds = jax.ShapeDtypeStruct
    small_scratch = pltpu.VMEM((v, half), F4)

    def to_all(blocks):
        sent = blocks.reshape((devices,) + blocks.shape[3:])
        got = lax.all_to_all(sent, axes, 0, 0, tiled=True)
        other = lax.ppermute(got, "grp", swap)
        shape = (groups, tiles) + got.shape[1:]
        return got.reshape(shape), other.reshape(shape)

    def to_owner(keep, send):
        recv = lax.ppermute(send, "grp", swap)
        out = call(rows_kernel, sds((pairs, tiles, 2 * local_k + 1, v, half), BF), [VM, VM], (keep, recv))
        out = out.reshape((pairs * tiles,) + out.shape[2:])
        return lax.all_to_all(out, axes, 0, 0, tiled=True, axis_index_groups=same_core)

    all_shape = sds((pairs, 2, tiles, local_k + 1, v, half), BF)
    slots = pairs * local_k + 1
    task_outs = (
        sds((slots, v, levels), F4),
        sds((slots, v, levels), F4),
        sds((2, total_k, v, half), F4),
    )
    task_scratch = (
        pltpu.VMEM((2, total_k, v, half), BF),
        pltpu.VMEM((2, slots - 1, v, levels), F4),
        small_scratch,
    )
    flat = sds((local_k, v, width), F4)
    ray_shape = sds((v, half), F4)

    sent = call(start_kernel, all_shape, [VM] * 3, (initial, energy, coeff), (small_scratch,))
    mine, other = to_all(sent)
    keep, send, dens, small = call(
        functools.partial(first_tasks_kernel, count=count),
        task_outs + (sds((2, v, half), F4),),
        [SM, SM, SM, VM, VM, VM],
        (core, assign, ranks, mine, other, screen),
        task_scratch,
    )
    got = to_owner(keep, send)
    sent, basis, precond, ray0 = call(
        functools.partial(after_first_kernel, count=count),
        (all_shape, flat, flat, ray_shape),
        [VM] * 5,
        (got, initial, energy, coeff, small),
        (small_scratch,),
    )
    mine, other = to_all(sent)
    keep, send, dens, small = call(
        functools.partial(next_tasks_kernel, count=count),
        task_outs + (sds((3, v, half), F4),),
        [SM, SM, SM, VM, VM, VM, VM, VM],
        (core, assign, ranks, mine, other, dens, small, screen),
        task_scratch,
    )
    got = to_owner(keep, send)
    sent, residual, basis, precond, ray1 = call(
        functools.partial(last_rows_kernel, count=count),
        (sds((devices, v, half), BF), flat, flat, flat, ray_shape),
        [VM] * 6,
        (got, basis, precond, energy, coeff, small),
        (small_scratch,),
    )
    got = lax.all_to_all(sent, axes, 0, 0, tiled=True)
    basis = call(
        functools.partial(finish_kernel, count=count), flat, [VM] * 3, (got, precond, basis)
    )
    rayleigh = jnp.stack([ray0[:, :v].T, ray1[:, :v].T])
    return (rayleigh, basis, residual)


def solution(mesh):
    placed = (
        P("grp", None, "tile"),
        P("grp", "tile"),
        P(),
        P(("grp", "tile")),
        P(("grp", "tile"), None, None),
        P("grp", None, "tile"),
    )
    return jax.shard_map(
        per_device,
        mesh=mesh,
        in_specs=placed,
        out_specs=(P(), P("grp", None, "tile"), P("grp", None, "tile")),
        check_vma=False,
    )
```

time: 442 us -> 117 us (0.26)
  blocking collectives: 293 us -> 48.4 us
  waiting for transfers between devices: 100 us -> 22.8 us
  Pallas kernels: 0 us -> 30.2 us
  matrix products: 19.4 us -> 0 us
  between operations: 14.9 us -> 0.68 us
  starting transfers between devices: 0.08 us -> 8.68 us
  other arithmetic: 8.74 us -> 0.6 us
    psum x9 -> x0, blocking collectives: 273 us -> none  [the longest x3 124 us: orthonormal(): gram = lax.psum(inner_sum(block, block), ('grp', 'tile')) / count]
    unnamed x4 -> x0, waiting for transfers between devices: 100 us -> none
    all_to_all x0 -> x3, blocking collectives: none -> 48.4 us  [the longest x2 32.2 us: to_all(): got = lax.all_to_all(sent, axes, 0, 0, tiled=True)]
    pallas_call x0 -> x8, Pallas kernels: none -> 30.2 us  [call(): pl.pallas_call(body, out_shape=outs, in_specs=ins, out_specs=jax.tree.map...]
    all_gather x2 -> x0, blocking collectives: 19.9 us -> none  [apply_kernel(): lax.all_gather(dens_local.astype(jnp.bfloat16), 'grp', axis=0, tiled=True)]
    dot_general x26 -> x0, matrix products: 18.8 us -> none  [the longest x2 6.77 us: apply_kernel(): jnp.einsum('tnh,tgh->tng', task_dens, screen, preferred_element_type=jnp....]
    all_to_all x0 -> x2, waiting for transfers between devices: none -> 17.9 us  [the longest x1 11.7 us: to_owner(): lax.all_to_all(out, axes, 0, 0, tiled=True, axis_index_groups=same_core)]
    another operation x16 -> x1, other arithmetic: 8.6 us -> 0.6 us  [per_device(): rayleigh = jnp.stack([ray0[:, :v].T, ray1[:, :v].T])]
  transfers between devices with their start and end apart: 2 -> 6, of which waited for: 2 -> 6; matrix products, arithmetic and copies ran while one was open for 0% -> 1% of each run, Pallas kernels for 0% -> 0%
where the time goes in v1:
time: 117 us; the launch traced here: 116 us
  blocking collectives  48.4 us (41%)
  Pallas kernels  30.2 us (26%)
  waiting for transfers between devices  22.8 us (19%)
  starting transfers between devices  8.68 us (7%)
  local copies, waits for them, and re-layouts  4.9 us (4%)
    all_to_all x2, blocking collectives, to_all(): got = lax.all_to_all(sent, axes, 0, 0, tiled=True)  32.2 us
    pallas_call x8, Pallas kernels, call(): pl.pallas_call(body, out_shape=outs, in_specs=ins, out_specs=jax.tree.map...  30.2 us
    all_to_all x1, blocking collectives, to_owner(): lax.all_to_all(out, axes, 0, 0, tiled=True, axis_index_groups=same_core)  16.3 us
    all_to_all x1, waiting for transfers between devices, to_owner(): lax.all_to_all(out, axes, 0, 0, tiled=True, axis_index_groups=same_core)  11.7 us
    all_to_all x1, waiting for transfers between devices, per_device(): got = lax.all_to_all(sent, axes, 0, 0, tiled=True)  6.13 us
    unnamed x18, local copies, waits for them, and re-layouts  4.06 us
    all_to_all x1, starting transfers between devices, to_owner(): lax.all_to_all(out, axes, 0, 0, tiled=True, axis_index_groups=same_core)  3.76 us
    all_to_all x1, starting transfers between devices, per_device(): got = lax.all_to_all(sent, axes, 0, 0, tiled=True)  2.56 us
  transfers between devices with their start and end apart: 6, of which 6 were waited for; matrix products, arithmetic and copies ran while one was open for 1% of the time, Pallas kernels for 0%

profile of v1, /device:TPU:0, one launch (start us, length us, event | category | flops | bytes accessed | tf_op | source)
XLA Modules:
  0.0 116.3 jit_solution(15814891092162852525)
XLA Ops:
  0.6 3.3 %shard_map.85 = bf16[4,2,4,5,8,128]{5,4,3,2,1,0:T(8,128)(2,1)} custom-call(f32[4,8,1024]{2,1,0:T(8,128)} %x_ref.3, f32[4,1024]{1,0:T(4,128)} %e_ref.5, bf16[4,256,1024]{2,1,0:T(8,128)(2,1)} %c_ref.5), custom_call_target="tpu_custom_call" | custom-call | tf_op jit(solution)/shard_map/pallas_call | solution.py:342
  3.9 18.4 %all_to_all.25 = bf16[32,5,8,128]{3,2,1,0:T(8,128)(2,1)S(1)} all-to-all(bf16[32,5,8,128]{3,2,1,0:T(8,128)(2,1)} %bitcast.16), channel_id=1, replica_groups=mesh['grp'=8,'tile'=4] {'grp','tile'}, dimensions={0} | all-to-all | bytes 655360 | tf_op jit(solution)/shard_map/all_to_all | solution.py:370
  22.3 0.0 copy-start.1
  22.3 0.8 collective-permute-start
  23.1 1.3 %collective-permute-done = bf16[32,5,8,128]{3,2,1,0:T(8,128)(2,1)S(1)} collective-permute-done((bf16[32,5,8,128]{3,2,1,0:T(8,128)(2,1)S(1)}, bf16[32,5,8,128]{3,2,1,0:T(8,128)(2,1)S(1)}, u32[]{:S(2)}, u32[]{:S(2)}) %collective-permute-start) | collective-permute-done | bytes 327712 | tf_op jit(solution)/shard_map/ppermute | solution.py:371
  24.4 0.0 copy-start.4
  24.4 0.0 copy-done.1
  24.4 0.7 copy-done.4
  25.1 6.3 %shard_map.86 = (f32[17,8,256]{2,1,0:T(8,128)}, f32[17,8,256]{2,1,0:T(8,128)}, f32[2,32,8,128]{3,2,1,0:T(8,128)}, f32[2,8,128]{2,1,0:T(8,128)}) custom-call(s32[1]{0:T(128)} %bitcast.core_ref, s32[32]{0:T(128)} %assign_ref.3, s32[32,32]{1,0:T(8,128)} %ranks_ref.3, bf16[8,4,5,8,128]{4,3,2,1,0:T(8,128)(2,1)} %bitcast.17, bf16[8,4,5,8,128]{4,3,2,1,0:T(8,128)(2,1)} %bitcast.22, ...), custom_call_target="tpu_custom_call" | custom-call | tf_op jit(solution)/shard_map/pallas_call | solution.py:342
  31.4 0.4 collective-permute-start.1
  31.8 1.2 %collective-permute-done.1.recv_ref = f32[17,8,256]{2,1,0:T(8,128)S(1)} collective-permute-done((f32[17,8,256]{2,1,0:T(8,128)}, f32[17,8,256]{2,1,0:T(8,128)S(1)}, u32[]{:S(2)}, u32[]{:S(2)}) %collective-permute-start.1) | collective-permute-done | bytes 139296 | tf_op jit(solution)/shard_map/ppermute | solution.py:376
  33.0 0.0 copy-start.6
  33.0 0.6 copy-done.6
  33.6 1.8 %shard_map.87 = bf16[4,4,9,8,128]{4,3,2,1,0:T(8,128)(2,1)} custom-call(f32[17,8,256]{2,1,0:T(8,128)} %get-tuple-element.19.keep_ref, f32[17,8,256]{2,1,0:T(8,128)} %copy-done.6), custom_call_target="tpu_custom_call" | custom-call | tf_op jit(solution)/shard_map/pallas_call | solution.py:342
  35.4 16.3 %all_to_all.26.recv_ref = bf16[16,9,8,128]{3,2,1,0:T(8,128)(2,1)} all-to-all(bf16[16,9,8,128]{3,2,1,0:T(8,128)(2,1)} %bitcast.19), channel_id=1, replica_groups={{0,1,2,3,8,9,10,11,16,17,18,19,24,25,26,27},{4,5,6,7,12,13,14,15,20,21,..., dimensions={0} | all-to-all | bytes 589824 | tf_op jit(solution)/shard_map/all_to_all | solution.py:379
  51.7 3.8 %shard_map.88 = (bf16[4,2,4,5,8,128]{5,4,3,2,1,0:T(8,128)(2,1)}, f32[4,8,1024]{2,1,0:T(8,128)}, f32[4,8,1024]{2,1,0:T(8,128)}, f32[8,128]{1,0:T(8,128)}) custom-call(bf16[16,9,8,128]{3,2,1,0:T(8,128)(2,1)} %all_to_all.26.recv_ref, f32[4,8,1024]{2,1,0:T(8,128)} %x_ref.3, f32[4,1024]{1,0:T(4,128)} %e_ref.5, bf16[4,256,1024]{2,1,0:T(8,128)(2,1)} %c_ref.5, ...), custom_call_target="tpu_custom_call" | custom-call | tf_op jit(solution)/shard_map/pallas_call | solution.py:342
  55.5 0.0 copy-start.8
  55.5 13.8 %all_to_all.27 = bf16[32,5,8,128]{3,2,1,0:T(8,128)(2,1)S(1)} all-to-all(bf16[32,5,8,128]{3,2,1,0:T(8,128)(2,1)} %bitcast.21), channel_id=1, replica_groups=mesh['grp'=8,'tile'=4] {'grp','tile'}, dimensions={0} | all-to-all | bytes 655360 | tf_op jit(solution)/shard_map/all_to_all | solution.py:370
  69.3 0.0 copy-start
  69.3 0.8 collective-permute-start.2
  70.1 1.3 %collective-permute-done.2 = bf16[32,5,8,128]{3,2,1,0:T(8,128)(2,1)S(1)} collective-permute-done((bf16[32,5,8,128]{3,2,1,0:T(8,128)(2,1)S(1)}, bf16[32,5,8,128]{3,2,1,0:T(8,128)(2,1)S(1)}, u32[]{:S(2)}, u32[]{:S(2)}) %collective-permute-start.2) | collective-permute-done | bytes 327712 | tf_op jit(solution)/shard_map/ppermute | solution.py:371
  71.4 0.0 copy-start.3
  71.4 0.0 copy-done
  71.4 0.7 copy-done.3
  72.1 6.7 %shard_map.89 = (f32[17,8,256]{2,1,0:T(8,128)}, f32[17,8,256]{2,1,0:T(8,128)}, f32[2,32,8,128]{3,2,1,0:T(8,128)}, f32[3,8,128]{2,1,0:T(8,128)}) custom-call(s32[1]{0:T(128)} %bitcast.core_ref, s32[32]{0:T(128)} %assign_ref.3, s32[32,32]{1,0:T(8,128)} %ranks_ref.3, bf16[8,4,5,8,128]{4,3,2,1,0:T(8,128)(2,1)} %bitcast.15, bf16[8,4,5,8,128]{4,3,2,1,0:T(8,128)(2,1)} %bitcast.20, ...), custom_call_target="tpu_custom_call" | custom-call | tf_op jit(solution)/shard_map/pallas_call | solution.py:342
  78.8 0.4 collective-permute-start.3
  79.2 1.2 %collective-permute-done.3.recv_ref = f32[17,8,256]{2,1,0:T(8,128)S(1)} collective-permute-done((f32[17,8,256]{2,1,0:T(8,128)}, f32[17,8,256]{2,1,0:T(8,128)S(1)}, u32[]{:S(2)}, u32[]{:S(2)}) %collective-permute-start.3) | collective-permute-done | bytes 139296 | tf_op jit(solution)/shard_map/ppermute | solution.py:376
  80.4 0.0 copy-start.7
  80.4 0.6 copy-done.7
  81.0 1.8 %shard_map.90 = bf16[4,4,9,8,128]{4,3,2,1,0:T(8,128)(2,1)} custom-call(f32[17,8,256]{2,1,0:T(8,128)} %get-tuple-element.25.keep_ref, f32[17,8,256]{2,1,0:T(8,128)} %copy-done.7), custom_call_target="tpu_custom_call" | custom-call | tf_op jit(solution)/shard_map/pallas_call | solution.py:342
  82.8 3.8 %all-to-all-start.3 = ((bf16[16,9,8,128]{3,2,1,0:T(8,128)(2,1)}), bf16[16,9,8,128]{3,2,1,0:T(8,128)(2,1)S(1)}, u32[]{:S(2)}, u32[]{:S(2)}) async-start(bf16[16,9,8,128]{3,2,1,0:T(8,128)(2,1)} %bitcast.18), calls=%async_computation.3 | async-start | bytes 589824 | tf_op jit(solution)/shard_map/all_to_all | solution.py:379
  86.6 0.0 copy-done.8
  86.6 0.1 copy.9
  86.7 11.7 %all-to-all-done.3.recv_ref = bf16[16,9,8,128]{3,2,1,0:T(8,128)(2,1)S(1)} async-done(((bf16[16,9,8,128]{3,2,1,0:T(8,128)(2,1)}), bf16[16,9,8,128]{3,2,1,0:T(8,128)(2,1)S(1)}, u32[]{:S(2)}, u32[]{:S(2)}) %all-to-all-start.3) | async-done | bytes 294944 | tf_op jit(solution)/shard_map/all_to_all | solution.py:379
  98.4 0.0 copy-start.2
  98.4 0.7 copy-done.2
  99.1 3.5 %shard_map.91 = (bf16[32,8,128]{2,1,0:T(8,128)(2,1)}, f32[4,8,1024]{2,1,0:T(8,128)}, f32[4,8,1024]{2,1,0:T(8,128)}, f32[4,8,1024]{2,1,0:T(8,128)}, f32[8,128]{1,0:T(8,128)}) custom-call(bf16[16,9,8,128]{3,2,1,0:T(8,128)(2,1)} %copy-done.2, f32[4,8,1024]{2,1,0:T(8,128)} %get-tuple-element.27.v_ref, f32[4,8,1024]{2,1,0:T(8,128)} %get-tuple-element.28.p_ref, ...), custom_call_target="tpu_custom_call" | custom-call | tf_op jit(solution)/shard_map/pallas_call | solution.py:342
  102.6 2.6 %all-to-all-start.4 = ((bf16[32,8,128]{2,1,0:T(8,128)(2,1)}), bf16[32,8,128]{2,1,0:T(8,128)(2,1)S(1)}, u32[]{:S(2)}, u32[]{:S(2)}) async-start(bf16[32,8,128]{2,1,0:T(8,128)(2,1)} %get-tuple-element.31), calls=%async_computation.4 | async-start | bytes 131072 | tf_op jit(solution)/shard_map/all_to_all | solution.py:429
  105.2 0.7 slice_bitcast_fusion
  105.9 0.1 copy.10
  106.0 0.6 pad_maximum_fusion
  106.6 6.1 %all-to-all-done.4.recv_ref = bf16[32,8,128]{2,1,0:T(8,128)(2,1)S(1)} async-done(((bf16[32,8,128]{2,1,0:T(8,128)(2,1)}), bf16[32,8,128]{2,1,0:T(8,128)(2,1)S(1)}, u32[]{:S(2)}, u32[]{:S(2)}) %all-to-all-start.4) | async-done | bytes 65568 | tf_op jit(solution)/shard_map/all_to_all | solution.py:429
  112.7 0.0 copy-start.5
  112.7 0.6 copy-done.5
  113.3 3.0 %shard_map.92 = f32[4,8,1024]{2,1,0:T(8,128)} custom-call(bf16[32,8,128]{2,1,0:T(8,128)(2,1)} %copy-done.5, f32[4,8,1024]{2,1,0:T(8,128)} %get-tuple-element.32.q_ref, f32[4,8,1024]{2,1,0:T(8,128)} %get-tuple-element.33.b_ref), custom_call_target="tpu_custom_call" | custom-call | tf_op jit(solution)/shard_map/pallas_call | solution.py:342
  (1 shorter events, 0.0 us)
Async XLA Ops:
  22.3 2.1 %copy-start.1 = (bf16[32,5,8,128]{3,2,1,0:T(8,128)(2,1)}, bf16[32,5,8,128]{3,2,1,0:T(8,128)(2,1)S(1)}, u32[]{:S(2)}) copy-start(bf16[32,5,8,128]{3,2,1,0:T(8,128)(2,1)S(1)} %all_to_all.25) | copy-start | bytes 983044
  22.3 2.1 %collective-permute-start = (bf16[32,5,8,128]{3,2,1,0:T(8,128)(2,1)S(1)}, bf16[32,5,8,128]{3,2,1,0:T(8,128)(2,1)S(1)}, u32[]{:S(2)}, u32[]{:S(2)}) collective-permute-start(bf16[32,5,8,128]{3,2,1,0:T(8,128)(2,1)S(1)} %all_to_all.25), channel_id=1, source_target_pairs={{0,4},{4,0},{8,12},{12,8},{16,20},{20,16},{24,28},{28,24},{1,5},{5... | collective-permute-start | bytes 983048 | tf_op jit(solution)/shard_map/ppermute | solution.py:371
  24.4 0.7 copy-start.4
  31.4 1.6 %collective-permute-start.1 = (f32[17,8,256]{2,1,0:T(8,128)}, f32[17,8,256]{2,1,0:T(8,128)S(1)}, u32[]{:S(2)}, u32[]{:S(2)}) collective-permute-start(f32[17,8,256]{2,1,0:T(8,128)} %get-tuple-element.20), channel_id=1, source_target_pairs={{0,4},{4,0},{8,12},{12,8},{16,20},{20,16},{24,28},{28,24},{1,5},{5... | collective-permute-start | bytes 417800 | tf_op jit(solution)/shard_map/ppermute | solution.py:376
  33.0 0.6 copy-start.6
  55.5 31.1 %copy-start.8 = (f32[8,128]{1,0:T(8,128)S(1)}, f32[8,128]{1,0:T(8,128)}, u32[]{:S(2)}) copy-start(f32[8,128]{1,0:T(8,128)} %get-tuple-element.22) | copy-start | bytes 12292
  69.3 2.1 %copy-start = (bf16[32,5,8,128]{3,2,1,0:T(8,128)(2,1)}, bf16[32,5,8,128]{3,2,1,0:T(8,128)(2,1)S(1)}, u32[]{:S(2)}) copy-start(bf16[32,5,8,128]{3,2,1,0:T(8,128)(2,1)S(1)} %all_to_all.27) | copy-start | bytes 983044
  69.3 2.1 %collective-permute-start.2 = (bf16[32,5,8,128]{3,2,1,0:T(8,128)(2,1)S(1)}, bf16[32,5,8,128]{3,2,1,0:T(8,128)(2,1)S(1)}, u32[]{:S(2)}, u32[]{:S(2)}) collective-permute-start(bf16[32,5,8,128]{3,2,1,0:T(8,128)(2,1)S(1)} %all_to_all.27), channel_id=1, source_target_pairs={{0,4},{4,0},{8,12},{12,8},{16,20},{20,16},{24,28},{28,24},{1,5},{5... | collective-permute-start | bytes 983048 | tf_op jit(solution)/shard_map/ppermute | solution.py:371
  71.4 0.7 copy-start.3
  78.8 1.6 %collective-permute-start.3 = (f32[17,8,256]{2,1,0:T(8,128)}, f32[17,8,256]{2,1,0:T(8,128)S(1)}, u32[]{:S(2)}, u32[]{:S(2)}) collective-permute-start(f32[17,8,256]{2,1,0:T(8,128)} %get-tuple-element.26), channel_id=1, source_target_pairs={{0,4},{4,0},{8,12},{12,8},{16,20},{20,16},{24,28},{28,24},{1,5},{5... | collective-permute-start | bytes 417800 | tf_op jit(solution)/shard_map/ppermute | solution.py:376
  80.4 0.6 copy-start.7
  82.8 15.6 %all-to-all-start.3 = ((bf16[16,9,8,128]{3,2,1,0:T(8,128)(2,1)}), bf16[16,9,8,128]{3,2,1,0:T(8,128)(2,1)S(1)}, u32[]{:S(2)}, u32[]{:S(2)}) async-start(bf16[16,9,8,128]{3,2,1,0:T(8,128)(2,1)} %bitcast.18), calls=%async_computation.3 | async-start | bytes 589824 | tf_op jit(solution)/shard_map/all_to_all | solution.py:379
  98.4 0.7 copy-start.2
  102.6 10.1 %all-to-all-start.4 = ((bf16[32,8,128]{2,1,0:T(8,128)(2,1)}), bf16[32,8,128]{2,1,0:T(8,128)(2,1)S(1)}, u32[]{:S(2)}, u32[]{:S(2)}) async-start(bf16[32,8,128]{2,1,0:T(8,128)(2,1)} %get-tuple-element.31), calls=%async_computation.4 | async-start | bytes 131072 | tf_op jit(solution)/shard_map/all_to_all | solution.py:429
  112.7 0.6 copy-start.5

commit v2 on v1

v2 whole, which is shorter than its diff:
```python
import functools

import jax
import jax.numpy as jnp
from jax import lax
from jax.experimental import pallas as pl
from jax.experimental.pallas import tpu as pltpu
from jax.sharding import PartitionSpec as P

ITERS = 2
LANES = 128
BF = jnp.bfloat16
F4 = jnp.float32
NT = (((1,), (1,)), ((), ()))
NN = (((1,), (0,)), ((), ()))


def split2(x):
    high = x.astype(BF)
    return high, (x - high.astype(F4)).astype(BF)


def mm(left, right, dims):
    return lax.dot_general(left, right, dims, preferred_element_type=F4)


def exact(left, right, dims):
    return lax.dot_general(
        left, right, dims, preferred_element_type=F4, precision=lax.Precision.HIGHEST
    )


def apply_small(weights, block):
    total = weights[:, 0:1] * block[0:1, :]
    for m in range(1, weights.shape[1]):
        total = total + weights[:, m : m + 1] * block[m : m + 1, :]
    return total


def inverse_cholesky(gram):
    v = gram.shape[0]
    row_id = lax.broadcasted_iota(jnp.int32, (v, v), 0)
    col_id = lax.broadcasted_iota(jnp.int32, (v, v), 1)
    inverse = (row_id == col_id).astype(F4)
    rest = gram
    for j in range(v):
        scale = 1.0 / jnp.sqrt(rest[j : j + 1, j : j + 1])
        col = rest[:, j : j + 1] * scale
        row = rest[j : j + 1, :] * scale
        inv_row = inverse[j : j + 1, :] * scale
        below = jnp.where(row_id[:, 0:1] > j, col, 0.0)
        inverse = jnp.where(row_id == j, inv_row, inverse - below * inv_row)
        if j + 1 < v:
            rest = rest - col * row
    return inverse


def pack_moments(scratch, parts):
    total = None
    for i, part in enumerate(parts):
        width = part.shape[1]
        scratch[...] = jnp.zeros(scratch.shape, F4)
        scratch[:, 0:width] = part
        placed = scratch[...]
        if i:
            placed = pltpu.roll(placed, i * width, 1)
        total = placed if total is None else total + placed
    used = sum(part.shape[1] for part in parts)
    first = total.astype(BF).astype(F4)
    left = total - first
    second = left.astype(BF).astype(F4)
    third = (left - second).astype(BF).astype(F4)
    packed = first + pltpu.roll(second, used, 1) + pltpu.roll(third, 2 * used, 1)
    return packed.astype(BF)


def unpack_moments(total, used):
    width = total.shape[1]
    return total + pltpu.roll(total, width - used, 1) + pltpu.roll(total, width - 2 * used, 1)


def store_for_all(out_ref, dens_halves, moments):
    pairs, _, tiles, blocks = out_ref.shape[:4]

    def one(g, carry):
        for h in range(2):
            for t in range(tiles):
                for k in range(blocks - 1):
                    out_ref[g, h, t, k] = dens_halves[k][h]
                out_ref[g, h, t, blocks - 1] = moments
        return carry

    lax.fori_loop(0, pairs, one, 0, unroll=True)


def project(block, coeff):
    high, low = split2(block)
    both = mm(jnp.concatenate([high, low], 0), coeff, NT)
    v = block.shape[0]
    total = both[:v] + both[v:]
    half = total.shape[1] // 2
    return [total[:, :half].astype(BF), total[:, half:].astype(BF)]


def start_kernel(x_hbm, e_hbm, c_hbm, out_ref, x_ref, e_ref, c_ref, sems, c_sems, scratch):
    local_k, v, _ = x_ref.shape
    copies = [
        pltpu.make_async_copy(x_hbm, x_ref, sems.at[0]),
        pltpu.make_async_copy(e_hbm, e_ref, sems.at[1]),
    ]
    c_copies = [pltpu.make_async_copy(c_hbm.at[k], c_ref.at[k], c_sems.at[k]) for k in range(local_k)]
    for copy in copies + c_copies:
        copy.start()
    for copy in copies:
        copy.wait()
    halves = []
    moments = None
    for k in range(local_k):
        x = x_ref[k]
        xh, xl = split2(x)
        eh, el = split2(x * e_ref[k : k + 1, :])
        big = mm(jnp.concatenate([xh, xl], 0), jnp.concatenate([xh, eh], 0), NT)
        small = mm(xh, jnp.concatenate([xl, el], 0), NT)
        part = big[:v] + big[v:] + small
        moments = part if moments is None else moments + part
        c_copies[k].wait()
        halves.append(project(x, c_ref[k]))
    store_for_all(out_ref, halves, pack_moments(scratch, [moments]))


def gather_kernel(mine_ref, dens_ref, moments_ref):
    groups, tiles, blocks = mine_ref.shape[:3]
    local_k = blocks - 1
    moments = None
    for g in range(groups):
        for k in range(local_k):
            total = mine_ref[g, 0, k].astype(F4)
            for t in range(1, tiles):
                total = total + mine_ref[g, t, k].astype(F4)
            dens_ref[g * local_k + k] = total
        for t in range(tiles):
            block = mine_ref[g, t, local_k].astype(F4)
            moments = block if moments is None else moments + block
    moments_ref[...] = moments


CHUNKS = 4


class Tasks:
    def __init__(self, assign_hbm, ranks_hbm, screen_hbm, core_ref, scratch):
        self.assign, self.ranks, self.screen, self.acc, self.dens_b, self.sems, self.small = scratch
        self.core = core_ref[0]
        chunk = self.screen.shape[0] // CHUNKS
        self.heads = [
            pltpu.make_async_copy(assign_hbm, self.assign, self.sems.at[CHUNKS]),
            pltpu.make_async_copy(ranks_hbm, self.ranks, self.sems.at[CHUNKS + 1]),
        ]
        self.chunks = []
        for i in range(CHUNKS):
            part = pl.ds(i * chunk, chunk)
            self.chunks.append(
                pltpu.make_async_copy(screen_hbm.at[part], self.screen.at[part], self.sems.at[i])
            )
        for copy in self.heads + self.chunks:
            copy.start()
        self.acc[...] = jnp.zeros(self.acc.shape, F4)

    def set_dens(self, dens_ref, which, k, dens):
        slot = (self.core + which) % 2
        dens_ref[slot, k] = dens
        self.dens_b[slot, k] = dens.astype(BF)

    def run(self, dens_ref, keep_ref, send_ref, coupled_ref):
        total_k, v, half = self.dens_b.shape[1:]
        lane = lax.broadcasted_iota(jnp.int32, (v, 2 * half), 1)
        for copy in self.heads:
            copy.wait()

        def one(t, carry):
            pair = self.assign[t]
            row = pair // total_k
            col = pair - row * total_k
            keep = lane < self.ranks[row, col]
            vec = jnp.concatenate([self.dens_b[0, col], self.dens_b[1, col]], 1)
            vec = jnp.where(keep, vec, 0.0).astype(BF)
            term = jnp.where(keep, mm(vec, self.screen[t], NT), 0.0)
            self.acc[0, row] = self.acc[0, row] + term[:, :half]
            self.acc[1, row] = self.acc[1, row] + term[:, half:]
            return carry

        chunk = self.screen.shape[0] // CHUNKS
        for i in range(CHUNKS):
            self.chunks[i].wait()
            lax.fori_loop(i * chunk, (i + 1) * chunk, one, 0, unroll=True)
        total = None
        for k in range(total_k):
            for h in range(2):
                rh, rl = split2(self.acc[h, k])
                dh, dl = split2(dens_ref[h, k])
                big = mm(jnp.concatenate([rh, rl], 0), dh, NT)
                part = big[:v] + big[v:] + mm(rh, dl, NT)
                total = part if total is None else total + part
            keep_ref[k] = self.acc[self.core, k]
            send_ref[k] = self.acc[1 - self.core, k]
        coupled_ref[...] = pack_moments(self.small, [total])


def pad_small(scratch, small):
    scratch[...] = jnp.zeros(scratch.shape, F4)
    scratch[:, 0 : small.shape[1]] = small
    return scratch[...]


def first_tasks_kernel(core_ref, assign_hbm, ranks_hbm, screen_hbm, mine_ref, other_ref, moments_ref,
                       keep_ref, send_ref, coupled_ref, dens_ref, small_ref, *scratch, count):
    tasks = Tasks(assign_hbm, ranks_hbm, screen_hbm, core_ref, scratch)
    v = mine_ref.shape[1]
    moments = unpack_moments(moments_ref[...], 2 * v)
    inverse = inverse_cholesky(moments[:, 0:v] / count)
    for k in range(mine_ref.shape[0]):
        for which, ref in ((0, mine_ref), (1, other_ref)):
            tasks.set_dens(dens_ref, which, k, apply_small(inverse, ref[k]))
    tasks.run(dens_ref, keep_ref, send_ref, coupled_ref)
    weighted = moments[:, v : 2 * v] / count
    diag = exact(exact(inverse, weighted, NN), inverse, NT)
    small_ref[0] = pad_small(tasks.small, inverse)
    small_ref[1] = pad_small(tasks.small, diag)


def next_tasks_kernel(core_ref, assign_hbm, ranks_hbm, screen_hbm, mine_ref, other_ref, moments_ref,
                      prev_dens_ref, prev_small_ref, keep_ref, send_ref, coupled_ref, dens_ref,
                      small_ref, *scratch, count):
    tasks = Tasks(assign_hbm, ranks_hbm, screen_hbm, core_ref, scratch)
    v = mine_ref.shape[1]
    moments = unpack_moments(moments_ref[...], 4 * v) / count
    pp = moments[:, 0:v]
    mix = moments[:, v : 2 * v]
    inverse = inverse_cholesky(pp - exact(mix, mix, NT))
    both = apply_small(inverse, mix)
    for k in range(mine_ref.shape[0]):
        for which, ref in ((0, mine_ref), (1, other_ref)):
            dens = apply_small(inverse, ref[k])
            dens = dens - apply_small(both, prev_dens_ref[(tasks.core + which) % 2, k])
            tasks.set_dens(dens_ref, which, k, dens)
    tasks.run(dens_ref, keep_ref, send_ref, coupled_ref)
    rp = moments[:, 2 * v : 3 * v]
    rv = moments[:, 3 * v : 4 * v]
    prev_diag = prev_small_ref[1][:, 0:v]
    weighted = rp - exact(rv, mix, NT) - exact(mix, rv, NT) + exact(exact(mix, prev_diag, NN), mix, NT)
    diag = exact(exact(inverse, weighted, NN), inverse, NT)
    small_ref[0] = pad_small(tasks.small, inverse)
    small_ref[1] = pad_small(tasks.small, diag)
    small_ref[2] = pad_small(tasks.small, both)


def rows_kernel(keep_ref, recv_ref, coupled_ref, out_ref):
    groups, tiles, blocks = out_ref.shape[:3]
    local_k = blocks - 1
    for g in range(groups):
        for k in range(local_k):
            rows = (keep_ref[g * local_k + k] + recv_ref[g * local_k + k]).astype(BF)
            for t in range(tiles):
                out_ref[g, t, k] = rows
        for t in range(tiles):
            out_ref[g, t, local_k] = coupled_ref[...]


def sum_rows(recv_ref):
    pairs, _, tiles, blocks, v, _ = recv_ref.shape

    def summed(block, halves):
        total = None
        for g in range(pairs):
            for h in halves:
                for t in range(tiles):
                    part = recv_ref[g, h, t, block].astype(F4)
                    total = part if total is None else total + part
        return total

    rows = []
    for k in range(blocks - 1):
        rows.append(jnp.concatenate([summed(k, (0,)), summed(k, (1,))], 1).astype(BF))
    return rows, unpack_moments(summed(blocks - 1, (0, 1)), v)[:, 0:v]


def after_first_kernel(recv_ref, x_ref, e_ref, c_ref, small_ref, out_ref, v_ref, p_ref, ray_ref, scratch, *, count):
    local_k, v, _ = x_ref.shape
    rows, coupled_part = sum_rows(recv_ref)
    inverse = small_ref[0][:, 0:v]
    ray = small_ref[1][:, 0:v] + coupled_part / count
    ray_ref[...] = pad_small(scratch, ray)
    halves = []
    moments = None
    for k in range(local_k):
        basis = apply_small(inverse, x_ref[k])
        energy = e_ref[k : k + 1, :]
        sigma = energy * basis + mm(rows[k], c_ref[k], NN)
        residual = sigma - apply_small(ray, basis)
        precond = residual / energy
        v_ref[k] = basis
        p_ref[k] = precond
        halves.append(project(precond, c_ref[k]))
        bh, bl = split2(basis)
        rh, rl = split2(residual)
        ph, pw = split2(precond)
        big = mm(jnp.concatenate([ph, rh, pw, rl], 0), jnp.concatenate([ph, bh], 0), NT)
        small = mm(jnp.concatenate([ph, rh], 0), jnp.concatenate([pw, bl], 0), NT)
        part = big[: 2 * v] + big[2 * v :] + small
        moments = part if moments is None else moments + part
    store_for_all(out_ref, halves, pack_moments(scratch, [moments[:v], moments[v:]]))


def last_rows_kernel(recv_ref, v_ref, p_ref, e_ref, c_ref, small_ref, out_ref, res_ref, basis_ref, q_ref, ray_ref, scratch, *, count):
    local_k, v, _ = v_ref.shape
    rows, coupled_part = sum_rows(recv_ref)
    inverse = small_ref[0][:, 0:v]
    both = small_ref[2][:, 0:v]
    ray = small_ref[1][:, 0:v] + coupled_part / count
    ray_ref[...] = pad_small(scratch, ray)
    moments = None
    for k in range(local_k):
        basis = apply_small(inverse, p_ref[k]) - apply_small(both, v_ref[k])
        energy = e_ref[k : k + 1, :]
        sigma = energy * basis + mm(rows[k], c_ref[k], NN)
        residual = sigma - apply_small(ray, basis)
        precond = residual / energy
        res_ref[k] = residual
        basis_ref[k] = basis
        q_ref[k] = precond
        bh, bl = split2(basis)
        ph, pw = split2(precond)
        big = mm(jnp.concatenate([ph, pw], 0), jnp.concatenate([ph, bh], 0), NT)
        part = big[:v] + big[v:] + mm(ph, jnp.concatenate([pw, bl], 0), NT)
        moments = part if moments is None else moments + part
    packed = pack_moments(scratch, [moments])
    for d in range(out_ref.shape[0]):
        out_ref[d] = packed


def finish_kernel(recv_ref, q_ref, b_ref, ray0_ref, ray1_ref, out_ref, ray_ref, *, count):
    local_k, v, _ = q_ref.shape
    total = recv_ref[0].astype(F4)
    for d in range(1, recv_ref.shape[0]):
        total = total + recv_ref[d].astype(F4)
    moments = unpack_moments(total, 2 * v) / count
    mix = moments[:, v : 2 * v]
    inverse = inverse_cholesky(moments[:, 0:v] - exact(mix, mix, NT))
    both = exact(inverse, mix, NN)
    for k in range(local_k):
        out_ref[k] = apply_small(inverse, q_ref[k]) - apply_small(both, b_ref[k])
    ray_ref[0] = ray0_ref[:, 0:v].T
    ray_ref[1] = ray1_ref[:, 0:v].T


VM = pl.BlockSpec(memory_space=pltpu.VMEM)
SM = pl.BlockSpec(memory_space=pltpu.SMEM)
ANY = pl.BlockSpec(memory_space=pltpu.HBM)


def call(body, outs, ins, args, scratch=()):
    args = [
        pltpu.with_memory_space_constraint(arg, pltpu.HBM) if spec is ANY else arg
        for arg, spec in zip(args, ins)
    ]
    return pl.pallas_call(
        body,
        out_shape=outs,
        in_specs=ins,
        out_specs=jax.tree.map(lambda _: VM, outs),
        scratch_shapes=scratch,
        compiler_params=pltpu.CompilerParams(vmem_limit_bytes=16 << 20),
    )(*args)


def per_device(coeff, energy, ranks, assign, screen, initial):
    groups = lax.axis_size("grp")
    tiles = lax.axis_size("tile")
    devices = groups * tiles
    pairs = groups // 2
    local_k, v, width = initial.shape
    levels = coeff.shape[1]
    half = levels // 2
    total_k = local_k * groups
    count = float(total_k * width * tiles)
    core = (lax.axis_index("grp") % 2).reshape(1)
    axes = ("grp", "tile")
    swap = [(g, g ^ 1) for g in range(groups)]
    sds = jax.ShapeDtypeStruct
    small_scratch = pltpu.VMEM((v, half), F4)
    dma = pltpu.SemaphoreType.DMA
    half_shape = sds((total_k, v, half), F4)

    def exchange(blocks, shape):
        sent = blocks.reshape((devices,) + blocks.shape[-3:])
        return lax.all_to_all(sent, axes, 0, 0, tiled=True).reshape(shape + sent.shape[1:])

    def to_all(blocks):
        got = exchange(blocks, (groups, tiles))
        mine, moments = call(gather_kernel, (half_shape, sds((v, half), F4)), [VM], (got,))
        return mine, lax.ppermute(mine, "grp", swap), moments

    def to_owner(keep, send, coupled):
        recv = lax.ppermute(send, "grp", swap)
        shape = sds((groups, tiles, local_k + 1, v, half), BF)
        out = call(rows_kernel, shape, [VM] * 3, (keep, recv, coupled))
        return exchange(out, (pairs, 2, tiles))

    all_shape = sds((pairs, 2, tiles, local_k + 1, v, half), BF)
    task_outs = (half_shape, half_shape, sds((v, half), BF), sds((2, total_k, v, half), F4))
    task_scratch = (
        pltpu.SMEM(assign.shape, jnp.int32),
        pltpu.SMEM(ranks.shape, jnp.int32),
        pltpu.VMEM(screen.shape, BF),
        pltpu.VMEM((2, total_k, v, half), F4),
        pltpu.VMEM((2, total_k, v, half), BF),
        dma((CHUNKS + 2,)),
        small_scratch,
    )
    task_ins = [SM, ANY, ANY, ANY]
    flat = sds((local_k, v, width), F4)
    ray_shape = sds((v, half), F4)

    sent = call(
        start_kernel,
        all_shape,
        [ANY] * 3,
        (initial, energy, coeff),
        (
            pltpu.VMEM(initial.shape, F4),
            pltpu.VMEM(energy.shape, F4),
            pltpu.VMEM(coeff.shape, BF),
            dma((2,)),
            dma((local_k,)),
            small_scratch,
        ),
    )
    mine, other, moments = to_all(sent)
    keep, send, coupled, dens, small = call(
        functools.partial(first_tasks_kernel, count=count),
        task_outs + (sds((2, v, half), F4),),
        task_ins + [VM] * 3,
        (core, assign, ranks, screen, mine, other, moments),
        task_scratch,
    )
    got = to_owner(keep, send, coupled)
    sent, basis, precond, ray0 = call(
        functools.partial(after_first_kernel, count=count),
        (all_shape, flat, flat, ray_shape),
        [VM] * 5,
        (got, initial, energy, coeff, small),
        (small_scratch,),
    )
    mine, other, moments = to_all(sent)
    keep, send, coupled, dens, small = call(
        functools.partial(next_tasks_kernel, count=count),
        task_outs + (sds((3, v, half), F4),),
        task_ins + [VM] * 5,
        (core, assign, ranks, screen, mine, other, moments, dens, small),
        task_scratch,
    )
    got = to_owner(keep, send, coupled)
    sent, residual, basis, precond, ray1 = call(
        functools.partial(last_rows_kernel, count=count),
        (sds((devices, v, half), BF), flat, flat, flat, ray_shape),
        [VM] * 6,
        (got, basis, precond, energy, coeff, small),
        (small_scratch,),
    )
    got = lax.all_to_all(sent, axes, 0, 0, tiled=True)
    basis, rayleigh = call(
        functools.partial(finish_kernel, count=count),
        (flat, sds((2, v, v), F4)),
        [VM] * 5,
        (got, precond, basis, ray0, ray1),
    )
    return (rayleigh, basis, residual)


def solution(mesh):
    placed = (
        P("grp", None, "tile"),
        P("grp", "tile"),
        P(),
        P(("grp", "tile")),
        P(("grp", "tile"), None, None),
        P("grp", None, "tile"),
    )
    return jax.shard_map(
        per_device,
        mesh=mesh,
        in_specs=placed,
        out_specs=(P(), P("grp", None, "tile"), P("grp", None, "tile")),
        check_vma=False,
    )
```

time: 117 us -> 94.6 us (0.81)
  blocking collectives: 48.4 us -> 70 us
  waiting for transfers between devices: 22.8 us -> 3.95 us
  Pallas kernels: 30.2 us -> 17.1 us
  starting transfers between devices: 8.68 us -> 2.59 us
  local copies, waits for them, and re-layouts: 4.9 us -> 0.01 us
    all_to_all x3 -> x5, blocking collectives: 48.4 us -> 70 us  [the longest x4 59.5 us: exchange(): lax.all_to_all(sent, axes, 0, 0, tiled=True).reshape(shape + sent.shape[1:])]
    all_to_all x2 -> x0, waiting for transfers between devices: 17.9 us -> none  [the longest x1 11.7 us: to_owner(): lax.all_to_all(out, axes, 0, 0, tiled=True, axis_index_groups=same_core)]
    pallas_call x8 -> x10, Pallas kernels: 30.2 us -> 17.1 us  [call(): pl.pallas_call(body, out_shape=outs, in_specs=ins, out_specs=jax.tree.map...]
    all_to_all x2 -> x0, starting transfers between devices: 6.32 us -> none  [the longest x1 3.76 us: to_owner(): lax.all_to_all(out, axes, 0, 0, tiled=True, axis_index_groups=same_core)]
    unnamed x18 -> x6, local copies, waits for them, and re-layouts: 4.06 us -> 0.01 us
  transfers between devices with their start and end apart: 6 -> 4, of which waited for: 6 -> 4; matrix products, arithmetic and copies ran while one was open for 1% -> 0% of each run, Pallas kernels for 0% -> 0%
where the time goes in v2:
time: 94.6 us; the launch traced here: 94.4 us
  blocking collectives  70 us (74%)
  Pallas kernels  17.1 us (18%)
  waiting for transfers between devices  3.95 us (4%)
  starting transfers between devices  2.59 us (3%)
    all_to_all x4, blocking collectives, exchange(): lax.all_to_all(sent, axes, 0, 0, tiled=True).reshape(shape + sent.shape[1:])  59.5 us
    pallas_call x10, Pallas kernels, call(): pl.pallas_call(body, out_shape=outs, in_specs=ins, out_specs=jax.tree.map...  17.1 us
    all_to_all x1, blocking collectives, per_device(): got = lax.all_to_all(sent, axes, 0, 0, tiled=True)  10.5 us
    ppermute x2, waiting for transfers between devices, to_owner(): recv = lax.ppermute(send, 'grp', swap)  1.97 us
    ppermute x2, waiting for transfers between devices, to_all(): return (mine, lax.ppermute(mine, 'grp', swap), moments)  1.97 us
  transfers between devices with their start and end apart: 4, of which 4 were waited for; matrix products, arithmetic and copies ran while one was open for 0% of the time, Pallas kernels for 0%

profile of v2, /device:TPU:0, one launch (start us, length us, event | category | flops | bytes accessed | tf_op | source)
XLA Modules:
  0.0 94.4 jit_solution(14225111748285502312)
XLA Ops:
  0.6 0.0 copy-start.2
  0.6 0.0 copy-start
  0.7 0.0 copy-start.1
  0.7 3.2 %shard_map.85 = bf16[4,2,4,5,8,128]{5,4,3,2,1,0:T(8,128)(2,1)S(1)} custom-call(f32[4,8,1024]{2,1,0:T(8,128)} %x_ref.1, f32[4,1024]{1,0:T(4,128)} %e_ref.3, bf16[4,256,1024]{2,1,0:T(8,128)(2,1)} %c_ref.3), custom_call_target="tpu_custom_call" | custom-call | tf_op jit(solution)/shard_map/pallas_call | solution.py:366
  3.9 18.2 %all_to_all.25 = bf16[32,5,8,128]{3,2,1,0:T(8,128)(2,1)S(1)} all-to-all(bf16[32,5,8,128]{3,2,1,0:T(8,128)(2,1)S(1)} %bitcast.10), channel_id=1, replica_groups=mesh['grp'=8,'tile'=4] {'grp','tile'}, dimensions={0} | all-to-all | bytes 655360 | tf_op jit(solution)/shard_map/all_to_all | solution.py:396
  22.1 0.1 shard_map.86
  22.2 0.9 collective-permute-start
  23.0 1.0 %collective-permute-done.other_ref = f32[32,8,128]{2,1,0:T(8,128)S(1)} collective-permute-done((f32[32,8,128]{2,1,0:T(8,128)S(1)}, f32[32,8,128]{2,1,0:T(8,128)S(1)}, u32[]{:S(2)}, u32[]{:S(2)}) %collective-permute-start) | collective-permute-done | bytes 131104 | tf_op jit(solution)/shard_map/ppermute | solution.py:401
  24.0 3.5 %shard_map.87 = (f32[32,8,128]{2,1,0:T(8,128)S(1)}, f32[32,8,128]{2,1,0:T(8,128)S(1)}, bf16[8,128]{1,0:T(8,128)(2,1)S(1)}, f32[2,32,8,128]{3,2,1,0:T(8,128)S(1)}, f32[2,8,128]{2,1,0:T(8,128)S(1)}) custom-call(s32[1]{0:T(128)} %bitcast.core_ref, s32[32]{0:T(128)} %assign_hbm.3, s32[32,32]{1,0:T(8,128)} %ranks_hbm.3, bf16[32,256,256]{2,1,0:T(8,128)(2,1)} %screen_hbm.3, ...), custom_call_target="tpu_custom_call" | custom-call | tf_op jit(solution)/shard_map/pallas_call | solution.py:366
  27.6 0.4 collective-permute-start.1
  28.0 1.0 %collective-permute-done.1.recv_ref = f32[32,8,128]{2,1,0:T(8,128)S(1)} collective-permute-done((f32[32,8,128]{2,1,0:T(8,128)S(1)}, f32[32,8,128]{2,1,0:T(8,128)S(1)}, u32[]{:S(2)}, u32[]{:S(2)}) %collective-permute-start.1) | collective-permute-done | bytes 131104 | tf_op jit(solution)/shard_map/ppermute | solution.py:404
  29.0 13.6 %all_to_all.26 = bf16[32,5,8,128]{3,2,1,0:T(8,128)(2,1)S(1)} all-to-all(bf16[32,5,8,128]{3,2,1,0:T(8,128)(2,1)S(1)} %bitcast.12), channel_id=1, replica_groups=mesh['grp'=8,'tile'=4] {'grp','tile'}, dimensions={0} | all-to-all | bytes 655360 | tf_op jit(solution)/shard_map/all_to_all | solution.py:396
  42.7 0.0 copy-done.2
  42.7 0.0 copy-done
  42.7 0.0 copy-done.1
  42.7 1.4 %shard_map.89 = (bf16[4,2,4,5,8,128]{5,4,3,2,1,0:T(8,128)(2,1)S(1)}, f32[4,8,1024]{2,1,0:T(8,128)S(1)}, f32[4,8,1024]{2,1,0:T(8,128)S(1)}, f32[8,128]{1,0:T(8,128)S(1)}) custom-call(bf16[4,2,4,5,8,128]{5,4,3,2,1,0:T(8,128)(2,1)S(1)} %bitcast.9, f32[4,8,1024]{2,1,0:T(8,128)S(1)} %copy-done.1, f32[4,1024]{1,0:T(4,128)S(1)} %copy-done.2, ...), custom_call_target="tpu_custom_call" | custom-call | tf_op jit(solution)/shard_map/pallas_call | solution.py:366
  44.1 14.1 %all_to_all.27 = bf16[32,5,8,128]{3,2,1,0:T(8,128)(2,1)S(1)} all-to-all(bf16[32,5,8,128]{3,2,1,0:T(8,128)(2,1)S(1)} %bitcast.16), channel_id=1, replica_groups=mesh['grp'=8,'tile'=4] {'grp','tile'}, dimensions={0} | all-to-all | bytes 655360 | tf_op jit(solution)/shard_map/all_to_all | solution.py:396
  58.2 0.1 shard_map.90
  58.3 0.9 collective-permute-start.2
  59.1 1.0 %collective-permute-done.2.other_ref = f32[32,8,128]{2,1,0:T(8,128)S(1)} collective-permute-done((f32[32,8,128]{2,1,0:T(8,128)S(1)}, f32[32,8,128]{2,1,0:T(8,128)S(1)}, u32[]{:S(2)}, u32[]{:S(2)}) %collective-permute-start.2) | collective-permute-done | bytes 131104 | tf_op jit(solution)/shard_map/ppermute | solution.py:401
  60.1 5.2 %shard_map.91 = (f32[32,8,128]{2,1,0:T(8,128)S(1)}, f32[32,8,128]{2,1,0:T(8,128)S(1)}, bf16[8,128]{1,0:T(8,128)(2,1)S(1)}, f32[2,32,8,128]{3,2,1,0:T(8,128)}, f32[3,8,128]{2,1,0:T(8,128)S(1)}) custom-call(s32[1]{0:T(128)} %bitcast.core_ref, s32[32]{0:T(128)} %assign_hbm.3, s32[32,32]{1,0:T(8,128)} %ranks_hbm.3, bf16[32,256,256]{2,1,0:T(8,128)(2,1)} %screen_hbm.3, ...), custom_call_target="tpu_custom_call" | custom-call | tf_op jit(solution)/shard_map/pallas_call | solution.py:366
  65.3 0.4 collective-permute-start.3
  65.7 1.0 %collective-permute-done.3.recv_ref = f32[32,8,128]{2,1,0:T(8,128)S(1)} collective-permute-done((f32[32,8,128]{2,1,0:T(8,128)S(1)}, f32[32,8,128]{2,1,0:T(8,128)S(1)}, u32[]{:S(2)}, u32[]{:S(2)}) %collective-permute-start.3) | collective-permute-done | bytes 131104 | tf_op jit(solution)/shard_map/ppermute | solution.py:404
  66.7 13.6 %all_to_all.28 = bf16[32,5,8,128]{3,2,1,0:T(8,128)(2,1)S(1)} all-to-all(bf16[32,5,8,128]{3,2,1,0:T(8,128)(2,1)S(1)} %bitcast.14), channel_id=1, replica_groups=mesh['grp'=8,'tile'=4] {'grp','tile'}, dimensions={0} | all-to-all | bytes 655360 | tf_op jit(solution)/shard_map/all_to_all | solution.py:396
  80.4 1.5 %shard_map.93 = (bf16[32,8,128]{2,1,0:T(8,128)(2,1)S(1)}, f32[4,8,1024]{2,1,0:T(8,128)}, f32[4,8,1024]{2,1,0:T(8,128)S(1)}, f32[4,8,1024]{2,1,0:T(8,128)S(1)}, f32[8,128]{1,0:T(8,128)S(1)}) custom-call(bf16[4,2,4,5,8,128]{5,4,3,2,1,0:T(8,128)(2,1)S(1)} %bitcast.15, f32[4,8,1024]{2,1,0:T(8,128)S(1)} %get-tuple-element.40.v_ref, ...), custom_call_target="tpu_custom_call" | custom-call | tf_op jit(solution)/shard_map/pallas_call | solution.py:366
  81.9 10.5 %all_to_all.29.recv_ref = bf16[32,8,128]{2,1,0:T(8,128)(2,1)S(1)} all-to-all(bf16[32,8,128]{2,1,0:T(8,128)(2,1)S(1)} %get-tuple-element.43), channel_id=1, replica_groups=mesh['grp'=8,'tile'=4] {'grp','tile'}, dimensions={0} | all-to-all | bytes 131072 | tf_op jit(solution)/shard_map/all_to_all | solution.py:470
  92.4 2.0 %shard_map.94 = (f32[4,8,1024]{2,1,0:T(8,128)}, f32[2,8,8]{2,1,0:T(8,128)}) custom-call(bf16[32,8,128]{2,1,0:T(8,128)(2,1)S(1)} %all_to_all.29.recv_ref, f32[4,8,1024]{2,1,0:T(8,128)S(1)} %get-tuple-element.44.q_ref, f32[4,8,1024]{2,1,0:T(8,128)S(1)} %get-tuple-element.45.b_ref, f32[8,128]{1,0:T(8,128)S(1)} %get-tuple-element.46.ray0_ref, ...), custom_call_target="tpu_custom_call" | custom-call | tf_op jit(solution)/shard_map/pallas_call | solution.py:366
  (2 shorter events, 0.1 us)
Async XLA Ops:
  0.6 42.0 %copy-start.2 = (f32[4,1024]{1,0:T(4,128)S(1)}, f32[4,1024]{1,0:T(4,128)}, u32[]{:S(2)}) copy-start(f32[4,1024]{1,0:T(4,128)} %e_ref.3) | copy-start | bytes 49156
  0.6 42.0 %copy-start = (bf16[4,256,1024]{2,1,0:T(8,128)(2,1)S(1)}, bf16[4,256,1024]{2,1,0:T(8,128)(2,1)}, u32[]{:S(2)}) copy-start(bf16[4,256,1024]{2,1,0:T(8,128)(2,1)} %c_ref.3) | copy-start | bytes 6291460
  0.7 42.0 %copy-start.1 = (f32[4,8,1024]{2,1,0:T(8,128)S(1)}, f32[4,8,1024]{2,1,0:T(8,128)}, u32[]{:S(2)}) copy-start(f32[4,8,1024]{2,1,0:T(8,128)} %x_ref.1) | copy-start | bytes 393220
  22.2 1.9 %collective-permute-start = (f32[32,8,128]{2,1,0:T(8,128)S(1)}, f32[32,8,128]{2,1,0:T(8,128)S(1)}, u32[]{:S(2)}, u32[]{:S(2)}) collective-permute-start(f32[32,8,128]{2,1,0:T(8,128)S(1)} %get-tuple-element.27.mine_ref), channel_id=1, source_target_pairs={{0,4},{4,0},{8,12},{12,8},{16,20},{20,16},{24,28},{28,24},{1,5},{5... | collective-permute-start | bytes 393224 | tf_op jit(solution)/shard_map/ppermute | solution.py:401
  27.6 1.4 %collective-permute-start.1 = (f32[32,8,128]{2,1,0:T(8,128)S(1)}, f32[32,8,128]{2,1,0:T(8,128)S(1)}, u32[]{:S(2)}, u32[]{:S(2)}) collective-permute-start(f32[32,8,128]{2,1,0:T(8,128)S(1)} %get-tuple-element.30), channel_id=1, source_target_pairs={{0,4},{4,0},{8,12},{12,8},{16,20},{20,16},{24,28},{28,24},{1,5},{5... | collective-permute-start | bytes 393224 | tf_op jit(solution)/shard_map/ppermute | solution.py:404
  58.3 1.9 %collective-permute-start.2 = (f32[32,8,128]{2,1,0:T(8,128)S(1)}, f32[32,8,128]{2,1,0:T(8,128)S(1)}, u32[]{:S(2)}, u32[]{:S(2)}) collective-permute-start(f32[32,8,128]{2,1,0:T(8,128)S(1)} %get-tuple-element.34.mine_ref), channel_id=1, source_target_pairs={{0,4},{4,0},{8,12},{12,8},{16,20},{20,16},{24,28},{28,24},{1,5},{5... | collective-permute-start | bytes 393224 | tf_op jit(solution)/shard_map/ppermute | solution.py:401
  65.3 1.4 %collective-permute-start.3 = (f32[32,8,128]{2,1,0:T(8,128)S(1)}, f32[32,8,128]{2,1,0:T(8,128)S(1)}, u32[]{:S(2)}, u32[]{:S(2)}) collective-permute-start(f32[32,8,128]{2,1,0:T(8,128)S(1)} %get-tuple-element.38), channel_id=1, source_target_pairs={{0,4},{4,0},{8,12},{12,8},{16,20},{20,16},{24,28},{28,24},{1,5},{5... | collective-permute-start | bytes 393224 | tf_op jit(solution)/shard_map/ppermute | solution.py:404

commit v3 on v2

--- a/solution.py
+++ b/solution.py
@@ -102,14 +102,15 @@
     return [total[:, :half].astype(BF), total[:, half:].astype(BF)]
 
 
-def start_kernel(x_hbm, e_hbm, c_hbm, out_ref, x_ref, e_ref, c_ref, sems, c_sems, scratch):
+def start_kernel(x_hbm, e_hbm, c_hbm, s_hbm, out_ref, x_ref, e_ref, c_ref, s_ref, sems, c_sems, scratch):
     local_k, v, _ = x_ref.shape
     copies = [
         pltpu.make_async_copy(x_hbm, x_ref, sems.at[0]),
         pltpu.make_async_copy(e_hbm, e_ref, sems.at[1]),
     ]
     c_copies = [pltpu.make_async_copy(c_hbm.at[k], c_ref.at[k], c_sems.at[k]) for k in range(local_k)]
-    for copy in copies + c_copies:
+    screen_copy = pltpu.make_async_copy(s_hbm, s_ref, sems.at[2])
+    for copy in copies + c_copies + [screen_copy]:
         copy.start()
     for copy in copies:
         copy.wait()
@@ -126,6 +127,7 @@
         c_copies[k].wait()
         halves.append(project(x, c_ref[k]))
     store_for_all(out_ref, halves, pack_moments(scratch, [moments]))
+    screen_copy.wait()
 
 
 def gather_kernel(mine_ref, dens_ref, moments_ref):
@@ -144,25 +146,16 @@
     moments_ref[...] = moments
 
 
-CHUNKS = 4
-
-
 class Tasks:
-    def __init__(self, assign_hbm, ranks_hbm, screen_hbm, core_ref, scratch):
-        self.assign, self.ranks, self.screen, self.acc, self.dens_b, self.sems, self.small = scratch
-        self.core = core_ref[0]
-        chunk = self.screen.shape[0] // CHUNKS
+    def __init__(self, assign_hbm, ranks_hbm, screen_ref, scratch):
+        self.assign, self.ranks, self.acc, self.dens_b, self.sems, self.small = scratch
+        self.screen = screen_ref
+        self.core = lax.axis_index("grp") % 2
         self.heads = [
-            pltpu.make_async_copy(assign_hbm, self.assign, self.sems.at[CHUNKS]),
-            pltpu.make_async_copy(ranks_hbm, self.ranks, self.sems.at[CHUNKS + 1]),
+            pltpu.make_async_copy(assign_hbm, self.assign, self.sems.at[0]),
+            pltpu.make_async_copy(ranks_hbm, self.ranks, self.sems.at[1]),
         ]
-        self.chunks = []
-        for i in range(CHUNKS):
-            part = pl.ds(i * chunk, chunk)
-            self.chunks.append(
-                pltpu.make_async_copy(screen_hbm.at[part], self.screen.at[part], self.sems.at[i])
-            )
-        for copy in self.heads + self.chunks:
+        for copy in self.heads:
             copy.start()
         self.acc[...] = jnp.zeros(self.acc.shape, F4)
 
@@ -189,10 +182,7 @@
             self.acc[1, row] = self.acc[1, row] + term[:, half:]
             return carry
 
-        chunk = self.screen.shape[0] // CHUNKS
-        for i in range(CHUNKS):
-            self.chunks[i].wait()
-            lax.fori_loop(i * chunk, (i + 1) * chunk, one, 0, unroll=True)
+        lax.fori_loop(0, self.screen.shape[0], one, 0, unroll=True)
         total = None
         for k in range(total_k):
             for h in range(2):
@@ -212,9 +202,9 @@
     return scratch[...]
 
 
-def first_tasks_kernel(core_ref, assign_hbm, ranks_hbm, screen_hbm, mine_ref, other_ref, moments_ref,
+def first_tasks_kernel(assign_hbm, ranks_hbm, screen_ref, mine_ref, other_ref, moments_ref,
                        keep_ref, send_ref, coupled_ref, dens_ref, small_ref, *scratch, count):
-    tasks = Tasks(assign_hbm, ranks_hbm, screen_hbm, core_ref, scratch)
+    tasks = Tasks(assign_hbm, ranks_hbm, screen_ref, scratch)
     v = mine_ref.shape[1]
     moments = unpack_moments(moments_ref[...], 2 * v)
     inverse = inverse_cholesky(moments[:, 0:v] / count)
@@ -228,10 +218,10 @@
     small_ref[1] = pad_small(tasks.small, diag)
 
 
-def next_tasks_kernel(core_ref, assign_hbm, ranks_hbm, screen_hbm, mine_ref, other_ref, moments_ref,
-                      prev_dens_ref, prev_small_ref, keep_ref, send_ref, coupled_ref, dens_ref,
-                      small_ref, *scratch, count):
-    tasks = Tasks(assign_hbm, ranks_hbm, screen_hbm, core_ref, scratch)
+def next_tasks_kernel(assign_hbm, ranks_hbm, screen_ref, mine_ref, other_ref, moments_ref,
+                      prev_dens_ref, prev_small_ref, keep_ref, send_ref, coupled_ref, small_ref,
+                      dens_ref, *scratch, count):
+    tasks = Tasks(assign_hbm, ranks_hbm, screen_ref, scratch)
     v = mine_ref.shape[1]
     moments = unpack_moments(moments_ref[...], 4 * v) / count
     pp = moments[:, 0:v]
@@ -354,11 +344,10 @@
 
 
 VM = pl.BlockSpec(memory_space=pltpu.VMEM)
-SM = pl.BlockSpec(memory_space=pltpu.SMEM)
 ANY = pl.BlockSpec(memory_space=pltpu.HBM)
 
 
-def call(body, outs, ins, args, scratch=()):
+def call(body, outs, ins, args, scratch=(), cost=None):
     args = [
         pltpu.with_memory_space_constraint(arg, pltpu.HBM) if spec is ANY else arg
         for arg, spec in zip(args, ins)
@@ -370,6 +359,7 @@
         out_specs=jax.tree.map(lambda _: VM, outs),
         scratch_shapes=scratch,
         compiler_params=pltpu.CompilerParams(vmem_limit_bytes=16 << 20),
+        cost_estimate=cost,
     )(*args)
 
 
@@ -383,7 +373,6 @@
     half = levels // 2
     total_k = local_k * groups
     count = float(total_k * width * tiles)
-    core = (lax.axis_index("grp") % 2).reshape(1)
     axes = ("grp", "tile")
     swap = [(g, g ^ 1) for g in range(groups)]
     sds = jax.ShapeDtypeStruct
@@ -407,30 +396,27 @@
         return exchange(out, (pairs, 2, tiles))
 
     all_shape = sds((pairs, 2, tiles, local_k + 1, v, half), BF)
-    task_outs = (half_shape, half_shape, sds((v, half), BF), sds((2, total_k, v, half), F4))
+    task_outs = (half_shape, half_shape, sds((v, half), BF))
+    dens_shape = (2, total_k, v, half)
     task_scratch = (
         pltpu.SMEM(assign.shape, jnp.int32),
         pltpu.SMEM(ranks.shape, jnp.int32),
-        pltpu.VMEM(screen.shape, BF),
         pltpu.VMEM((2, total_k, v, half), F4),
         pltpu.VMEM((2, total_k, v, half), BF),
-        dma((CHUNKS + 2,)),
+        dma((2,)),
         small_scratch,
     )
-    task_ins = [SM, ANY, ANY, ANY]
     flat = sds((local_k, v, width), F4)
     ray_shape = sds((v, half), F4)
 
-    sent = call(
+    inputs = (initial, energy, coeff, screen)
+    sent, initial, energy, coeff, screen = call(
         start_kernel,
-        all_shape,
-        [ANY] * 3,
-        (initial, energy, coeff),
+        (all_shape,) + tuple(sds(a.shape, a.dtype) for a in inputs),
+        [ANY] * 4,
+        inputs,
         (
-            pltpu.VMEM(initial.shape, F4),
-            pltpu.VMEM(energy.shape, F4),
-            pltpu.VMEM(coeff.shape, BF),
-            dma((2,)),
+            dma((3,)),
             dma((local_k,)),
             small_scratch,
         ),
@@ -438,9 +424,9 @@
     mine, other, moments = to_all(sent)
     keep, send, coupled, dens, small = call(
         functools.partial(first_tasks_kernel, count=count),
-        task_outs + (sds((2, v, half), F4),),
-        task_ins + [VM] * 3,
-        (core, assign, ranks, screen, mine, other, moments),
+        task_outs + (sds(dens_shape, F4), sds((2, v, half), F4)),
+        [ANY, ANY] + [VM] * 4,
+        (assign, ranks, screen, mine, other, moments),
         task_scratch,
     )
     got = to_owner(keep, send, coupled)
@@ -452,12 +438,12 @@
         (small_scratch,),
     )
     mine, other, moments = to_all(sent)
-    keep, send, coupled, dens, small = call(
+    keep, send, coupled, small = call(
         functools.partial(next_tasks_kernel, count=count),
         task_outs + (sds((3, v, half), F4),),
-        task_ins + [VM] * 5,
-        (core, assign, ranks, screen, mine, other, moments, dens, small),
-        task_scratch,
+        [ANY, ANY] + [VM] * 6,
+        (assign, ranks, screen, mine, other, moments, dens, small),
+        (pltpu.VMEM(dens_shape, F4),) + task_scratch,
     )
     got = to_owner(keep, send, coupled)
     sent, residual, basis, precond, ray1 = call(

time: 94.6 us -> 92.2 us (0.975)
  Pallas kernels: 17.1 us -> 14.7 us
    pallas_call x10, Pallas kernels: 17.1 us -> 14.7 us  [call(): pl.pallas_call(body, out_shape=outs, in_specs=ins, out_specs=jax.tree.map...]
where the time goes in v3:
time: 92.2 us; the launch traced here: 91.9 us
  blocking collectives  70 us (76%)
  Pallas kernels  14.7 us (16%)
  waiting for transfers between devices  3.95 us (4%)
  starting transfers between devices  2.6 us (3%)
    all_to_all x4, blocking collectives, exchange(): lax.all_to_all(sent, axes, 0, 0, tiled=True).reshape(shape + sent.shape[1:])  59.5 us
    pallas_call x10, Pallas kernels, call(): pl.pallas_call(body, out_shape=outs, in_specs=ins, out_specs=jax.tree.map...  14.7 us
    all_to_all x1, blocking collectives, per_device(): got = lax.all_to_all(sent, axes, 0, 0, tiled=True)  10.5 us
    ppermute x2, waiting for transfers between devices, to_owner(): recv = lax.ppermute(send, 'grp', swap)  1.97 us
    ppermute x2, waiting for transfers between devices, to_all(): return (mine, lax.ppermute(mine, 'grp', swap), moments)  1.97 us
  transfers between devices with their start and end apart: 4, of which 4 were waited for; matrix products, arithmetic and copies ran while one was open for 0% of the time, Pallas kernels for 0%

profile of v3, /device:TPU:0, one launch (start us, length us, event | category | flops | bytes accessed | tf_op | source)
XLA Modules:
  0.0 91.9 jit_solution(10644335443817509037)
XLA Ops:
  0.6 3.0 %shard_map.85 = (bf16[4,2,4,5,8,128]{5,4,3,2,1,0:T(8,128)(2,1)S(1)}, f32[4,8,1024]{2,1,0:T(8,128)S(1)}, f32[4,1024]{1,0:T(4,128)S(1)}, bf16[4,256,1024]{2,1,0:T(8,128)(2,1)S(1)}, bf16[32,256,256]{2,1,0:T(8,128)(2,1)S(1)}) custom-call(f32[4,8,1024]{2,1,0:T(8,128)} %x_hbm.1, f32[4,1024]{1,0:T(4,128)} %e_hbm.1, bf16[4,256,1024]{2,1,0:T(8,128)(2,1)} %c_hbm.1, ...), custom_call_target="tpu_custom_call" | custom-call | tf_op jit(solution)/shard_map/pallas_call | solution.py:355
  3.6 18.2 %all_to_all.25 = bf16[32,5,8,128]{3,2,1,0:T(8,128)(2,1)S(1)} all-to-all(bf16[32,5,8,128]{3,2,1,0:T(8,128)(2,1)S(1)} %bitcast.15), channel_id=1, replica_groups=mesh['grp'=8,'tile'=4] {'grp','tile'}, dimensions={0} | all-to-all | bytes 655360 | tf_op jit(solution)/shard_map/all_to_all | solution.py:385
  21.8 0.1 shard_map.86
  21.9 0.9 collective-permute-start
  22.7 1.0 %collective-permute-done.other_ref = f32[32,8,128]{2,1,0:T(8,128)S(1)} collective-permute-done((f32[32,8,128]{2,1,0:T(8,128)S(1)}, f32[32,8,128]{2,1,0:T(8,128)S(1)}, u32[]{:S(2)}, u32[]{:S(2)}) %collective-permute-start) | collective-permute-done | bytes 131104 | tf_op jit(solution)/shard_map/ppermute | solution.py:390
  23.7 2.9 %shard_map.87 = (f32[32,8,128]{2,1,0:T(8,128)S(1)}, f32[32,8,128]{2,1,0:T(8,128)S(1)}, bf16[8,128]{1,0:T(8,128)(2,1)S(1)}, f32[2,32,8,128]{3,2,1,0:T(8,128)S(1)}, f32[2,8,128]{2,1,0:T(8,128)S(1)}) custom-call(s32[32]{0:T(128)} %assign_hbm.3, s32[32,32]{1,0:T(8,128)} %ranks_hbm.3, bf16[32,256,256]{2,1,0:T(8,128)(2,1)S(1)} %get-tuple-element.32.screen_ref, ...), custom_call_target="tpu_custom_call" | custom-call | tf_op jit(solution)/shard_map/pallas_call | solution.py:355
  26.6 0.4 collective-permute-start.1
  27.0 1.0 %collective-permute-done.1.recv_ref = f32[32,8,128]{2,1,0:T(8,128)S(1)} collective-permute-done((f32[32,8,128]{2,1,0:T(8,128)S(1)}, f32[32,8,128]{2,1,0:T(8,128)S(1)}, u32[]{:S(2)}, u32[]{:S(2)}) %collective-permute-start.1) | collective-permute-done | bytes 131104 | tf_op jit(solution)/shard_map/ppermute | solution.py:393
  28.1 13.6 %all_to_all.26 = bf16[32,5,8,128]{3,2,1,0:T(8,128)(2,1)S(1)} all-to-all(bf16[32,5,8,128]{3,2,1,0:T(8,128)(2,1)S(1)} %bitcast.10), channel_id=1, replica_groups=mesh['grp'=8,'tile'=4] {'grp','tile'}, dimensions={0} | all-to-all | bytes 655360 | tf_op jit(solution)/shard_map/all_to_all | solution.py:385
  41.7 1.5 %shard_map.89 = (bf16[4,2,4,5,8,128]{5,4,3,2,1,0:T(8,128)(2,1)S(1)}, f32[4,8,1024]{2,1,0:T(8,128)S(1)}, f32[4,8,1024]{2,1,0:T(8,128)S(1)}, f32[8,128]{1,0:T(8,128)S(1)}) custom-call(bf16[4,2,4,5,8,128]{5,4,3,2,1,0:T(8,128)(2,1)S(1)} %bitcast.8, f32[4,8,1024]{2,1,0:T(8,128)S(1)} %get-tuple-element.39.x_ref, f32[4,1024]{1,0:T(4,128)S(1)} %get-tuple-element.40.e_ref, ...), custom_call_target="tpu_custom_call" | custom-call | tf_op jit(solution)/shard_map/pallas_call | solution.py:355
  43.2 14.1 %all_to_all.27 = bf16[32,5,8,128]{3,2,1,0:T(8,128)(2,1)S(1)} all-to-all(bf16[32,5,8,128]{3,2,1,0:T(8,128)(2,1)S(1)} %bitcast.14), channel_id=1, replica_groups=mesh['grp'=8,'tile'=4] {'grp','tile'}, dimensions={0} | all-to-all | bytes 655360 | tf_op jit(solution)/shard_map/all_to_all | solution.py:385
  57.2 0.1 shard_map.90
  57.3 0.9 collective-permute-start.2
  58.2 1.0 %collective-permute-done.2.other_ref = f32[32,8,128]{2,1,0:T(8,128)S(1)} collective-permute-done((f32[32,8,128]{2,1,0:T(8,128)S(1)}, f32[32,8,128]{2,1,0:T(8,128)S(1)}, u32[]{:S(2)}, u32[]{:S(2)}) %collective-permute-start.2) | collective-permute-done | bytes 131104 | tf_op jit(solution)/shard_map/ppermute | solution.py:390
  59.2 3.7 %shard_map.91 = (f32[32,8,128]{2,1,0:T(8,128)S(1)}, f32[32,8,128]{2,1,0:T(8,128)S(1)}, bf16[8,128]{1,0:T(8,128)(2,1)S(1)}, f32[3,8,128]{2,1,0:T(8,128)S(1)}) custom-call(s32[32]{0:T(128)} %assign_hbm.3, s32[32,32]{1,0:T(8,128)} %ranks_hbm.3, bf16[32,256,256]{2,1,0:T(8,128)(2,1)S(1)} %get-tuple-element.32.screen_ref, ...), custom_call_target="tpu_custom_call" | custom-call | tf_op jit(solution)/shard_map/pallas_call | solution.py:355
  62.9 0.4 collective-permute-start.3
  63.3 1.0 %collective-permute-done.3.recv_ref = f32[32,8,128]{2,1,0:T(8,128)S(1)} collective-permute-done((f32[32,8,128]{2,1,0:T(8,128)S(1)}, f32[32,8,128]{2,1,0:T(8,128)S(1)}, u32[]{:S(2)}, u32[]{:S(2)}) %collective-permute-start.3) | collective-permute-done | bytes 131104 | tf_op jit(solution)/shard_map/ppermute | solution.py:393
  64.3 13.6 %all_to_all.28 = bf16[32,5,8,128]{3,2,1,0:T(8,128)(2,1)S(1)} all-to-all(bf16[32,5,8,128]{3,2,1,0:T(8,128)(2,1)S(1)} %bitcast.12), channel_id=1, replica_groups=mesh['grp'=8,'tile'=4] {'grp','tile'}, dimensions={0} | all-to-all | bytes 655360 | tf_op jit(solution)/shard_map/all_to_all | solution.py:385
  78.0 1.5 %shard_map.93 = (bf16[32,8,128]{2,1,0:T(8,128)(2,1)S(1)}, f32[4,8,1024]{2,1,0:T(8,128)}, f32[4,8,1024]{2,1,0:T(8,128)S(1)}, f32[4,8,1024]{2,1,0:T(8,128)S(1)}, f32[8,128]{1,0:T(8,128)S(1)}) custom-call(bf16[4,2,4,5,8,128]{5,4,3,2,1,0:T(8,128)(2,1)S(1)} %bitcast.13, f32[4,8,1024]{2,1,0:T(8,128)S(1)} %get-tuple-element.50.v_ref, ...), custom_call_target="tpu_custom_call" | custom-call | tf_op jit(solution)/shard_map/pallas_call | solution.py:355
  79.5 10.5 %all_to_all.29.recv_ref = bf16[32,8,128]{2,1,0:T(8,128)(2,1)S(1)} all-to-all(bf16[32,8,128]{2,1,0:T(8,128)(2,1)S(1)} %get-tuple-element.53), channel_id=1, replica_groups=mesh['grp'=8,'tile'=4] {'grp','tile'}, dimensions={0} | all-to-all | bytes 131072 | tf_op jit(solution)/shard_map/all_to_all | solution.py:456
  90.0 1.9 %shard_map.94 = (f32[4,8,1024]{2,1,0:T(8,128)}, f32[2,8,8]{2,1,0:T(8,128)}) custom-call(bf16[32,8,128]{2,1,0:T(8,128)(2,1)S(1)} %all_to_all.29.recv_ref, f32[4,8,1024]{2,1,0:T(8,128)S(1)} %get-tuple-element.54.q_ref, f32[4,8,1024]{2,1,0:T(8,128)S(1)} %get-tuple-element.55.b_ref, f32[8,128]{1,0:T(8,128)S(1)} %get-tuple-element.56.ray0_ref, ...), custom_call_target="tpu_custom_call" | custom-call | tf_op jit(solution)/shard_map/pallas_call | solution.py:355
  (2 shorter events, 0.1 us)
Async XLA Ops:
  21.9 1.9 %collective-permute-start = (f32[32,8,128]{2,1,0:T(8,128)S(1)}, f32[32,8,128]{2,1,0:T(8,128)S(1)}, u32[]{:S(2)}, u32[]{:S(2)}) collective-permute-start(f32[32,8,128]{2,1,0:T(8,128)S(1)} %get-tuple-element.34.mine_ref), channel_id=1, source_target_pairs={{0,4},{4,0},{8,12},{12,8},{16,20},{20,16},{24,28},{28,24},{1,5},{5... | collective-permute-start | bytes 393224 | tf_op jit(solution)/shard_map/ppermute | solution.py:390
  26.6 1.4 %collective-permute-start.1 = (f32[32,8,128]{2,1,0:T(8,128)S(1)}, f32[32,8,128]{2,1,0:T(8,128)S(1)}, u32[]{:S(2)}, u32[]{:S(2)}) collective-permute-start(f32[32,8,128]{2,1,0:T(8,128)S(1)} %get-tuple-element.37), channel_id=1, source_target_pairs={{0,4},{4,0},{8,12},{12,8},{16,20},{20,16},{24,28},{28,24},{1,5},{5... | collective-permute-start | bytes 393224 | tf_op jit(solution)/shard_map/ppermute | solution.py:393
  57.3 1.9 %collective-permute-start.2 = (f32[32,8,128]{2,1,0:T(8,128)S(1)}, f32[32,8,128]{2,1,0:T(8,128)S(1)}, u32[]{:S(2)}, u32[]{:S(2)}) collective-permute-start(f32[32,8,128]{2,1,0:T(8,128)S(1)} %get-tuple-element.44.mine_ref), channel_id=1, source_target_pairs={{0,4},{4,0},{8,12},{12,8},{16,20},{20,16},{24,28},{28,24},{1,5},{5... | collective-permute-start | bytes 393224 | tf_op jit(solution)/shard_map/ppermute | solution.py:390
  62.9 1.4 %collective-permute-start.3 = (f32[32,8,128]{2,1,0:T(8,128)S(1)}, f32[32,8,128]{2,1,0:T(8,128)S(1)}, u32[]{:S(2)}, u32[]{:S(2)}) collective-permute-start(f32[32,8,128]{2,1,0:T(8,128)S(1)} %get-tuple-element.48), channel_id=1, source_target_pairs={{0,4},{4,0},{8,12},{12,8},{16,20},{20,16},{24,28},{28,24},{1,5},{5... | collective-permute-start | bytes 393224 | tf_op jit(solution)/shard_map/ppermute | solution.py:393

commit v4 on v3

--- a/solution.py
+++ b/solution.py
@@ -146,102 +146,110 @@
     moments_ref[...] = moments
 
 
-class Tasks:
-    def __init__(self, assign_hbm, ranks_hbm, screen_ref, scratch):
-        self.assign, self.ranks, self.acc, self.dens_b, self.sems, self.small = scratch
-        self.screen = screen_ref
-        self.core = lax.axis_index("grp") % 2
-        self.heads = [
-            pltpu.make_async_copy(assign_hbm, self.assign, self.sems.at[0]),
-            pltpu.make_async_copy(ranks_hbm, self.ranks, self.sems.at[1]),
-        ]
-        for copy in self.heads:
-            copy.start()
-        self.acc[...] = jnp.zeros(self.acc.shape, F4)
-
-    def set_dens(self, dens_ref, which, k, dens):
-        slot = (self.core + which) % 2
-        dens_ref[slot, k] = dens
-        self.dens_b[slot, k] = dens.astype(BF)
-
-    def run(self, dens_ref, keep_ref, send_ref, coupled_ref):
-        total_k, v, half = self.dens_b.shape[1:]
-        lane = lax.broadcasted_iota(jnp.int32, (v, 2 * half), 1)
-        for copy in self.heads:
-            copy.wait()
-
-        def one(t, carry):
-            pair = self.assign[t]
-            row = pair // total_k
-            col = pair - row * total_k
-            keep = lane < self.ranks[row, col]
-            vec = jnp.concatenate([self.dens_b[0, col], self.dens_b[1, col]], 1)
-            vec = jnp.where(keep, vec, 0.0).astype(BF)
-            term = jnp.where(keep, mm(vec, self.screen[t], NT), 0.0)
-            self.acc[0, row] = self.acc[0, row] + term[:, :half]
-            self.acc[1, row] = self.acc[1, row] + term[:, half:]
-            return carry
-
-        lax.fori_loop(0, self.screen.shape[0], one, 0, unroll=True)
-        total = None
-        for k in range(total_k):
-            for h in range(2):
-                rh, rl = split2(self.acc[h, k])
-                dh, dl = split2(dens_ref[h, k])
-                big = mm(jnp.concatenate([rh, rl], 0), dh, NT)
-                part = big[:v] + big[v:] + mm(rh, dl, NT)
-                total = part if total is None else total + part
-            keep_ref[k] = self.acc[self.core, k]
-            send_ref[k] = self.acc[1 - self.core, k]
-        coupled_ref[...] = pack_moments(self.small, [total])
-
-
 def pad_small(scratch, small):
     scratch[...] = jnp.zeros(scratch.shape, F4)
     scratch[:, 0 : small.shape[1]] = small
     return scratch[...]
 
 
-def first_tasks_kernel(assign_hbm, ranks_hbm, screen_ref, mine_ref, other_ref, moments_ref,
-                       keep_ref, send_ref, coupled_ref, dens_ref, small_ref, *scratch, count):
-    tasks = Tasks(assign_hbm, ranks_hbm, screen_ref, scratch)
-    v = mine_ref.shape[1]
+def first_factor_kernel(moments_ref, small_ref, scratch, *, count):
+    v = moments_ref.shape[0]
     moments = unpack_moments(moments_ref[...], 2 * v)
-    inverse = inverse_cholesky(moments[:, 0:v] / count)
-    for k in range(mine_ref.shape[0]):
+    small_ref[0] = pad_small(scratch, inverse_cholesky(moments[:, 0:v] / count))
+
+
+def next_factor_kernel(moments_ref, small_ref, scratch, *, count):
+    v = moments_ref.shape[0]
+    moments = unpack_moments(moments_ref[...], 4 * v) / count
+    mix = moments[:, v : 2 * v]
+    inverse = inverse_cholesky(moments[:, 0:v] - exact(mix, mix, NT))
+    small_ref[0] = pad_small(scratch, inverse)
+    small_ref[1] = pad_small(scratch, apply_small(inverse, mix))
+
+
+def own_core():
+    return lax.axis_index("grp") % 2
+
+
+def tasks_kernel(assign_hbm, ranks_hbm, screen_ref, mine_ref, other_ref, small_ref, *refs):
+    prev_dens_ref = None
+    if len(refs) > 8:
+        prev_dens_ref, refs = refs[0], refs[1:]
+    keep_ref, send_ref, dens_ref, assign_ref, ranks_ref, acc_ref, terms_ref, sems = refs
+    heads = [
+        pltpu.make_async_copy(assign_hbm, assign_ref, sems.at[0]),
+        pltpu.make_async_copy(ranks_hbm, ranks_ref, sems.at[1]),
+    ]
+    for copy in heads:
+        copy.start()
+    acc_ref[...] = jnp.zeros(acc_ref.shape, F4)
+    core = own_core()
+    total_k, v, half = mine_ref.shape
+    inverse = small_ref[0][:, 0:v]
+    for k in range(total_k):
         for which, ref in ((0, mine_ref), (1, other_ref)):
-            tasks.set_dens(dens_ref, which, k, apply_small(inverse, ref[k]))
-    tasks.run(dens_ref, keep_ref, send_ref, coupled_ref)
-    weighted = moments[:, v : 2 * v] / count
-    diag = exact(exact(inverse, weighted, NN), inverse, NT)
-    small_ref[0] = pad_small(tasks.small, inverse)
-    small_ref[1] = pad_small(tasks.small, diag)
-
-
-def next_tasks_kernel(assign_hbm, ranks_hbm, screen_ref, mine_ref, other_ref, moments_ref,
-                      prev_dens_ref, prev_small_ref, keep_ref, send_ref, coupled_ref, small_ref,
-                      dens_ref, *scratch, count):
-    tasks = Tasks(assign_hbm, ranks_hbm, screen_ref, scratch)
-    v = mine_ref.shape[1]
+            slot = (core + which) % 2
+            dens = apply_small(inverse, ref[k])
+            if prev_dens_ref is not None:
+                dens = dens - apply_small(small_ref[1][:, 0:v], prev_dens_ref[slot, k])
+            dens_ref[slot, k] = dens
+            terms_ref[slot, k] = jnp.concatenate(split2(dens), 0)
+    lane = lax.broadcasted_iota(jnp.int32, (2 * v, 2 * half), 1)
+    for copy in heads:
+        copy.wait()
+
+    def one(t, carry):
+        pair = assign_ref[t]
+        row = pair // total_k
+        col = pair - row * total_k
+        keep = lane < ranks_ref[row, col]
+        vec = jnp.concatenate([terms_ref[0, col], terms_ref[1, col]], 1)
+        vec = jnp.where(keep, vec, jnp.zeros_like(vec))
+        term = mm(vec, screen_ref[t], NT)
+        term = jnp.where(keep[:v], term[:v] + term[v:], 0.0)
+        acc_ref[0, row] = acc_ref[0, row] + term[:, :half]
+        acc_ref[1, row] = acc_ref[1, row] + term[:, half:]
+        return carry
+
+    lax.fori_loop(0, screen_ref.shape[0], one, 0, unroll=True)
+    for k in range(total_k):
+        keep_ref[k] = acc_ref[core, k]
+        send_ref[k] = acc_ref[1 - core, k]
+
+
+def coupled_part(keep_ref, send_ref, dens_ref):
+    total_k, v, _ = keep_ref.shape
+    core = own_core()
+    total = None
+    for k in range(total_k):
+        for which, ref in ((0, keep_ref), (1, send_ref)):
+            rh, rl = split2(ref[k])
+            dh, dl = split2(dens_ref[(core + which) % 2, k])
+            big = mm(jnp.concatenate([rh, rl], 0), dh, NT)
+            part = big[:v] + big[v:] + mm(rh, dl, NT)
+            total = part if total is None else total + part
+    return total
+
+
+def first_coupled_kernel(keep_ref, send_ref, dens_ref, moments_ref, small_ref, coupled_ref, diag_ref, scratch, *, count):
+    v = moments_ref.shape[0]
+    coupled_ref[...] = pack_moments(scratch, [coupled_part(keep_ref, send_ref, dens_ref)])
+    weighted = unpack_moments(moments_ref[...], 2 * v)[:, v : 2 * v] / count
+    inverse = small_ref[0][:, 0:v]
+    diag_ref[...] = pad_small(scratch, exact(exact(inverse, weighted, NN), inverse, NT))
+
+
+def next_coupled_kernel(keep_ref, send_ref, dens_ref, moments_ref, small_ref, prev_diag_ref, coupled_ref, diag_ref, scratch, *, count):
+    v = moments_ref.shape[0]
+    coupled_ref[...] = pack_moments(scratch, [coupled_part(keep_ref, send_ref, dens_ref)])
     moments = unpack_moments(moments_ref[...], 4 * v) / count
-    pp = moments[:, 0:v]
     mix = moments[:, v : 2 * v]
-    inverse = inverse_cholesky(pp - exact(mix, mix, NT))
-    both = apply_small(inverse, mix)
-    for k in range(mine_ref.shape[0]):
-        for which, ref in ((0, mine_ref), (1, other_ref)):
-            dens = apply_small(inverse, ref[k])
-            dens = dens - apply_small(both, prev_dens_ref[(tasks.core + which) % 2, k])
-            tasks.set_dens(dens_ref, which, k, dens)
-    tasks.run(dens_ref, keep_ref, send_ref, coupled_ref)
     rp = moments[:, 2 * v : 3 * v]
     rv = moments[:, 3 * v : 4 * v]
-    prev_diag = prev_small_ref[1][:, 0:v]
-    weighted = rp - exact(rv, mix, NT) - exact(mix, rv, NT) + exact(exact(mix, prev_diag, NN), mix, NT)
-    diag = exact(exact(inverse, weighted, NN), inverse, NT)
-    small_ref[0] = pad_small(tasks.small, inverse)
-    small_ref[1] = pad_small(tasks.small, diag)
-    small_ref[2] = pad_small(tasks.small, both)
+    mixed = exact(exact(mix, prev_diag_ref[:, 0:v], NN), mix, NT)
+    weighted = rp - exact(rv, mix, NT) - exact(mix, rv, NT) + mixed
+    inverse = small_ref[0][:, 0:v]
+    diag_ref[...] = pad_small(scratch, exact(exact(inverse, weighted, NN), inverse, NT))
 
 
 def rows_kernel(keep_ref, recv_ref, coupled_ref, out_ref):
@@ -270,22 +278,28 @@
 
     rows = []
     for k in range(blocks - 1):
-        rows.append(jnp.concatenate([summed(k, (0,)), summed(k, (1,))], 1).astype(BF))
+        rows.append(jnp.concatenate([summed(k, (0,)), summed(k, (1,))], 1))
     return rows, unpack_moments(summed(blocks - 1, (0, 1)), v)[:, 0:v]
 
 
-def after_first_kernel(recv_ref, x_ref, e_ref, c_ref, small_ref, out_ref, v_ref, p_ref, ray_ref, scratch, *, count):
+def expand(rows, coeff):
+    both = mm(jnp.concatenate(split2(rows), 0), coeff, NN)
+    v = rows.shape[0]
+    return both[:v] + both[v:]
+
+
+def after_first_kernel(recv_ref, x_ref, e_ref, c_ref, small_ref, diag_ref, out_ref, v_ref, p_ref, ray_ref, scratch, *, count):
     local_k, v, _ = x_ref.shape
-    rows, coupled_part = sum_rows(recv_ref)
+    rows, coupled = sum_rows(recv_ref)
     inverse = small_ref[0][:, 0:v]
-    ray = small_ref[1][:, 0:v] + coupled_part / count
+    ray = diag_ref[:, 0:v] + coupled / count
     ray_ref[...] = pad_small(scratch, ray)
     halves = []
     moments = None
     for k in range(local_k):
         basis = apply_small(inverse, x_ref[k])
         energy = e_ref[k : k + 1, :]
-        sigma = energy * basis + mm(rows[k], c_ref[k], NN)
+        sigma = energy * basis + expand(rows[k], c_ref[k])
         residual = sigma - apply_small(ray, basis)
         precond = residual / energy
         v_ref[k] = basis
@@ -301,18 +315,18 @@
     store_for_all(out_ref, halves, pack_moments(scratch, [moments[:v], moments[v:]]))
 
 
-def last_rows_kernel(recv_ref, v_ref, p_ref, e_ref, c_ref, small_ref, out_ref, res_ref, basis_ref, q_ref, ray_ref, scratch, *, count):
+def last_rows_kernel(recv_ref, v_ref, p_ref, e_ref, c_ref, small_ref, diag_ref, out_ref, res_ref, basis_ref, q_ref, ray_ref, scratch, *, count):
     local_k, v, _ = v_ref.shape
-    rows, coupled_part = sum_rows(recv_ref)
+    rows, coupled = sum_rows(recv_ref)
     inverse = small_ref[0][:, 0:v]
-    both = small_ref[2][:, 0:v]
-    ray = small_ref[1][:, 0:v] + coupled_part / count
+    both = small_ref[1][:, 0:v]
+    ray = diag_ref[:, 0:v] + coupled / count
     ray_ref[...] = pad_small(scratch, ray)
     moments = None
     for k in range(local_k):
         basis = apply_small(inverse, p_ref[k]) - apply_small(both, v_ref[k])
         energy = e_ref[k : k + 1, :]
-        sigma = energy * basis + mm(rows[k], c_ref[k], NN)
+        sigma = energy * basis + expand(rows[k], c_ref[k])
         residual = sigma - apply_small(ray, basis)
         precond = residual / energy
         res_ref[k] = residual
@@ -379,6 +393,7 @@
     small_scratch = pltpu.VMEM((v, half), F4)
     dma = pltpu.SemaphoreType.DMA
     half_shape = sds((total_k, v, half), F4)
+    small_shape = sds((v, half), F4)
 
     def exchange(blocks, shape):
         sent = blocks.reshape((devices,) + blocks.shape[-3:])
@@ -386,28 +401,40 @@
 
     def to_all(blocks):
         got = exchange(blocks, (groups, tiles))
-        mine, moments = call(gather_kernel, (half_shape, sds((v, half), F4)), [VM], (got,))
+        mine, moments = call(gather_kernel, (half_shape, small_shape), [VM], (got,))
         return mine, lax.ppermute(mine, "grp", swap), moments
 
-    def to_owner(keep, send, coupled):
-        recv = lax.ppermute(send, "grp", swap)
+    def to_owner(keep, recv, coupled):
         shape = sds((groups, tiles, local_k + 1, v, half), BF)
         out = call(rows_kernel, shape, [VM] * 3, (keep, recv, coupled))
         return exchange(out, (pairs, 2, tiles))
 
+    def factor(body, matrices, moments):
+        shape = sds((matrices, v, half), F4)
+        return call(functools.partial(body, count=count), shape, [VM], (moments,), (small_scratch,))
+
+    def run_tasks(*args):
+        dens_shape = (2, total_k, v, half)
+        return call(
+            tasks_kernel,
+            (half_shape, half_shape, sds(dens_shape, F4)),
+            [ANY, ANY] + [VM] * (len(args) + 1),
+            (assign, ranks, screen) + args,
+            (
+                pltpu.SMEM(assign.shape, jnp.int32),
+                pltpu.SMEM(ranks.shape, jnp.int32),
+                pltpu.VMEM(dens_shape, F4),
+                pltpu.VMEM((2, total_k, 2 * v, half), BF),
+                dma((2,)),
+            ),
+        )
+
+    def couple(body, *args):
+        outs = (sds((v, half), BF), small_shape)
+        return call(functools.partial(body, count=count), outs, [VM] * len(args), args, (small_scratch,))
+
     all_shape = sds((pairs, 2, tiles, local_k + 1, v, half), BF)
-    task_outs = (half_shape, half_shape, sds((v, half), BF))
-    dens_shape = (2, total_k, v, half)
-    task_scratch = (
-        pltpu.SMEM(assign.shape, jnp.int32),
-        pltpu.SMEM(ranks.shape, jnp.int32),
-        pltpu.VMEM((2, total_k, v, half), F4),
-        pltpu.VMEM((2, total_k, v, half), BF),
-        dma((2,)),
-        small_scratch,
-    )
     flat = sds((local_k, v, width), F4)
-    ray_shape = sds((v, half), F4)
 
     inputs = (initial, energy, coeff, screen)
     sent, initial, energy, coeff, screen = call(
@@ -415,42 +442,32 @@
         (all_shape,) + tuple(sds(a.shape, a.dtype) for a in inputs),
         [ANY] * 4,
         inputs,
-        (
-            dma((3,)),
-            dma((local_k,)),
-            small_scratch,
-        ),
+        (dma((3,)), dma((local_k,)), small_scratch),
     )
     mine, other, moments = to_all(sent)
-    keep, send, coupled, dens, small = call(
-        functools.partial(first_tasks_kernel, count=count),
-        task_outs + (sds(dens_shape, F4), sds((2, v, half), F4)),
-        [ANY, ANY] + [VM] * 4,
-        (assign, ranks, screen, mine, other, moments),
-        task_scratch,
-    )
-    got = to_owner(keep, send, coupled)
+    small = factor(first_factor_kernel, 1, moments)
+    keep, send, dens = run_tasks(mine, other, small)
+    recv = lax.ppermute(send, "grp", swap)
+    coupled, diag = couple(first_coupled_kernel, keep, send, dens, moments, small)
+    got = to_owner(keep, recv, coupled)
     sent, basis, precond, ray0 = call(
         functools.partial(after_first_kernel, count=count),
-        (all_shape, flat, flat, ray_shape),
-        [VM] * 5,
-        (got, initial, energy, coeff, small),
+        (all_shape, flat, flat, small_shape),
+        [VM] * 6,
+        (got, initial, energy, coeff, small, diag),
         (small_scratch,),
     )
     mine, other, moments = to_all(sent)
-    keep, send, coupled, small = call(
-        functools.partial(next_tasks_kernel, count=count),
-        task_outs + (sds((3, v, half), F4),),
-        [ANY, ANY] + [VM] * 6,
-        (assign, ranks, screen, mine, other, moments, dens, small),
-        (pltpu.VMEM(dens_shape, F4),) + task_scratch,
-    )
-    got = to_owner(keep, send, coupled)
+    small = factor(next_factor_kernel, 2, moments)
+    keep, send, dens = run_tasks(mine, other, small, dens)
+    recv = lax.ppermute(send, "grp", swap)
+    coupled, diag = couple(next_coupled_kernel, keep, send, dens, moments, small, diag)
+    got = to_owner(keep, recv, coupled)
     sent, residual, basis, precond, ray1 = call(
         functools.partial(last_rows_kernel, count=count),
-        (sds((devices, v, half), BF), flat, flat, flat, ray_shape),
-        [VM] * 6,
-        (got, basis, precond, energy, coeff, small),
+        (sds((devices, v, half), BF), flat, flat, flat, small_shape),
+        [VM] * 7,
+        (got, basis, precond, energy, coeff, small, diag),
         (small_scratch,),
     )
     got = lax.all_to_all(sent, axes, 0, 0, tiled=True)

time: 92.2 us -> 90.2 us (0.978)
  waiting for transfers between devices: 3.95 us -> 0.67 us
  Pallas kernels: 14.7 us -> 16.1 us
    ppermute x2, waiting for transfers between devices: 1.97 us -> 0.24 us  [to_all(): return (mine, lax.ppermute(mine, 'grp', swap), moments)]
    ppermute x2, waiting for transfers between devices: 1.97 us -> 0.44 us  [per_device(): recv = lax.ppermute(send, 'grp', swap)]
    pallas_call x10 -> x14, Pallas kernels: 14.7 us -> 16.1 us  [call(): pl.pallas_call(body, out_shape=outs, in_specs=ins, out_specs=jax.tree.map...]
  transfers between devices with their start and end apart: 4 -> 4, of which waited for: 4 -> 3; matrix products, arithmetic and copies ran while one was open for 0% -> 0% of each run, Pallas kernels for 0% -> 4%
where the time goes in v4:
time: 90.2 us; the launch traced here: 89.8 us
  blocking collectives  69.9 us (77%)
  Pallas kernels  16.1 us (18%)
  starting transfers between devices  2.45 us (3%)
    all_to_all x4, blocking collectives, exchange(): lax.all_to_all(sent, axes, 0, 0, tiled=True).reshape(shape + sent.shape[1:])  59.4 us
    pallas_call x14, Pallas kernels, call(): pl.pallas_call(body, out_shape=outs, in_specs=ins, out_specs=jax.tree.map...  16.1 us
    all_to_all x1, blocking collectives, per_device(): got = lax.all_to_all(sent, axes, 0, 0, tiled=True)  10.5 us
  transfers between devices with their start and end apart: 4, of which 3 were waited for; matrix products, arithmetic and copies ran while one was open for 0% of the time, Pallas kernels for 4%

profile of v4, /device:TPU:0, one launch (start us, length us, event | category | flops | bytes accessed | tf_op | source)
XLA Modules:
  0.0 89.8 jit_solution(8010198123565027876)
XLA Ops:
  0.6 3.0 %shard_map.85 = (bf16[4,2,4,5,8,128]{5,4,3,2,1,0:T(8,128)(2,1)S(1)}, f32[4,8,1024]{2,1,0:T(8,128)S(1)}, f32[4,1024]{1,0:T(4,128)S(1)}, bf16[4,256,1024]{2,1,0:T(8,128)(2,1)S(1)}, bf16[32,256,256]{2,1,0:T(8,128)(2,1)S(1)}) custom-call(f32[4,8,1024]{2,1,0:T(8,128)} %x_hbm.1, f32[4,1024]{1,0:T(4,128)} %e_hbm.1, bf16[4,256,1024]{2,1,0:T(8,128)(2,1)} %c_hbm.1, ...), custom_call_target="tpu_custom_call" | custom-call | tf_op jit(solution)/shard_map/pallas_call | solution.py:369
  3.6 18.2 %all_to_all.25 = bf16[32,5,8,128]{3,2,1,0:T(8,128)(2,1)S(1)} all-to-all(bf16[32,5,8,128]{3,2,1,0:T(8,128)(2,1)S(1)} %bitcast.15), channel_id=1, replica_groups=mesh['grp'=8,'tile'=4] {'grp','tile'}, dimensions={0} | all-to-all | bytes 655360 | tf_op jit(solution)/shard_map/all_to_all | solution.py:400
  21.8 0.1 shard_map.86
  21.9 0.9 collective-permute-start
  22.7 0.8 shard_map.87.small_ref
  23.5 0.2 collective-permute-done.other_ref
  23.7 2.2 %shard_map.88 = (f32[32,8,128]{2,1,0:T(8,128)S(1)}, f32[32,8,128]{2,1,0:T(8,128)S(1)}, f32[2,32,8,128]{3,2,1,0:T(8,128)S(1)}) custom-call(s32[32]{0:T(128)} %assign_hbm.3, s32[32,32]{1,0:T(8,128)} %ranks_hbm.3, bf16[32,256,256]{2,1,0:T(8,128)(2,1)S(1)} %get-tuple-element.33.screen_ref, f32[32,8,128]{2,1,0:T(8,128)S(1)} %get-tuple-element.35.mine_ref, ...), custom_call_target="tpu_custom_call" | custom-call | tf_op jit(solution)/shard_map/pallas_call | solution.py:369
  25.9 0.4 collective-permute-start.1
  26.3 0.6 shard_map.89
  27.0 0.3 collective-permute-done.1.recv_ref
  27.4 13.6 %all_to_all.26 = bf16[32,5,8,128]{3,2,1,0:T(8,128)(2,1)S(1)} all-to-all(bf16[32,5,8,128]{3,2,1,0:T(8,128)(2,1)S(1)} %bitcast.10), channel_id=1, replica_groups=mesh['grp'=8,'tile'=4] {'grp','tile'}, dimensions={0} | all-to-all | bytes 655360 | tf_op jit(solution)/shard_map/all_to_all | solution.py:400
  41.0 1.4 %shard_map.91 = (bf16[4,2,4,5,8,128]{5,4,3,2,1,0:T(8,128)(2,1)S(1)}, f32[4,8,1024]{2,1,0:T(8,128)S(1)}, f32[4,8,1024]{2,1,0:T(8,128)S(1)}, f32[8,128]{1,0:T(8,128)S(1)}) custom-call(bf16[4,2,4,5,8,128]{5,4,3,2,1,0:T(8,128)(2,1)S(1)} %bitcast.8, f32[4,8,1024]{2,1,0:T(8,128)S(1)} %get-tuple-element.41.x_ref, f32[4,1024]{1,0:T(4,128)S(1)} %get-tuple-element.42.e_ref, ...), custom_call_target="tpu_custom_call" | custom-call | tf_op jit(solution)/shard_map/pallas_call | solution.py:369
  42.4 14.1 %all_to_all.27 = bf16[32,5,8,128]{3,2,1,0:T(8,128)(2,1)S(1)} all-to-all(bf16[32,5,8,128]{3,2,1,0:T(8,128)(2,1)S(1)} %bitcast.14), channel_id=1, replica_groups=mesh['grp'=8,'tile'=4] {'grp','tile'}, dimensions={0} | all-to-all | bytes 655360 | tf_op jit(solution)/shard_map/all_to_all | solution.py:400
  56.5 0.1 shard_map.92
  56.6 0.9 collective-permute-start.2
  57.5 1.1 %shard_map.93.small_ref = f32[2,8,128]{2,1,0:T(8,128)S(1)} custom-call(f32[8,128]{1,0:T(8,128)S(1)} %get-tuple-element.47.moments_ref), custom_call_target="tpu_custom_call" | custom-call | tf_op jit(solution)/shard_map/pallas_call | solution.py:369
  58.6 0.0 collective-permute-done.2.other_ref
  58.6 2.3 %shard_map.94 = (f32[32,8,128]{2,1,0:T(8,128)S(1)}, f32[32,8,128]{2,1,0:T(8,128)S(1)}, f32[2,32,8,128]{3,2,1,0:T(8,128)S(1)}) custom-call(s32[32]{0:T(128)} %assign_hbm.3, s32[32,32]{1,0:T(8,128)} %ranks_hbm.3, bf16[32,256,256]{2,1,0:T(8,128)(2,1)S(1)} %get-tuple-element.33.screen_ref, f32[32,8,128]{2,1,0:T(8,128)S(1)} %get-tuple-element.46.mine_ref, ...), custom_call_target="tpu_custom_call" | custom-call | tf_op jit(solution)/shard_map/pallas_call | solution.py:369
  60.9 0.3 collective-permute-start.3
  61.2 1.0 %shard_map.95 = (bf16[8,128]{1,0:T(8,128)(2,1)S(1)}, f32[8,128]{1,0:T(8,128)S(1)}) custom-call(f32[32,8,128]{2,1,0:T(8,128)S(1)} %get-tuple-element.48.keep_ref, f32[32,8,128]{2,1,0:T(8,128)S(1)} %get-tuple-element.49.send_ref, f32[2,32,8,128]{3,2,1,0:T(8,128)S(1)} %get-tuple-element.50.dens_ref, f32[8,128]{1,0:T(8,128)S(1)} %get-tuple-element.47.moments_ref, ...), custom_call_target="tpu_custom_call" | custom-call | tf_op jit(solution)/shard_map/pallas_call | solution.py:369
  62.2 0.1 collective-permute-done.3.recv_ref
  62.4 13.5 %all_to_all.28 = bf16[32,5,8,128]{3,2,1,0:T(8,128)(2,1)S(1)} all-to-all(bf16[32,5,8,128]{3,2,1,0:T(8,128)(2,1)S(1)} %bitcast.12), channel_id=1, replica_groups=mesh['grp'=8,'tile'=4] {'grp','tile'}, dimensions={0} | all-to-all | bytes 655360 | tf_op jit(solution)/shard_map/all_to_all | solution.py:400
  75.9 1.5 %shard_map.97 = (bf16[32,8,128]{2,1,0:T(8,128)(2,1)S(1)}, f32[4,8,1024]{2,1,0:T(8,128)}, f32[4,8,1024]{2,1,0:T(8,128)S(1)}, f32[4,8,1024]{2,1,0:T(8,128)S(1)}, f32[8,128]{1,0:T(8,128)S(1)}) custom-call(bf16[4,2,4,5,8,128]{5,4,3,2,1,0:T(8,128)(2,1)S(1)} %bitcast.13, f32[4,8,1024]{2,1,0:T(8,128)S(1)} %get-tuple-element.52.v_ref, ...), custom_call_target="tpu_custom_call" | custom-call | tf_op jit(solution)/shard_map/pallas_call | solution.py:369
  77.4 10.5 %all_to_all.29.recv_ref = bf16[32,8,128]{2,1,0:T(8,128)(2,1)S(1)} all-to-all(bf16[32,8,128]{2,1,0:T(8,128)(2,1)S(1)} %get-tuple-element.55), channel_id=1, replica_groups=mesh['grp'=8,'tile'=4] {'grp','tile'}, dimensions={0} | all-to-all | bytes 131072 | tf_op jit(solution)/shard_map/all_to_all | solution.py:473
  87.9 1.9 %shard_map.98 = (f32[4,8,1024]{2,1,0:T(8,128)}, f32[2,8,8]{2,1,0:T(8,128)}) custom-call(bf16[32,8,128]{2,1,0:T(8,128)(2,1)S(1)} %all_to_all.29.recv_ref, f32[4,8,1024]{2,1,0:T(8,128)S(1)} %get-tuple-element.56.q_ref, f32[4,8,1024]{2,1,0:T(8,128)S(1)} %get-tuple-element.57.b_ref, f32[8,128]{1,0:T(8,128)S(1)} %get-tuple-element.58.ray0_ref, ...), custom_call_target="tpu_custom_call" | custom-call | tf_op jit(solution)/shard_map/pallas_call | solution.py:369
  (2 shorter events, 0.1 us)
Async XLA Ops:
  21.9 1.9 %collective-permute-start = (f32[32,8,128]{2,1,0:T(8,128)S(1)}, f32[32,8,128]{2,1,0:T(8,128)S(1)}, u32[]{:S(2)}, u32[]{:S(2)}) collective-permute-start(f32[32,8,128]{2,1,0:T(8,128)S(1)} %get-tuple-element.35.mine_ref), channel_id=1, source_target_pairs={{0,4},{4,0},{8,12},{12,8},{16,20},{20,16},{24,28},{28,24},{1,5},{5... | collective-permute-start | bytes 393224 | tf_op jit(solution)/shard_map/ppermute | solution.py:405
  25.9 1.4 %collective-permute-start.1 = (f32[32,8,128]{2,1,0:T(8,128)S(1)}, f32[32,8,128]{2,1,0:T(8,128)S(1)}, u32[]{:S(2)}, u32[]{:S(2)}) collective-permute-start(f32[32,8,128]{2,1,0:T(8,128)S(1)} %get-tuple-element.38.send_ref), channel_id=1, source_target_pairs={{0,4},{4,0},{8,12},{12,8},{16,20},{20,16},{24,28},{28,24},{1,5},{5... | collective-permute-start | bytes 393224 | tf_op jit(solution)/shard_map/ppermute | solution.py:450
  56.6 2.0 %collective-permute-start.2 = (f32[32,8,128]{2,1,0:T(8,128)S(1)}, f32[32,8,128]{2,1,0:T(8,128)S(1)}, u32[]{:S(2)}, u32[]{:S(2)}) collective-permute-start(f32[32,8,128]{2,1,0:T(8,128)S(1)} %get-tuple-element.46.mine_ref), channel_id=1, source_target_pairs={{0,4},{4,0},{8,12},{12,8},{16,20},{20,16},{24,28},{28,24},{1,5},{5... | collective-permute-start | bytes 393224 | tf_op jit(solution)/shard_map/ppermute | solution.py:405
  60.9 1.4 %collective-permute-start.3 = (f32[32,8,128]{2,1,0:T(8,128)S(1)}, f32[32,8,128]{2,1,0:T(8,128)S(1)}, u32[]{:S(2)}, u32[]{:S(2)}) collective-permute-start(f32[32,8,128]{2,1,0:T(8,128)S(1)} %get-tuple-element.49.send_ref), channel_id=1, source_target_pairs={{0,4},{4,0},{8,12},{12,8},{16,20},{20,16},{24,28},{28,24},{1,5},{5... | collective-permute-start | bytes 393224 | tf_op jit(solution)/shard_map/ppermute | solution.py:463

commit v5 on v4

--- a/solution.py
+++ b/solution.py
@@ -43,40 +43,55 @@
     col_id = lax.broadcasted_iota(jnp.int32, (v, v), 1)
     inverse = (row_id == col_id).astype(F4)
     rest = gram
-    for j in range(v):
-        scale = 1.0 / jnp.sqrt(rest[j : j + 1, j : j + 1])
-        col = rest[:, j : j + 1] * scale
-        row = rest[j : j + 1, :] * scale
-        inv_row = inverse[j : j + 1, :] * scale
-        below = jnp.where(row_id[:, 0:1] > j, col, 0.0)
-        inverse = jnp.where(row_id == j, inv_row, inverse - below * inv_row)
-        if j + 1 < v:
-            rest = rest - col * row
-    return inverse
+    for j in range(v - 1):
+        col = jnp.broadcast_to(rest[:, j : j + 1], (v, v))
+        factor = jnp.where(row_id > j, col * (1.0 / col[j : j + 1, :]), 0.0)
+        rest = rest - factor * rest[j : j + 1, :]
+        inverse = inverse - factor * inverse[j : j + 1, :]
+    pivots = jnp.sum(jnp.where(row_id == col_id, rest, 0.0), 1, keepdims=True)
+    return inverse * (1.0 / jnp.sqrt(pivots))
+
+
+def pieces(block):
+    sub = block.shape[0] // 2
+    return [block[:sub].astype(BF), block[sub:].astype(BF)]
+
+
+def terms_of(used, lanes):
+    return min(3, lanes // 2 // used)
 
 
 def pack_moments(scratch, parts):
     total = None
     for i, part in enumerate(parts):
         width = part.shape[1]
-        scratch[...] = jnp.zeros(scratch.shape, F4)
-        scratch[:, 0:width] = part
-        placed = scratch[...]
+        placed = pad_small(scratch, part)
         if i:
             placed = pltpu.roll(placed, i * width, 1)
         total = placed if total is None else total + placed
     used = sum(part.shape[1] for part in parts)
-    first = total.astype(BF).astype(F4)
-    left = total - first
-    second = left.astype(BF).astype(F4)
-    third = (left - second).astype(BF).astype(F4)
-    packed = first + pltpu.roll(second, used, 1) + pltpu.roll(third, 2 * used, 1)
-    return packed.astype(BF)
-
-
-def unpack_moments(total, used):
-    width = total.shape[1]
-    return total + pltpu.roll(total, width - used, 1) + pltpu.roll(total, width - 2 * used, 1)
+    packed = None
+    for i in range(terms_of(used, total.shape[1])):
+        term = total.astype(BF).astype(F4)
+        total = total - term
+        packed = term if packed is None else packed + pltpu.roll(term, i * used, 1)
+    sub = packed.shape[0] // 2
+    return (packed[:sub] + pltpu.roll(packed, packed.shape[1] // 2, 1)[sub:]).astype(BF)
+
+
+def unpack_moments(block, used):
+    width = block.shape[1]
+    total = jnp.concatenate([block, pltpu.roll(block, width // 2, 1)], 0)
+    result = total
+    for i in range(1, terms_of(used, width)):
+        result = result + pltpu.roll(total, width - i * used, 1)
+    return result
+
+
+def pad_small(scratch, small):
+    scratch[...] = jnp.zeros(scratch.shape, F4)
+    scratch[:, 0 : small.shape[1]] = small
+    return scratch[...]
 
 
 def store_for_all(out_ref, dens_halves, moments):
@@ -86,7 +101,7 @@
         for h in range(2):
             for t in range(tiles):
                 for k in range(blocks - 1):
-                    out_ref[g, h, t, k] = dens_halves[k][h]
+                    out_ref[g, h, t, k] = dens_halves[k // 2][h][k % 2]
                 out_ref[g, h, t, blocks - 1] = moments
         return carry
 
@@ -99,7 +114,7 @@
     v = block.shape[0]
     total = both[:v] + both[v:]
     half = total.shape[1] // 2
-    return [total[:, :half].astype(BF), total[:, half:].astype(BF)]
+    return [pieces(total[:, :half]), pieces(total[:, half:])]
 
 
 def start_kernel(x_hbm, e_hbm, c_hbm, s_hbm, out_ref, x_ref, e_ref, c_ref, s_ref, sems, c_sems, scratch):
@@ -131,35 +146,30 @@
 
 
 def gather_kernel(mine_ref, dens_ref, moments_ref):
-    groups, tiles, blocks = mine_ref.shape[:3]
-    local_k = blocks - 1
+    groups, tiles, blocks, sub, _ = mine_ref.shape
+    local_k = blocks // 2
     moments = None
     for g in range(groups):
-        for k in range(local_k):
-            total = mine_ref[g, 0, k].astype(F4)
+        for b in range(blocks - 1):
+            total = mine_ref[g, 0, b].astype(F4)
             for t in range(1, tiles):
-                total = total + mine_ref[g, t, k].astype(F4)
-            dens_ref[g * local_k + k] = total
+                total = total + mine_ref[g, t, b].astype(F4)
+            row = b % 2 * sub
+            dens_ref[g * local_k + b // 2, row : row + sub, :] = total
         for t in range(tiles):
-            block = mine_ref[g, t, local_k].astype(F4)
+            block = mine_ref[g, t, blocks - 1].astype(F4)
             moments = block if moments is None else moments + block
     moments_ref[...] = moments
 
 
-def pad_small(scratch, small):
-    scratch[...] = jnp.zeros(scratch.shape, F4)
-    scratch[:, 0 : small.shape[1]] = small
-    return scratch[...]
-
-
 def first_factor_kernel(moments_ref, small_ref, scratch, *, count):
-    v = moments_ref.shape[0]
+    v = 2 * moments_ref.shape[0]
     moments = unpack_moments(moments_ref[...], 2 * v)
     small_ref[0] = pad_small(scratch, inverse_cholesky(moments[:, 0:v] / count))
 
 
 def next_factor_kernel(moments_ref, small_ref, scratch, *, count):
-    v = moments_ref.shape[0]
+    v = 2 * moments_ref.shape[0]
     moments = unpack_moments(moments_ref[...], 4 * v) / count
     mix = moments[:, v : 2 * v]
     inverse = inverse_cholesky(moments[:, 0:v] - exact(mix, mix, NT))
@@ -232,7 +242,7 @@
 
 
 def first_coupled_kernel(keep_ref, send_ref, dens_ref, moments_ref, small_ref, coupled_ref, diag_ref, scratch, *, count):
-    v = moments_ref.shape[0]
+    v = 2 * moments_ref.shape[0]
     coupled_ref[...] = pack_moments(scratch, [coupled_part(keep_ref, send_ref, dens_ref)])
     weighted = unpack_moments(moments_ref[...], 2 * v)[:, v : 2 * v] / count
     inverse = small_ref[0][:, 0:v]
@@ -240,7 +250,7 @@
 
 
 def next_coupled_kernel(keep_ref, send_ref, dens_ref, moments_ref, small_ref, prev_diag_ref, coupled_ref, diag_ref, scratch, *, count):
-    v = moments_ref.shape[0]
+    v = 2 * moments_ref.shape[0]
     coupled_ref[...] = pack_moments(scratch, [coupled_part(keep_ref, send_ref, dens_ref)])
     moments = unpack_moments(moments_ref[...], 4 * v) / count
     mix = moments[:, v : 2 * v]
@@ -254,18 +264,19 @@
 
 def rows_kernel(keep_ref, recv_ref, coupled_ref, out_ref):
     groups, tiles, blocks = out_ref.shape[:3]
-    local_k = blocks - 1
+    local_k = blocks // 2
     for g in range(groups):
         for k in range(local_k):
-            rows = (keep_ref[g * local_k + k] + recv_ref[g * local_k + k]).astype(BF)
+            rows = pieces(keep_ref[g * local_k + k] + recv_ref[g * local_k + k])
             for t in range(tiles):
-                out_ref[g, t, k] = rows
+                out_ref[g, t, 2 * k] = rows[0]
+                out_ref[g, t, 2 * k + 1] = rows[1]
         for t in range(tiles):
-            out_ref[g, t, local_k] = coupled_ref[...]
+            out_ref[g, t, blocks - 1] = coupled_ref[...]
 
 
 def sum_rows(recv_ref):
-    pairs, _, tiles, blocks, v, _ = recv_ref.shape
+    pairs, _, tiles, blocks, sub, _ = recv_ref.shape
 
     def summed(block, halves):
         total = None
@@ -276,10 +287,11 @@
                     total = part if total is None else total + part
         return total
 
-    rows = []
-    for k in range(blocks - 1):
-        rows.append(jnp.concatenate([summed(k, (0,)), summed(k, (1,))], 1))
-    return rows, unpack_moments(summed(blocks - 1, (0, 1)), v)[:, 0:v]
+    def both(k, half):
+        return jnp.concatenate([summed(2 * k, (half,)), summed(2 * k + 1, (half,))], 0)
+
+    rows = [jnp.concatenate([both(k, 0), both(k, 1)], 1) for k in range(blocks // 2)]
+    return rows, unpack_moments(summed(blocks - 1, (0, 1)), 2 * sub)[:, 0 : 2 * sub]
 
 
 def expand(rows, coeff):
@@ -315,13 +327,14 @@
     store_for_all(out_ref, halves, pack_moments(scratch, [moments[:v], moments[v:]]))
 
 
-def last_rows_kernel(recv_ref, v_ref, p_ref, e_ref, c_ref, small_ref, diag_ref, out_ref, res_ref, basis_ref, q_ref, ray_ref, scratch, *, count):
+def last_rows_kernel(recv_ref, v_ref, p_ref, e_ref, c_ref, small_ref, diag_ref, out_ref, res_hbm, basis_ref, q_ref, ray_ref, res_ref, sems, scratch, *, count):
     local_k, v, _ = v_ref.shape
     rows, coupled = sum_rows(recv_ref)
     inverse = small_ref[0][:, 0:v]
     both = small_ref[1][:, 0:v]
     ray = diag_ref[:, 0:v] + coupled / count
     ray_ref[...] = pad_small(scratch, ray)
+    copies = []
     moments = None
     for k in range(local_k):
         basis = apply_small(inverse, p_ref[k]) - apply_small(both, v_ref[k])
@@ -330,6 +343,8 @@
         residual = sigma - apply_small(ray, basis)
         precond = residual / energy
         res_ref[k] = residual
+        copies.append(pltpu.make_async_copy(res_ref.at[k], res_hbm.at[k], sems.at[k]))
+        copies[-1].start()
         basis_ref[k] = basis
         q_ref[k] = precond
         bh, bl = split2(basis)
@@ -337,31 +352,63 @@
         big = mm(jnp.concatenate([ph, pw], 0), jnp.concatenate([ph, bh], 0), NT)
         part = big[:v] + big[v:] + mm(ph, jnp.concatenate([pw, bl], 0), NT)
         moments = part if moments is None else moments + part
-    packed = pack_moments(scratch, [moments])
+    packed = to_row(pad_small(scratch, moments), 2 * v)
     for d in range(out_ref.shape[0]):
         out_ref[d] = packed
-
-
-def finish_kernel(recv_ref, q_ref, b_ref, ray0_ref, ray1_ref, out_ref, ray_ref, *, count):
+    for copy in copies:
+        copy.wait()
+
+
+def diagonal_lanes(shape, width):
+    row_id = lax.broadcasted_iota(jnp.int32, shape, 0)
+    return lax.broadcasted_iota(jnp.int32, shape, 1) // width == row_id
+
+
+def fold_lanes(block, width):
+    shift = width
+    while shift < block.shape[1]:
+        block = block + pltpu.roll(block, shift, 1)
+        shift *= 2
+    return block
+
+
+def to_row(block, width):
+    spread = fold_lanes(block, width)
+    return jnp.sum(jnp.where(diagonal_lanes(block.shape, width), spread, 0.0), 0, keepdims=True)
+
+
+def from_row(row, rows, width):
+    block = jnp.broadcast_to(row, (rows, row.shape[1]))
+    return fold_lanes(jnp.where(diagonal_lanes(block.shape, width), block, 0.0), width)
+
+
+def finish_kernel(recv_ref, q_ref, b_ref, ray0_ref, ray1_ref, out_hbm, ray_hbm, out_ref, ray_ref, sems, *, count):
     local_k, v, _ = q_ref.shape
-    total = recv_ref[0].astype(F4)
-    for d in range(1, recv_ref.shape[0]):
-        total = total + recv_ref[d].astype(F4)
-    moments = unpack_moments(total, 2 * v) / count
+    ray_ref[0] = ray0_ref[:, 0:v].T
+    ray_ref[1] = ray1_ref[:, 0:v].T
+    copies = [pltpu.make_async_copy(ray_ref, ray_hbm, sems.at[local_k])]
+    copies[0].start()
+    row = jnp.sum(recv_ref[:, 0, :], 0, keepdims=True)
+    moments = from_row(row, v, 2 * v) / count
     mix = moments[:, v : 2 * v]
     inverse = inverse_cholesky(moments[:, 0:v] - exact(mix, mix, NT))
-    both = exact(inverse, mix, NN)
+    both = apply_small(inverse, mix)
     for k in range(local_k):
         out_ref[k] = apply_small(inverse, q_ref[k]) - apply_small(both, b_ref[k])
-    ray_ref[0] = ray0_ref[:, 0:v].T
-    ray_ref[1] = ray1_ref[:, 0:v].T
+        copies.append(pltpu.make_async_copy(out_ref.at[k], out_hbm.at[k], sems.at[k]))
+        copies[-1].start()
+    for copy in copies:
+        copy.wait()
 
 
 VM = pl.BlockSpec(memory_space=pltpu.VMEM)
 ANY = pl.BlockSpec(memory_space=pltpu.HBM)
 
 
-def call(body, outs, ins, args, scratch=(), cost=None):
+def call(body, outs, ins, args, scratch=(), to_hbm=()):
+    specs = VM
+    if isinstance(outs, tuple):
+        specs = tuple(ANY if i in to_hbm else VM for i in range(len(outs)))
     args = [
         pltpu.with_memory_space_constraint(arg, pltpu.HBM) if spec is ANY else arg
         for arg, spec in zip(args, ins)
@@ -370,10 +417,9 @@
         body,
         out_shape=outs,
         in_specs=ins,
-        out_specs=jax.tree.map(lambda _: VM, outs),
+        out_specs=specs,
         scratch_shapes=scratch,
         compiler_params=pltpu.CompilerParams(vmem_limit_bytes=16 << 20),
-        cost_estimate=cost,
     )(*args)
 
 
@@ -401,11 +447,11 @@
 
     def to_all(blocks):
         got = exchange(blocks, (groups, tiles))
-        mine, moments = call(gather_kernel, (half_shape, small_shape), [VM], (got,))
+        mine, moments = call(gather_kernel, (half_shape, sds((v // 2, half), F4)), [VM], (got,))
         return mine, lax.ppermute(mine, "grp", swap), moments
 
     def to_owner(keep, recv, coupled):
-        shape = sds((groups, tiles, local_k + 1, v, half), BF)
+        shape = sds((groups, tiles, 2 * local_k + 1, v // 2, half), BF)
         out = call(rows_kernel, shape, [VM] * 3, (keep, recv, coupled))
         return exchange(out, (pairs, 2, tiles))
 
@@ -430,10 +476,10 @@
         )
 
     def couple(body, *args):
-        outs = (sds((v, half), BF), small_shape)
+        outs = (sds((v // 2, half), BF), small_shape)
         return call(functools.partial(body, count=count), outs, [VM] * len(args), args, (small_scratch,))
 
-    all_shape = sds((pairs, 2, tiles, local_k + 1, v, half), BF)
+    all_shape = sds((pairs, 2, tiles, 2 * local_k + 1, v // 2, half), BF)
     flat = sds((local_k, v, width), F4)
 
     inputs = (initial, energy, coeff, screen)
@@ -465,10 +511,11 @@
     got = to_owner(keep, recv, coupled)
     sent, residual, basis, precond, ray1 = call(
         functools.partial(last_rows_kernel, count=count),
-        (sds((devices, v, half), BF), flat, flat, flat, small_shape),
+        (sds((devices, 1, half), F4), flat, flat, flat, small_shape),
         [VM] * 7,
         (got, basis, precond, energy, coeff, small, diag),
-        (small_scratch,),
+        (pltpu.VMEM(flat.shape, F4), dma((local_k,)), small_scratch),
+        (1,),
     )
     got = lax.all_to_all(sent, axes, 0, 0, tiled=True)
     basis, rayleigh = call(
@@ -476,6 +523,8 @@
         (flat, sds((2, v, v), F4)),
         [VM] * 5,
         (got, precond, basis, ray0, ray1),
+        (pltpu.VMEM(flat.shape, F4), pltpu.VMEM((2, v, v), F4), dma((local_k + 1,))),
+        (0, 1),
     )
     return (rayleigh, basis, residual)
 

time: 90.2 us -> 87.5 us (0.970)
  blocking collectives: 69.9 us -> 67.4 us
    all_to_all x4, blocking collectives: 59.4 us -> 57.6 us  [exchange(): lax.all_to_all(sent, axes, 0, 0, tiled=True).reshape(shape + sent.shape[1:])]
where the time goes in v5:
time: 87.5 us; the launch traced here: 87.2 us
  blocking collectives  67.4 us (77%)
  Pallas kernels  16.5 us (19%)
  starting transfers between devices  1.85 us (2%)
    all_to_all x4, blocking collectives, exchange(): lax.all_to_all(sent, axes, 0, 0, tiled=True).reshape(shape + sent.shape[1:])  57.6 us
    pallas_call x14, Pallas kernels, call(): pl.pallas_call(body, out_shape=outs, in_specs=ins, out_specs=specs, scrat...  16.5 us
    all_to_all x1, blocking collectives, per_device(): got = lax.all_to_all(sent, axes, 0, 0, tiled=True)  9.89 us
  transfers between devices with their start and end apart: 4, of which 3 were waited for; matrix products, arithmetic and copies ran while one was open for 0% of the time, Pallas kernels for 4%

profile of v5, /device:TPU:0, one launch (start us, length us, event | category | flops | bytes accessed | tf_op | source)
XLA Modules:
  0.0 87.2 jit_solution(10576701901898248502)
XLA Ops:
  0.6 3.0 %shard_map.85 = (bf16[4,2,4,9,4,128]{5,4,3,2,1,0:T(4,128)(2,1)S(1)}, f32[4,8,1024]{2,1,0:T(8,128)S(1)}, f32[4,1024]{1,0:T(4,128)S(1)}, bf16[4,256,1024]{2,1,0:T(8,128)(2,1)S(1)}, bf16[32,256,256]{2,1,0:T(8,128)(2,1)S(1)}) custom-call(f32[4,8,1024]{2,1,0:T(8,128)} %x_hbm.1, f32[4,1024]{1,0:T(4,128)} %e_hbm.1, bf16[4,256,1024]{2,1,0:T(8,128)(2,1)} %c_hbm.1, ...), custom_call_target="tpu_custom_call" | custom-call | tf_op jit(solution)/shard_map/pallas_call | solution.py:416
  3.6 17.8 %all_to_all.25 = bf16[32,9,4,128]{3,2,1,0:T(4,128)(2,1)S(1)} all-to-all(bf16[32,9,4,128]{3,2,1,0:T(4,128)(2,1)S(1)} %bitcast.15), channel_id=1, replica_groups=mesh['grp'=8,'tile'=4] {'grp','tile'}, dimensions={0} | all-to-all | bytes 589824 | tf_op jit(solution)/shard_map/all_to_all | solution.py:446
  21.4 0.1 shard_map.86
  21.5 0.6 collective-permute-start
  22.1 0.7 shard_map.87.small_ref
  22.8 0.3 collective-permute-done.other_ref
  23.1 2.2 %shard_map.88 = (f32[32,8,128]{2,1,0:T(8,128)S(1)}, f32[32,8,128]{2,1,0:T(8,128)S(1)}, f32[2,32,8,128]{3,2,1,0:T(8,128)S(1)}) custom-call(s32[32]{0:T(128)} %assign_hbm.3, s32[32,32]{1,0:T(8,128)} %ranks_hbm.3, bf16[32,256,256]{2,1,0:T(8,128)(2,1)S(1)} %get-tuple-element.33.screen_ref, f32[32,8,128]{2,1,0:T(8,128)S(1)} %get-tuple-element.35.mine_ref, ...), custom_call_target="tpu_custom_call" | custom-call | tf_op jit(solution)/shard_map/pallas_call | solution.py:416
  25.3 0.4 collective-permute-start.1
  25.7 0.7 shard_map.89
  26.4 0.3 collective-permute-done.1.recv_ref
  26.7 0.1 shard_map.90
  26.8 13.2 %all_to_all.26 = bf16[32,9,4,128]{3,2,1,0:T(4,128)(2,1)S(1)} all-to-all(bf16[32,9,4,128]{3,2,1,0:T(4,128)(2,1)S(1)} %bitcast.10), channel_id=1, replica_groups=mesh['grp'=8,'tile'=4] {'grp','tile'}, dimensions={0} | all-to-all | bytes 589824 | tf_op jit(solution)/shard_map/all_to_all | solution.py:446
  40.0 1.6 %shard_map.91 = (bf16[4,2,4,9,4,128]{5,4,3,2,1,0:T(4,128)(2,1)S(1)}, f32[4,8,1024]{2,1,0:T(8,128)S(1)}, f32[4,8,1024]{2,1,0:T(8,128)S(1)}, f32[8,128]{1,0:T(8,128)S(1)}) custom-call(bf16[4,2,4,9,4,128]{5,4,3,2,1,0:T(4,128)(2,1)S(1)} %bitcast.8, f32[4,8,1024]{2,1,0:T(8,128)S(1)} %get-tuple-element.41.x_ref, f32[4,1024]{1,0:T(4,128)S(1)} %get-tuple-element.42.e_ref, ...), custom_call_target="tpu_custom_call" | custom-call | tf_op jit(solution)/shard_map/pallas_call | solution.py:416
  41.6 13.4 %all_to_all.27 = bf16[32,9,4,128]{3,2,1,0:T(4,128)(2,1)S(1)} all-to-all(bf16[32,9,4,128]{3,2,1,0:T(4,128)(2,1)S(1)} %bitcast.14), channel_id=1, replica_groups=mesh['grp'=8,'tile'=4] {'grp','tile'}, dimensions={0} | all-to-all | bytes 589824 | tf_op jit(solution)/shard_map/all_to_all | solution.py:446
  55.0 0.1 shard_map.92
  55.1 0.6 collective-permute-start.2
  55.7 1.1 %shard_map.93.small_ref = f32[2,8,128]{2,1,0:T(8,128)S(1)} custom-call(f32[4,128]{1,0:T(4,128)S(1)} %get-tuple-element.47.moments_ref), custom_call_target="tpu_custom_call" | custom-call | tf_op jit(solution)/shard_map/pallas_call | solution.py:416
  56.8 0.0 collective-permute-done.2.other_ref
  56.8 2.3 %shard_map.94 = (f32[32,8,128]{2,1,0:T(8,128)S(1)}, f32[32,8,128]{2,1,0:T(8,128)S(1)}, f32[2,32,8,128]{3,2,1,0:T(8,128)S(1)}) custom-call(s32[32]{0:T(128)} %assign_hbm.3, s32[32,32]{1,0:T(8,128)} %ranks_hbm.3, bf16[32,256,256]{2,1,0:T(8,128)(2,1)S(1)} %get-tuple-element.33.screen_ref, f32[32,8,128]{2,1,0:T(8,128)S(1)} %get-tuple-element.46.mine_ref, ...), custom_call_target="tpu_custom_call" | custom-call | tf_op jit(solution)/shard_map/pallas_call | solution.py:416
  59.1 0.3 collective-permute-start.3
  59.4 1.0 %shard_map.95 = (bf16[4,128]{1,0:T(4,128)(2,1)S(1)}, f32[8,128]{1,0:T(8,128)S(1)}) custom-call(f32[32,8,128]{2,1,0:T(8,128)S(1)} %get-tuple-element.48.keep_ref, f32[32,8,128]{2,1,0:T(8,128)S(1)} %get-tuple-element.49.send_ref, f32[2,32,8,128]{3,2,1,0:T(8,128)S(1)} %get-tuple-element.50.dens_ref, f32[4,128]{1,0:T(4,128)S(1)} %get-tuple-element.47.moments_ref, ...), custom_call_target="tpu_custom_call" | custom-call | tf_op jit(solution)/shard_map/pallas_call | solution.py:416
  60.4 0.1 collective-permute-done.3.recv_ref
  60.5 0.1 shard_map.96
  60.6 13.1 %all_to_all.28 = bf16[32,9,4,128]{3,2,1,0:T(4,128)(2,1)S(1)} all-to-all(bf16[32,9,4,128]{3,2,1,0:T(4,128)(2,1)S(1)} %bitcast.12), channel_id=1, replica_groups=mesh['grp'=8,'tile'=4] {'grp','tile'}, dimensions={0} | all-to-all | bytes 589824 | tf_op jit(solution)/shard_map/all_to_all | solution.py:446
  73.7 1.6 %shard_map.97 = (f32[32,1,128]{2,1,0:T(1,128)S(1)}, f32[4,8,1024]{2,1,0:T(8,128)}, f32[4,8,1024]{2,1,0:T(8,128)S(1)}, f32[4,8,1024]{2,1,0:T(8,128)S(1)}, f32[8,128]{1,0:T(8,128)S(1)}) custom-call(bf16[4,2,4,9,4,128]{5,4,3,2,1,0:T(4,128)(2,1)S(1)} %bitcast.13, f32[4,8,1024]{2,1,0:T(8,128)S(1)} %get-tuple-element.52.v_ref, ...), custom_call_target="tpu_custom_call" | custom-call | tf_op jit(solution)/shard_map/pallas_call | solution.py:416
  75.3 9.9 %all_to_all.29.recv_ref = f32[32,1,128]{2,1,0:T(1,128)S(1)} all-to-all(f32[32,1,128]{2,1,0:T(1,128)S(1)} %get-tuple-element.55), channel_id=1, replica_groups=mesh['grp'=8,'tile'=4] {'grp','tile'}, dimensions={0} | all-to-all | bytes 32768 | tf_op jit(solution)/shard_map/all_to_all | solution.py:520
  85.2 1.9 %shard_map.98 = (f32[4,8,1024]{2,1,0:T(8,128)}, f32[2,8,8]{2,1,0:T(8,128)}) custom-call(f32[32,1,128]{2,1,0:T(1,128)S(1)} %all_to_all.29.recv_ref, f32[4,8,1024]{2,1,0:T(8,128)S(1)} %get-tuple-element.56.q_ref, f32[4,8,1024]{2,1,0:T(8,128)S(1)} %get-tuple-element.57.b_ref, f32[8,128]{1,0:T(8,128)S(1)} %get-tuple-element.58.ray0_ref, ...), custom_call_target="tpu_custom_call" | custom-call | tf_op jit(solution)/shard_map/pallas_call | solution.py:416
Async XLA Ops:
  21.5 1.6 %collective-permute-start = (f32[32,8,128]{2,1,0:T(8,128)S(1)}, f32[32,8,128]{2,1,0:T(8,128)S(1)}, u32[]{:S(2)}, u32[]{:S(2)}) collective-permute-start(f32[32,8,128]{2,1,0:T(8,128)S(1)} %get-tuple-element.35.mine_ref), channel_id=1, source_target_pairs={{0,4},{4,0},{8,12},{12,8},{16,20},{20,16},{24,28},{28,24},{1,5},{5... | collective-permute-start | bytes 393224 | tf_op jit(solution)/shard_map/ppermute | solution.py:451
  25.3 1.4 %collective-permute-start.1 = (f32[32,8,128]{2,1,0:T(8,128)S(1)}, f32[32,8,128]{2,1,0:T(8,128)S(1)}, u32[]{:S(2)}, u32[]{:S(2)}) collective-permute-start(f32[32,8,128]{2,1,0:T(8,128)S(1)} %get-tuple-element.38.send_ref), channel_id=1, source_target_pairs={{0,4},{4,0},{8,12},{12,8},{16,20},{20,16},{24,28},{28,24},{1,5},{5... | collective-permute-start | bytes 393224 | tf_op jit(solution)/shard_map/ppermute | solution.py:496
  55.1 1.7 %collective-permute-start.2 = (f32[32,8,128]{2,1,0:T(8,128)S(1)}, f32[32,8,128]{2,1,0:T(8,128)S(1)}, u32[]{:S(2)}, u32[]{:S(2)}) collective-permute-start(f32[32,8,128]{2,1,0:T(8,128)S(1)} %get-tuple-element.46.mine_ref), channel_id=1, source_target_pairs={{0,4},{4,0},{8,12},{12,8},{16,20},{20,16},{24,28},{28,24},{1,5},{5... | collective-permute-start | bytes 393224 | tf_op jit(solution)/shard_map/ppermute | solution.py:451
  59.1 1.4 %collective-permute-start.3 = (f32[32,8,128]{2,1,0:T(8,128)S(1)}, f32[32,8,128]{2,1,0:T(8,128)S(1)}, u32[]{:S(2)}, u32[]{:S(2)}) collective-permute-start(f32[32,8,128]{2,1,0:T(8,128)S(1)} %get-tuple-element.49.send_ref), channel_id=1, source_target_pairs={{0,4},{4,0},{8,12},{12,8},{16,20},{20,16},{24,28},{28,24},{1,5},{5... | collective-permute-start | bytes 393224 | tf_op jit(solution)/shard_map/ppermute | solution.py:509

commit v6 on v5

--- a/solution.py
+++ b/solution.py
@@ -124,12 +124,11 @@
         pltpu.make_async_copy(e_hbm, e_ref, sems.at[1]),
     ]
     c_copies = [pltpu.make_async_copy(c_hbm.at[k], c_ref.at[k], c_sems.at[k]) for k in range(local_k)]
-    screen_copy = pltpu.make_async_copy(s_hbm, s_ref, sems.at[2])
+    screen_copy = pltpu.make_async_copy(s_hbm.at[pl.ds(0, s_ref.shape[0])], s_ref, sems.at[2])
     for copy in copies + c_copies + [screen_copy]:
         copy.start()
     for copy in copies:
         copy.wait()
-    halves = []
     moments = None
     for k in range(local_k):
         x = x_ref[k]
@@ -139,9 +138,11 @@
         small = mm(xh, jnp.concatenate([xl, el], 0), NT)
         part = big[:v] + big[v:] + small
         moments = part if moments is None else moments + part
-        c_copies[k].wait()
-        halves.append(project(x, c_ref[k]))
-    store_for_all(out_ref, halves, pack_moments(scratch, [moments]))
+    packed = pack_moments(scratch, [moments])
+    for copy in c_copies:
+        copy.wait()
+    halves = [project(x_ref[k], c_ref[k]) for k in range(local_k)]
+    store_for_all(out_ref, halves, packed)
     screen_copy.wait()
 
 
@@ -181,17 +182,25 @@
     return lax.axis_index("grp") % 2
 
 
-def tasks_kernel(assign_hbm, ranks_hbm, screen_ref, mine_ref, other_ref, small_ref, *refs):
+def tasks_kernel(assign_hbm, ranks_hbm, head_ref, tail_ref, mine_ref, other_ref, small_ref, *refs, first):
     prev_dens_ref = None
-    if len(refs) > 8:
+    if first:
+        tail_hbm, tail_ref = tail_ref, refs[3]
+        refs = refs[:3] + refs[4:]
+    else:
         prev_dens_ref, refs = refs[0], refs[1:]
     keep_ref, send_ref, dens_ref, assign_ref, ranks_ref, acc_ref, terms_ref, sems = refs
-    heads = [
+    heads = head_ref.shape[0]
+    tails = tail_ref.shape[0]
+    tables = [
         pltpu.make_async_copy(assign_hbm, assign_ref, sems.at[0]),
         pltpu.make_async_copy(ranks_hbm, ranks_ref, sems.at[1]),
     ]
-    for copy in heads:
+    for copy in tables:
         copy.start()
+    if first:
+        tail_copy = pltpu.make_async_copy(tail_hbm.at[pl.ds(heads, tails)], tail_ref, sems.at[2])
+        tail_copy.start()
     acc_ref[...] = jnp.zeros(acc_ref.shape, F4)
     core = own_core()
     total_k, v, half = mine_ref.shape
@@ -205,11 +214,11 @@
             dens_ref[slot, k] = dens
             terms_ref[slot, k] = jnp.concatenate(split2(dens), 0)
     lane = lax.broadcasted_iota(jnp.int32, (2 * v, 2 * half), 1)
-    for copy in heads:
+    for copy in tables:
         copy.wait()
 
-    def one(t, carry):
-        pair = assign_ref[t]
+    def one(screen_ref, offset, t, carry):
+        pair = assign_ref[offset + t]
         row = pair // total_k
         col = pair - row * total_k
         keep = lane < ranks_ref[row, col]
@@ -221,7 +230,10 @@
         acc_ref[1, row] = acc_ref[1, row] + term[:, half:]
         return carry
 
-    lax.fori_loop(0, screen_ref.shape[0], one, 0, unroll=True)
+    lax.fori_loop(0, heads, functools.partial(one, head_ref, 0), 0, unroll=True)
+    if first:
+        tail_copy.wait()
+    lax.fori_loop(0, tails, functools.partial(one, tail_ref, heads), 0, unroll=True)
     for k in range(total_k):
         keep_ref[k] = acc_ref[core, k]
         send_ref[k] = acc_ref[1 - core, k]
@@ -303,23 +315,24 @@
 def after_first_kernel(recv_ref, x_ref, e_ref, c_ref, small_ref, diag_ref, out_ref, v_ref, p_ref, ray_ref, scratch, *, count):
     local_k, v, _ = x_ref.shape
     rows, coupled = sum_rows(recv_ref)
+    expanded = [expand(rows[k], c_ref[k]) for k in range(local_k)]
     inverse = small_ref[0][:, 0:v]
     ray = diag_ref[:, 0:v] + coupled / count
     ray_ref[...] = pad_small(scratch, ray)
-    halves = []
+    inverse_energy = 1.0 / e_ref[...]
+    residuals = []
+    for k in range(local_k):
+        basis = apply_small(inverse, x_ref[k])
+        residual = e_ref[k : k + 1, :] * basis + expanded[k] - apply_small(ray, basis)
+        residuals.append(residual)
+        v_ref[k] = basis
+        p_ref[k] = residual * inverse_energy[k : k + 1, :]
+    halves = [project(p_ref[k], c_ref[k]) for k in range(local_k)]
     moments = None
     for k in range(local_k):
-        basis = apply_small(inverse, x_ref[k])
-        energy = e_ref[k : k + 1, :]
-        sigma = energy * basis + expand(rows[k], c_ref[k])
-        residual = sigma - apply_small(ray, basis)
-        precond = residual / energy
-        v_ref[k] = basis
-        p_ref[k] = precond
-        halves.append(project(precond, c_ref[k]))
-        bh, bl = split2(basis)
-        rh, rl = split2(residual)
-        ph, pw = split2(precond)
+        bh, bl = split2(v_ref[k])
+        rh, rl = split2(residuals[k])
+        ph, pw = split2(p_ref[k])
         big = mm(jnp.concatenate([ph, rh, pw, rl], 0), jnp.concatenate([ph, bh], 0), NT)
         small = mm(jnp.concatenate([ph, rh], 0), jnp.concatenate([pw, bl], 0), NT)
         part = big[: 2 * v] + big[2 * v :] + small
@@ -330,25 +343,25 @@
 def last_rows_kernel(recv_ref, v_ref, p_ref, e_ref, c_ref, small_ref, diag_ref, out_ref, res_hbm, basis_ref, q_ref, ray_ref, res_ref, sems, scratch, *, count):
     local_k, v, _ = v_ref.shape
     rows, coupled = sum_rows(recv_ref)
+    expanded = [expand(rows[k], c_ref[k]) for k in range(local_k)]
     inverse = small_ref[0][:, 0:v]
     both = small_ref[1][:, 0:v]
     ray = diag_ref[:, 0:v] + coupled / count
     ray_ref[...] = pad_small(scratch, ray)
+    inverse_energy = 1.0 / e_ref[...]
     copies = []
-    moments = None
     for k in range(local_k):
         basis = apply_small(inverse, p_ref[k]) - apply_small(both, v_ref[k])
-        energy = e_ref[k : k + 1, :]
-        sigma = energy * basis + expand(rows[k], c_ref[k])
-        residual = sigma - apply_small(ray, basis)
-        precond = residual / energy
+        residual = e_ref[k : k + 1, :] * basis + expanded[k] - apply_small(ray, basis)
         res_ref[k] = residual
         copies.append(pltpu.make_async_copy(res_ref.at[k], res_hbm.at[k], sems.at[k]))
         copies[-1].start()
         basis_ref[k] = basis
-        q_ref[k] = precond
-        bh, bl = split2(basis)
-        ph, pw = split2(precond)
+        q_ref[k] = residual * inverse_energy[k : k + 1, :]
+    moments = None
+    for k in range(local_k):
+        bh, bl = split2(basis_ref[k])
+        ph, pw = split2(q_ref[k])
         big = mm(jnp.concatenate([ph, pw], 0), jnp.concatenate([ph, bh], 0), NT)
         part = big[:v] + big[v:] + mm(ph, jnp.concatenate([pw, bl], 0), NT)
         moments = part if moments is None else moments + part
@@ -459,19 +472,23 @@
         shape = sds((matrices, v, half), F4)
         return call(functools.partial(body, count=count), shape, [VM], (moments,), (small_scratch,))
 
-    def run_tasks(*args):
+    def run_tasks(tail, *args):
         dens_shape = (2, total_k, v, half)
+        outs = (half_shape, half_shape, sds(dens_shape, F4))
+        first = tail is screen
+        if first:
+            outs = outs + (sds((tails,) + screen.shape[1:], BF),)
         return call(
-            tasks_kernel,
-            (half_shape, half_shape, sds(dens_shape, F4)),
-            [ANY, ANY] + [VM] * (len(args) + 1),
-            (assign, ranks, screen) + args,
+            functools.partial(tasks_kernel, first=first),
+            outs,
+            [ANY, ANY, VM, ANY if first else VM] + [VM] * len(args),
+            (assign, ranks, head, tail) + args,
             (
                 pltpu.SMEM(assign.shape, jnp.int32),
                 pltpu.SMEM(ranks.shape, jnp.int32),
                 pltpu.VMEM(dens_shape, F4),
                 pltpu.VMEM((2, total_k, 2 * v, half), BF),
-                dma((2,)),
+                dma((3,)),
             ),
         )
 
@@ -482,17 +499,19 @@
     all_shape = sds((pairs, 2, tiles, 2 * local_k + 1, v // 2, half), BF)
     flat = sds((local_k, v, width), F4)
 
-    inputs = (initial, energy, coeff, screen)
-    sent, initial, energy, coeff, screen = call(
+    tails = screen.shape[0] // 4
+    inputs = (initial, energy, coeff)
+    head_shape = sds((screen.shape[0] - tails,) + screen.shape[1:], BF)
+    sent, initial, energy, coeff, head = call(
         start_kernel,
-        (all_shape,) + tuple(sds(a.shape, a.dtype) for a in inputs),
+        (all_shape,) + tuple(sds(a.shape, a.dtype) for a in inputs) + (head_shape,),
         [ANY] * 4,
-        inputs,
+        inputs + (screen,),
         (dma((3,)), dma((local_k,)), small_scratch),
     )
     mine, other, moments = to_all(sent)
     small = factor(first_factor_kernel, 1, moments)
-    keep, send, dens = run_tasks(mine, other, small)
+    keep, send, dens, tail = run_tasks(screen, mine, other, small)
     recv = lax.ppermute(send, "grp", swap)
     coupled, diag = couple(first_coupled_kernel, keep, send, dens, moments, small)
     got = to_owner(keep, recv, coupled)
@@ -505,7 +524,7 @@
     )
     mine, other, moments = to_all(sent)
     small = factor(next_factor_kernel, 2, moments)
-    keep, send, dens = run_tasks(mine, other, small, dens)
+    keep, send, dens = run_tasks(tail, mine, other, small, dens)
     recv = lax.ppermute(send, "grp", swap)
     coupled, diag = couple(next_coupled_kernel, keep, send, dens, moments, small, diag)
     got = to_owner(keep, recv, coupled)

time: 87.5 us -> 86.8 us (level)
  no operation moved by 1% of the time
where the time goes in v6:
time: 86.8 us; the launch traced here: 86.6 us
  blocking collectives  67.4 us (78%)
  Pallas kernels  16 us (18%)
  starting transfers between devices  1.85 us (2%)
    all_to_all x4, blocking collectives, exchange(): lax.all_to_all(sent, axes, 0, 0, tiled=True).reshape(shape + sent.shape[1:])  57.6 us
    pallas_call x14, Pallas kernels, call(): pl.pallas_call(body, out_shape=outs, in_specs=ins, out_specs=specs, scrat...  16 us
    all_to_all x1, blocking collectives, per_device(): got = lax.all_to_all(sent, axes, 0, 0, tiled=True)  9.89 us
  transfers between devices with their start and end apart: 4, of which 3 were waited for; matrix products, arithmetic and copies ran while one was open for 0% of the time, Pallas kernels for 4%

profile of v6, /device:TPU:0, one launch (start us, length us, event | category | flops | bytes accessed | tf_op | source)
XLA Modules:
  0.0 86.6 jit_solution(6879304022904582270)
XLA Ops:
  0.6 2.7 %shard_map.85 = (bf16[4,2,4,9,4,128]{5,4,3,2,1,0:T(4,128)(2,1)S(1)}, f32[4,8,1024]{2,1,0:T(8,128)S(1)}, f32[4,1024]{1,0:T(4,128)S(1)}, bf16[4,256,1024]{2,1,0:T(8,128)(2,1)S(1)}, bf16[24,256,256]{2,1,0:T(8,128)(2,1)S(1)}) custom-call(f32[4,8,1024]{2,1,0:T(8,128)} %x_hbm.1, f32[4,1024]{1,0:T(4,128)} %e_hbm.1, bf16[4,256,1024]{2,1,0:T(8,128)(2,1)} %c_hbm.1, ...), custom_call_target="tpu_custom_call" | custom-call | tf_op jit(solution)/shard_map/pallas_call | solution.py:429
  3.3 17.8 %all_to_all.25 = bf16[32,9,4,128]{3,2,1,0:T(4,128)(2,1)S(1)} all-to-all(bf16[32,9,4,128]{3,2,1,0:T(4,128)(2,1)S(1)} %bitcast.15), channel_id=1, replica_groups=mesh['grp'=8,'tile'=4] {'grp','tile'}, dimensions={0} | all-to-all | bytes 589824 | tf_op jit(solution)/shard_map/all_to_all | solution.py:459
  21.1 0.1 shard_map.86
  21.2 0.6 collective-permute-start
  21.8 0.7 shard_map.87.small_ref
  22.5 0.3 collective-permute-done.other_ref
  22.8 2.3 %shard_map.88 = (f32[32,8,128]{2,1,0:T(8,128)S(1)}, f32[32,8,128]{2,1,0:T(8,128)S(1)}, f32[2,32,8,128]{3,2,1,0:T(8,128)S(1)}, bf16[8,256,256]{2,1,0:T(8,128)(2,1)S(1)}) custom-call(s32[32]{0:T(128)} %assign_hbm.3, s32[32,32]{1,0:T(8,128)} %ranks_hbm.3, bf16[24,256,256]{2,1,0:T(8,128)(2,1)S(1)} %get-tuple-element.34.head_ref, bf16[32,256,256]{2,1,0:T(8,128)(2,1)} %tail_ref.1, ...), custom_call_target="tpu_custom_call" | custom-call | tf_op jit(solution)/shard_map/pallas_call | solution.py:429
  25.1 0.4 collective-permute-start.1
  25.5 0.7 shard_map.89
  26.2 0.3 collective-permute-done.1.recv_ref
  26.5 0.1 shard_map.90
  26.6 13.2 %all_to_all.26 = bf16[32,9,4,128]{3,2,1,0:T(4,128)(2,1)S(1)} all-to-all(bf16[32,9,4,128]{3,2,1,0:T(4,128)(2,1)S(1)} %bitcast.10), channel_id=1, replica_groups=mesh['grp'=8,'tile'=4] {'grp','tile'}, dimensions={0} | all-to-all | bytes 589824 | tf_op jit(solution)/shard_map/all_to_all | solution.py:459
  39.8 1.5 %shard_map.91 = (bf16[4,2,4,9,4,128]{5,4,3,2,1,0:T(4,128)(2,1)S(1)}, f32[4,8,1024]{2,1,0:T(8,128)S(1)}, f32[4,8,1024]{2,1,0:T(8,128)S(1)}, f32[8,128]{1,0:T(8,128)S(1)}) custom-call(bf16[4,2,4,9,4,128]{5,4,3,2,1,0:T(4,128)(2,1)S(1)} %bitcast.8, f32[4,8,1024]{2,1,0:T(8,128)S(1)} %get-tuple-element.43.x_ref, f32[4,1024]{1,0:T(4,128)S(1)} %get-tuple-element.44.e_ref, ...), custom_call_target="tpu_custom_call" | custom-call | tf_op jit(solution)/shard_map/pallas_call | solution.py:429
  41.3 13.4 %all_to_all.27 = bf16[32,9,4,128]{3,2,1,0:T(4,128)(2,1)S(1)} all-to-all(bf16[32,9,4,128]{3,2,1,0:T(4,128)(2,1)S(1)} %bitcast.14), channel_id=1, replica_groups=mesh['grp'=8,'tile'=4] {'grp','tile'}, dimensions={0} | all-to-all | bytes 589824 | tf_op jit(solution)/shard_map/all_to_all | solution.py:459
  54.7 0.1 shard_map.92
  54.8 0.6 collective-permute-start.2
  55.4 1.1 %shard_map.93.small_ref = f32[2,8,128]{2,1,0:T(8,128)S(1)} custom-call(f32[4,128]{1,0:T(4,128)S(1)} %get-tuple-element.49.moments_ref), custom_call_target="tpu_custom_call" | custom-call | tf_op jit(solution)/shard_map/pallas_call | solution.py:429
  56.5 0.0 collective-permute-done.2.other_ref
  56.5 2.3 %shard_map.94 = (f32[32,8,128]{2,1,0:T(8,128)S(1)}, f32[32,8,128]{2,1,0:T(8,128)S(1)}, f32[2,32,8,128]{3,2,1,0:T(8,128)S(1)}) custom-call(s32[32]{0:T(128)} %assign_hbm.3, s32[32,32]{1,0:T(8,128)} %ranks_hbm.3, bf16[24,256,256]{2,1,0:T(8,128)(2,1)S(1)} %get-tuple-element.34.head_ref, bf16[8,256,256]{2,1,0:T(8,128)(2,1)S(1)} %get-tuple-element.38.tail_ref, ...), custom_call_target="tpu_custom_call" | custom-call | tf_op jit(solution)/shard_map/pallas_call | solution.py:429
  58.9 0.3 collective-permute-start.3
  59.1 1.0 %shard_map.95 = (bf16[4,128]{1,0:T(4,128)(2,1)S(1)}, f32[8,128]{1,0:T(8,128)S(1)}) custom-call(f32[32,8,128]{2,1,0:T(8,128)S(1)} %get-tuple-element.50.keep_ref, f32[32,8,128]{2,1,0:T(8,128)S(1)} %get-tuple-element.51.send_ref, f32[2,32,8,128]{3,2,1,0:T(8,128)S(1)} %get-tuple-element.52.dens_ref, f32[4,128]{1,0:T(4,128)S(1)} %get-tuple-element.49.moments_ref, ...), custom_call_target="tpu_custom_call" | custom-call | tf_op jit(solution)/shard_map/pallas_call | solution.py:429
  60.2 0.1 collective-permute-done.3.recv_ref
  60.3 0.1 shard_map.96
  60.4 13.1 %all_to_all.28 = bf16[32,9,4,128]{3,2,1,0:T(4,128)(2,1)S(1)} all-to-all(bf16[32,9,4,128]{3,2,1,0:T(4,128)(2,1)S(1)} %bitcast.12), channel_id=1, replica_groups=mesh['grp'=8,'tile'=4] {'grp','tile'}, dimensions={0} | all-to-all | bytes 589824 | tf_op jit(solution)/shard_map/all_to_all | solution.py:459
  73.5 1.3 %shard_map.97 = (f32[32,1,128]{2,1,0:T(1,128)S(1)}, f32[4,8,1024]{2,1,0:T(8,128)}, f32[4,8,1024]{2,1,0:T(8,128)S(1)}, f32[4,8,1024]{2,1,0:T(8,128)S(1)}, f32[8,128]{1,0:T(8,128)S(1)}) custom-call(bf16[4,2,4,9,4,128]{5,4,3,2,1,0:T(4,128)(2,1)S(1)} %bitcast.13, f32[4,8,1024]{2,1,0:T(8,128)S(1)} %get-tuple-element.54.v_ref, ...), custom_call_target="tpu_custom_call" | custom-call | tf_op jit(solution)/shard_map/pallas_call | solution.py:429
  74.8 9.9 %all_to_all.29.recv_ref = f32[32,1,128]{2,1,0:T(1,128)S(1)} all-to-all(f32[32,1,128]{2,1,0:T(1,128)S(1)} %get-tuple-element.57), channel_id=1, replica_groups=mesh['grp'=8,'tile'=4] {'grp','tile'}, dimensions={0} | all-to-all | bytes 32768 | tf_op jit(solution)/shard_map/all_to_all | solution.py:539
  84.7 1.9 %shard_map.98 = (f32[4,8,1024]{2,1,0:T(8,128)}, f32[2,8,8]{2,1,0:T(8,128)}) custom-call(f32[32,1,128]{2,1,0:T(1,128)S(1)} %all_to_all.29.recv_ref, f32[4,8,1024]{2,1,0:T(8,128)S(1)} %get-tuple-element.58.q_ref, f32[4,8,1024]{2,1,0:T(8,128)S(1)} %get-tuple-element.59.b_ref, f32[8,128]{1,0:T(8,128)S(1)} %get-tuple-element.60.ray0_ref, ...), custom_call_target="tpu_custom_call" | custom-call | tf_op jit(solution)/shard_map/pallas_call | solution.py:429
Async XLA Ops:
  21.2 1.6 %collective-permute-start = (f32[32,8,128]{2,1,0:T(8,128)S(1)}, f32[32,8,128]{2,1,0:T(8,128)S(1)}, u32[]{:S(2)}, u32[]{:S(2)}) collective-permute-start(f32[32,8,128]{2,1,0:T(8,128)S(1)} %get-tuple-element.36.mine_ref), channel_id=1, source_target_pairs={{0,4},{4,0},{8,12},{12,8},{16,20},{20,16},{24,28},{28,24},{1,5},{5... | collective-permute-start | bytes 393224 | tf_op jit(solution)/shard_map/ppermute | solution.py:464
  25.1 1.4 %collective-permute-start.1 = (f32[32,8,128]{2,1,0:T(8,128)S(1)}, f32[32,8,128]{2,1,0:T(8,128)S(1)}, u32[]{:S(2)}, u32[]{:S(2)}) collective-permute-start(f32[32,8,128]{2,1,0:T(8,128)S(1)} %get-tuple-element.40.send_ref), channel_id=1, source_target_pairs={{0,4},{4,0},{8,12},{12,8},{16,20},{20,16},{24,28},{28,24},{1,5},{5... | collective-permute-start | bytes 393224 | tf_op jit(solution)/shard_map/ppermute | solution.py:515
  54.8 1.7 %collective-permute-start.2 = (f32[32,8,128]{2,1,0:T(8,128)S(1)}, f32[32,8,128]{2,1,0:T(8,128)S(1)}, u32[]{:S(2)}, u32[]{:S(2)}) collective-permute-start(f32[32,8,128]{2,1,0:T(8,128)S(1)} %get-tuple-element.48.mine_ref), channel_id=1, source_target_pairs={{0,4},{4,0},{8,12},{12,8},{16,20},{20,16},{24,28},{28,24},{1,5},{5... | collective-permute-start | bytes 393224 | tf_op jit(solution)/shard_map/ppermute | solution.py:464
  58.9 1.4 %collective-permute-start.3 = (f32[32,8,128]{2,1,0:T(8,128)S(1)}, f32[32,8,128]{2,1,0:T(8,128)S(1)}, u32[]{:S(2)}, u32[]{:S(2)}) collective-permute-start(f32[32,8,128]{2,1,0:T(8,128)S(1)} %get-tuple-element.51.send_ref), channel_id=1, source_target_pairs={{0,4},{4,0},{8,12},{12,8},{16,20},{20,16},{24,28},{28,24},{1,5},{5... | collective-permute-start | bytes 393224 | tf_op jit(solution)/shard_map/ppermute | solution.py:528

commit v7 on v6

--- a/solution.py
+++ b/solution.py
@@ -52,6 +52,23 @@
     return inverse * (1.0 / jnp.sqrt(pivots))
 
 
+def unit_factors(gram):
+    v = gram.shape[0]
+    row_id = lax.broadcasted_iota(jnp.int32, (v, v), 0)
+    col_id = lax.broadcasted_iota(jnp.int32, (v, v), 1)
+    lower = (row_id == col_id).astype(F4)
+    inverse = lower
+    rest = gram + 1e-4 * lower * gram
+    for j in range(v - 1):
+        col = jnp.broadcast_to(rest[:, j : j + 1], (v, v))
+        pivot = jnp.maximum(col[j : j + 1, :], 1e-30)
+        factor = jnp.where(row_id > j, col * (1.0 / pivot), 0.0)
+        rest = rest - factor * rest[j : j + 1, :]
+        inverse = inverse - factor * inverse[j : j + 1, :]
+        lower = lower + jnp.where(col_id == j, factor, 0.0)
+    return lower, inverse
+
+
 def pieces(block):
     sub = block.shape[0] // 2
     return [block[:sub].astype(BF), block[sub:].astype(BF)]
@@ -63,13 +80,13 @@
 
 def pack_moments(scratch, parts):
     total = None
-    for i, part in enumerate(parts):
-        width = part.shape[1]
+    used = 0
+    for part in parts:
         placed = pad_small(scratch, part)
-        if i:
-            placed = pltpu.roll(placed, i * width, 1)
+        if used:
+            placed = pltpu.roll(placed, used, 1)
         total = placed if total is None else total + placed
-    used = sum(part.shape[1] for part in parts)
+        used += part.shape[1]
     packed = None
     for i in range(terms_of(used, total.shape[1])):
         term = total.astype(BF).astype(F4)
@@ -112,7 +129,10 @@
     high, low = split2(block)
     both = mm(jnp.concatenate([high, low], 0), coeff, NT)
     v = block.shape[0]
-    total = both[:v] + both[v:]
+    return both[:v] + both[v:]
+
+
+def halves_of(total):
     half = total.shape[1] // 2
     return [pieces(total[:, :half]), pieces(total[:, half:])]
 
@@ -138,11 +158,12 @@
         small = mm(xh, jnp.concatenate([xl, el], 0), NT)
         part = big[:v] + big[v:] + small
         moments = part if moments is None else moments + part
-    packed = pack_moments(scratch, [moments])
     for copy in c_copies:
         copy.wait()
-    halves = [project(x_ref[k], c_ref[k]) for k in range(local_k)]
-    store_for_all(out_ref, halves, packed)
+    projected = [project(x_ref[k], c_ref[k]) for k in range(local_k)]
+    lower, inverse = unit_factors(moments[:, 0:v])
+    halves = [halves_of(apply_small(inverse, block)) for block in projected]
+    store_for_all(out_ref, halves, pack_moments(scratch, [moments, lower]))
     screen_copy.wait()
 
 
@@ -163,9 +184,32 @@
     moments_ref[...] = moments
 
 
+def first_gather_kernel(mine_ref, dens_ref, moments_ref):
+    groups, tiles, blocks, sub, lanes = mine_ref.shape
+    local_k = blocks // 2
+    v = 2 * sub
+    lane = lax.broadcasted_iota(jnp.int32, (v, lanes), 1)
+    own = (lane >= 2 * v) & (lane < 3 * v)
+    moments = None
+    for g in range(groups):
+        factors = None
+        for t in range(tiles):
+            block = mine_ref[g, t, blocks - 1].astype(F4)
+            moments = block if moments is None else moments + block
+            lower = jnp.where(own, unpack_moments(block, 3 * v), 0.0)
+            lower = pltpu.roll(lower, (lanes + (t - 2) * v) % lanes, 1)
+            factors = lower if factors is None else factors + lower
+        left = jnp.concatenate(split2(factors[:, : tiles * v]), 0)
+        for k in range(local_k):
+            sent = [mine_ref[g, t, 2 * k + i].astype(F4) for t in range(tiles) for i in range(2)]
+            both = mm(left, jnp.concatenate(sent, 0).astype(BF), NN)
+            dens_ref[g * local_k + k] = both[:v] + both[v:]
+    moments_ref[...] = moments
+
+
 def first_factor_kernel(moments_ref, small_ref, scratch, *, count):
     v = 2 * moments_ref.shape[0]
-    moments = unpack_moments(moments_ref[...], 2 * v)
+    moments = unpack_moments(moments_ref[...], 3 * v)
     small_ref[0] = pad_small(scratch, inverse_cholesky(moments[:, 0:v] / count))
 
 
@@ -256,7 +300,7 @@
 def first_coupled_kernel(keep_ref, send_ref, dens_ref, moments_ref, small_ref, coupled_ref, diag_ref, scratch, *, count):
     v = 2 * moments_ref.shape[0]
     coupled_ref[...] = pack_moments(scratch, [coupled_part(keep_ref, send_ref, dens_ref)])
-    weighted = unpack_moments(moments_ref[...], 2 * v)[:, v : 2 * v] / count
+    weighted = unpack_moments(moments_ref[...], 3 * v)[:, v : 2 * v] / count
     inverse = small_ref[0][:, 0:v]
     diag_ref[...] = pad_small(scratch, exact(exact(inverse, weighted, NN), inverse, NT))
 
@@ -327,7 +371,7 @@
         residuals.append(residual)
         v_ref[k] = basis
         p_ref[k] = residual * inverse_energy[k : k + 1, :]
-    halves = [project(p_ref[k], c_ref[k]) for k in range(local_k)]
+    halves = [halves_of(project(p_ref[k], c_ref[k])) for k in range(local_k)]
     moments = None
     for k in range(local_k):
         bh, bl = split2(v_ref[k])
@@ -458,9 +502,9 @@
         sent = blocks.reshape((devices,) + blocks.shape[-3:])
         return lax.all_to_all(sent, axes, 0, 0, tiled=True).reshape(shape + sent.shape[1:])
 
-    def to_all(blocks):
+    def to_all(blocks, body):
         got = exchange(blocks, (groups, tiles))
-        mine, moments = call(gather_kernel, (half_shape, sds((v // 2, half), F4)), [VM], (got,))
+        mine, moments = call(body, (half_shape, sds((v // 2, half), F4)), [VM], (got,))
         return mine, lax.ppermute(mine, "grp", swap), moments
 
     def to_owner(keep, recv, coupled):
@@ -509,7 +553,7 @@
         inputs + (screen,),
         (dma((3,)), dma((local_k,)), small_scratch),
     )
-    mine, other, moments = to_all(sent)
+    mine, other, moments = to_all(sent, first_gather_kernel)
     small = factor(first_factor_kernel, 1, moments)
     keep, send, dens, tail = run_tasks(screen, mine, other, small)
     recv = lax.ppermute(send, "grp", swap)
@@ -522,7 +566,7 @@
         (got, initial, energy, coeff, small, diag),
         (small_scratch,),
     )
-    mine, other, moments = to_all(sent)
+    mine, other, moments = to_all(sent, gather_kernel)
     small = factor(next_factor_kernel, 2, moments)
     keep, send, dens = run_tasks(tail, mine, other, small, dens)
     recv = lax.ppermute(send, "grp", swap)

time: 86.8 us -> 87.2 us (level)
  no operation moved by 1% of the time
where the time goes in v7:
time: 87.2 us; the launch traced here: 86.9 us
  blocking collectives  67.4 us (77%)
  Pallas kernels  16.3 us (19%)
  starting transfers between devices  1.86 us (2%)
    all_to_all x4, blocking collectives, exchange(): lax.all_to_all(sent, axes, 0, 0, tiled=True).reshape(shape + sent.shape[1:])  57.5 us
    pallas_call x14, Pallas kernels, call(): pl.pallas_call(body, out_shape=outs, in_specs=ins, out_specs=specs, scrat...  16.3 us
    all_to_all x1, blocking collectives, per_device(): got = lax.all_to_all(sent, axes, 0, 0, tiled=True)  9.89 us
  transfers between devices with their start and end apart: 4, of which 3 were waited for; matrix products, arithmetic and copies ran while one was open for 0% of the time, Pallas kernels for 4%

profile of v7, /device:TPU:0, one launch (start us, length us, event | category | flops | bytes accessed | tf_op | source)
XLA Modules:
  0.0 86.9 jit_solution(18390446806722593355)
XLA Ops:
  0.6 2.7 %shard_map.85 = (bf16[4,2,4,9,4,128]{5,4,3,2,1,0:T(4,128)(2,1)S(1)}, f32[4,8,1024]{2,1,0:T(8,128)S(1)}, f32[4,1024]{1,0:T(4,128)S(1)}, bf16[4,256,1024]{2,1,0:T(8,128)(2,1)S(1)}, bf16[24,256,256]{2,1,0:T(8,128)(2,1)S(1)}) custom-call(f32[4,8,1024]{2,1,0:T(8,128)} %x_hbm.1, f32[4,1024]{1,0:T(4,128)} %e_hbm.1, bf16[4,256,1024]{2,1,0:T(8,128)(2,1)} %c_hbm.1, ...), custom_call_target="tpu_custom_call" | custom-call | tf_op jit(solution)/shard_map/pallas_call | solution.py:473
  3.3 17.8 %all_to_all.25 = bf16[32,9,4,128]{3,2,1,0:T(4,128)(2,1)S(1)} all-to-all(bf16[32,9,4,128]{3,2,1,0:T(4,128)(2,1)S(1)} %bitcast.15), channel_id=1, replica_groups=mesh['grp'=8,'tile'=4] {'grp','tile'}, dimensions={0} | all-to-all | bytes 589824 | tf_op jit(solution)/shard_map/all_to_all | solution.py:503
  21.1 0.4 shard_map.86
  21.6 0.6 collective-permute-start
  22.2 0.7 shard_map.87.small_ref
  22.9 0.3 collective-permute-done.other_ref
  23.1 2.3 %shard_map.88 = (f32[32,8,128]{2,1,0:T(8,128)S(1)}, f32[32,8,128]{2,1,0:T(8,128)S(1)}, f32[2,32,8,128]{3,2,1,0:T(8,128)S(1)}, bf16[8,256,256]{2,1,0:T(8,128)(2,1)S(1)}) custom-call(s32[32]{0:T(128)} %assign_hbm.3, s32[32,32]{1,0:T(8,128)} %ranks_hbm.3, bf16[24,256,256]{2,1,0:T(8,128)(2,1)S(1)} %get-tuple-element.34.head_ref, bf16[32,256,256]{2,1,0:T(8,128)(2,1)} %tail_ref.1, ...), custom_call_target="tpu_custom_call" | custom-call | tf_op jit(solution)/shard_map/pallas_call | solution.py:473
  25.5 0.4 collective-permute-start.1
  25.9 0.7 shard_map.89
  26.6 0.3 collective-permute-done.1.recv_ref
  26.9 0.1 shard_map.90
  27.0 13.2 %all_to_all.26 = bf16[32,9,4,128]{3,2,1,0:T(4,128)(2,1)S(1)} all-to-all(bf16[32,9,4,128]{3,2,1,0:T(4,128)(2,1)S(1)} %bitcast.10), channel_id=1, replica_groups=mesh['grp'=8,'tile'=4] {'grp','tile'}, dimensions={0} | all-to-all | bytes 589824 | tf_op jit(solution)/shard_map/all_to_all | solution.py:503
  40.2 1.5 %shard_map.91 = (bf16[4,2,4,9,4,128]{5,4,3,2,1,0:T(4,128)(2,1)S(1)}, f32[4,8,1024]{2,1,0:T(8,128)S(1)}, f32[4,8,1024]{2,1,0:T(8,128)S(1)}, f32[8,128]{1,0:T(8,128)S(1)}) custom-call(bf16[4,2,4,9,4,128]{5,4,3,2,1,0:T(4,128)(2,1)S(1)} %bitcast.8, f32[4,8,1024]{2,1,0:T(8,128)S(1)} %get-tuple-element.43.x_ref, f32[4,1024]{1,0:T(4,128)S(1)} %get-tuple-element.44.e_ref, ...), custom_call_target="tpu_custom_call" | custom-call | tf_op jit(solution)/shard_map/pallas_call | solution.py:473
  41.7 13.4 %all_to_all.27 = bf16[32,9,4,128]{3,2,1,0:T(4,128)(2,1)S(1)} all-to-all(bf16[32,9,4,128]{3,2,1,0:T(4,128)(2,1)S(1)} %bitcast.14), channel_id=1, replica_groups=mesh['grp'=8,'tile'=4] {'grp','tile'}, dimensions={0} | all-to-all | bytes 589824 | tf_op jit(solution)/shard_map/all_to_all | solution.py:503
  55.1 0.1 shard_map.92
  55.2 0.6 collective-permute-start.2
  55.7 1.1 %shard_map.93.small_ref = f32[2,8,128]{2,1,0:T(8,128)S(1)} custom-call(f32[4,128]{1,0:T(4,128)S(1)} %get-tuple-element.49.moments_ref), custom_call_target="tpu_custom_call" | custom-call | tf_op jit(solution)/shard_map/pallas_call | solution.py:473
  56.9 0.0 collective-permute-done.2.other_ref
  56.9 2.3 %shard_map.94 = (f32[32,8,128]{2,1,0:T(8,128)S(1)}, f32[32,8,128]{2,1,0:T(8,128)S(1)}, f32[2,32,8,128]{3,2,1,0:T(8,128)S(1)}) custom-call(s32[32]{0:T(128)} %assign_hbm.3, s32[32,32]{1,0:T(8,128)} %ranks_hbm.3, bf16[24,256,256]{2,1,0:T(8,128)(2,1)S(1)} %get-tuple-element.34.head_ref, bf16[8,256,256]{2,1,0:T(8,128)(2,1)S(1)} %get-tuple-element.38.tail_ref, ...), custom_call_target="tpu_custom_call" | custom-call | tf_op jit(solution)/shard_map/pallas_call | solution.py:473
  59.2 0.3 collective-permute-start.3
  59.5 1.0 %shard_map.95 = (bf16[4,128]{1,0:T(4,128)(2,1)S(1)}, f32[8,128]{1,0:T(8,128)S(1)}) custom-call(f32[32,8,128]{2,1,0:T(8,128)S(1)} %get-tuple-element.50.keep_ref, f32[32,8,128]{2,1,0:T(8,128)S(1)} %get-tuple-element.51.send_ref, f32[2,32,8,128]{3,2,1,0:T(8,128)S(1)} %get-tuple-element.52.dens_ref, f32[4,128]{1,0:T(4,128)S(1)} %get-tuple-element.49.moments_ref, ...), custom_call_target="tpu_custom_call" | custom-call | tf_op jit(solution)/shard_map/pallas_call | solution.py:473
  60.5 0.1 collective-permute-done.3.recv_ref
  60.6 0.1 shard_map.96
  60.7 13.1 %all_to_all.28 = bf16[32,9,4,128]{3,2,1,0:T(4,128)(2,1)S(1)} all-to-all(bf16[32,9,4,128]{3,2,1,0:T(4,128)(2,1)S(1)} %bitcast.12), channel_id=1, replica_groups=mesh['grp'=8,'tile'=4] {'grp','tile'}, dimensions={0} | all-to-all | bytes 589824 | tf_op jit(solution)/shard_map/all_to_all | solution.py:503
  73.8 1.3 %shard_map.97 = (f32[32,1,128]{2,1,0:T(1,128)S(1)}, f32[4,8,1024]{2,1,0:T(8,128)}, f32[4,8,1024]{2,1,0:T(8,128)S(1)}, f32[4,8,1024]{2,1,0:T(8,128)S(1)}, f32[8,128]{1,0:T(8,128)S(1)}) custom-call(bf16[4,2,4,9,4,128]{5,4,3,2,1,0:T(4,128)(2,1)S(1)} %bitcast.13, f32[4,8,1024]{2,1,0:T(8,128)S(1)} %get-tuple-element.54.v_ref, ...), custom_call_target="tpu_custom_call" | custom-call | tf_op jit(solution)/shard_map/pallas_call | solution.py:473
  75.1 9.9 %all_to_all.29.recv_ref = f32[32,1,128]{2,1,0:T(1,128)S(1)} all-to-all(f32[32,1,128]{2,1,0:T(1,128)S(1)} %get-tuple-element.57), channel_id=1, replica_groups=mesh['grp'=8,'tile'=4] {'grp','tile'}, dimensions={0} | all-to-all | bytes 32768 | tf_op jit(solution)/shard_map/all_to_all | solution.py:583
  85.0 1.9 %shard_map.98 = (f32[4,8,1024]{2,1,0:T(8,128)}, f32[2,8,8]{2,1,0:T(8,128)}) custom-call(f32[32,1,128]{2,1,0:T(1,128)S(1)} %all_to_all.29.recv_ref, f32[4,8,1024]{2,1,0:T(8,128)S(1)} %get-tuple-element.58.q_ref, f32[4,8,1024]{2,1,0:T(8,128)S(1)} %get-tuple-element.59.b_ref, f32[8,128]{1,0:T(8,128)S(1)} %get-tuple-element.60.ray0_ref, ...), custom_call_target="tpu_custom_call" | custom-call | tf_op jit(solution)/shard_map/pallas_call | solution.py:473
Async XLA Ops:
  21.6 1.6 %collective-permute-start = (f32[32,8,128]{2,1,0:T(8,128)S(1)}, f32[32,8,128]{2,1,0:T(8,128)S(1)}, u32[]{:S(2)}, u32[]{:S(2)}) collective-permute-start(f32[32,8,128]{2,1,0:T(8,128)S(1)} %get-tuple-element.36.mine_ref), channel_id=1, source_target_pairs={{0,4},{4,0},{8,12},{12,8},{16,20},{20,16},{24,28},{28,24},{1,5},{5... | collective-permute-start | bytes 393224 | tf_op jit(solution)/shard_map/ppermute | solution.py:508
  25.5 1.4 %collective-permute-start.1 = (f32[32,8,128]{2,1,0:T(8,128)S(1)}, f32[32,8,128]{2,1,0:T(8,128)S(1)}, u32[]{:S(2)}, u32[]{:S(2)}) collective-permute-start(f32[32,8,128]{2,1,0:T(8,128)S(1)} %get-tuple-element.40.send_ref), channel_id=1, source_target_pairs={{0,4},{4,0},{8,12},{12,8},{16,20},{20,16},{24,28},{28,24},{1,5},{5... | collective-permute-start | bytes 393224 | tf_op jit(solution)/shard_map/ppermute | solution.py:559
  55.2 1.7 %collective-permute-start.2 = (f32[32,8,128]{2,1,0:T(8,128)S(1)}, f32[32,8,128]{2,1,0:T(8,128)S(1)}, u32[]{:S(2)}, u32[]{:S(2)}) collective-permute-start(f32[32,8,128]{2,1,0:T(8,128)S(1)} %get-tuple-element.48.mine_ref), channel_id=1, source_target_pairs={{0,4},{4,0},{8,12},{12,8},{16,20},{20,16},{24,28},{28,24},{1,5},{5... | collective-permute-start | bytes 393224 | tf_op jit(solution)/shard_map/ppermute | solution.py:508
  59.2 1.4 %collective-permute-start.3 = (f32[32,8,128]{2,1,0:T(8,128)S(1)}, f32[32,8,128]{2,1,0:T(8,128)S(1)}, u32[]{:S(2)}, u32[]{:S(2)}) collective-permute-start(f32[32,8,128]{2,1,0:T(8,128)S(1)} %get-tuple-element.51.send_ref), channel_id=1, source_target_pairs={{0,4},{4,0},{8,12},{12,8},{16,20},{20,16},{24,28},{28,24},{1,5},{5... | collective-permute-start | bytes 393224 | tf_op jit(solution)/shard_map/ppermute | solution.py:572

commit v8 on v7

--- a/solution.py
+++ b/solution.py
@@ -543,7 +543,7 @@
     all_shape = sds((pairs, 2, tiles, 2 * local_k + 1, v // 2, half), BF)
     flat = sds((local_k, v, width), F4)
 
-    tails = screen.shape[0] // 4
+    tails = screen.shape[0] // 2
     inputs = (initial, energy, coeff)
     head_shape = sds((screen.shape[0] - tails,) + screen.shape[1:], BF)
     sent, initial, energy, coeff, head = call(

time: 87.2 us -> 87 us (level)
  no operation moved by 1% of the time
where the time goes in v8:
time: 87 us; the launch traced here: 86.7 us
  blocking collectives  67.4 us (77%)
  Pallas kernels  16.1 us (19%)
  starting transfers between devices  1.86 us (2%)
    all_to_all x4, blocking collectives, exchange(): lax.all_to_all(sent, axes, 0, 0, tiled=True).reshape(shape + sent.shape[1:])  57.6 us
    pallas_call x14, Pallas kernels, call(): pl.pallas_call(body, out_shape=outs, in_specs=ins, out_specs=specs, scrat...  16.1 us
    all_to_all x1, blocking collectives, per_device(): got = lax.all_to_all(sent, axes, 0, 0, tiled=True)  9.89 us
  transfers between devices with their start and end apart: 4, of which 3 were waited for; matrix products, arithmetic and copies ran while one was open for 0% of the time, Pallas kernels for 4%

profile of v8, /device:TPU:0, one launch (start us, length us, event | category | flops | bytes accessed | tf_op | source)
XLA Modules:
  0.0 86.7 jit_solution(10533238864506336084)
XLA Ops:
  0.6 2.4 %shard_map.85 = (bf16[4,2,4,9,4,128]{5,4,3,2,1,0:T(4,128)(2,1)S(1)}, f32[4,8,1024]{2,1,0:T(8,128)S(1)}, f32[4,1024]{1,0:T(4,128)S(1)}, bf16[4,256,1024]{2,1,0:T(8,128)(2,1)S(1)}, bf16[16,256,256]{2,1,0:T(8,128)(2,1)S(1)}) custom-call(f32[4,8,1024]{2,1,0:T(8,128)} %x_hbm.1, f32[4,1024]{1,0:T(4,128)} %e_hbm.1, bf16[4,256,1024]{2,1,0:T(8,128)(2,1)} %c_hbm.1, ...), custom_call_target="tpu_custom_call" | custom-call | tf_op jit(solution)/shard_map/pallas_call | solution.py:473
  3.1 17.8 %all_to_all.25 = bf16[32,9,4,128]{3,2,1,0:T(4,128)(2,1)S(1)} all-to-all(bf16[32,9,4,128]{3,2,1,0:T(4,128)(2,1)S(1)} %bitcast.15), channel_id=1, replica_groups=mesh['grp'=8,'tile'=4] {'grp','tile'}, dimensions={0} | all-to-all | bytes 589824 | tf_op jit(solution)/shard_map/all_to_all | solution.py:503
  20.9 0.4 shard_map.86
  21.3 0.6 collective-permute-start
  21.9 0.7 shard_map.87.small_ref
  22.7 0.3 collective-permute-done.other_ref
  22.9 2.3 %shard_map.88 = (f32[32,8,128]{2,1,0:T(8,128)S(1)}, f32[32,8,128]{2,1,0:T(8,128)S(1)}, f32[2,32,8,128]{3,2,1,0:T(8,128)S(1)}, bf16[16,256,256]{2,1,0:T(8,128)(2,1)S(1)}) custom-call(s32[32]{0:T(128)} %assign_hbm.3, s32[32,32]{1,0:T(8,128)} %ranks_hbm.3, bf16[16,256,256]{2,1,0:T(8,128)(2,1)S(1)} %get-tuple-element.34.head_ref, ...), custom_call_target="tpu_custom_call" | custom-call | tf_op jit(solution)/shard_map/pallas_call | solution.py:473
  25.2 0.4 collective-permute-start.1
  25.7 0.7 shard_map.89
  26.4 0.3 collective-permute-done.1.recv_ref
  26.6 0.1 shard_map.90
  26.7 13.2 %all_to_all.26 = bf16[32,9,4,128]{3,2,1,0:T(4,128)(2,1)S(1)} all-to-all(bf16[32,9,4,128]{3,2,1,0:T(4,128)(2,1)S(1)} %bitcast.10), channel_id=1, replica_groups=mesh['grp'=8,'tile'=4] {'grp','tile'}, dimensions={0} | all-to-all | bytes 589824 | tf_op jit(solution)/shard_map/all_to_all | solution.py:503
  40.0 1.5 %shard_map.91 = (bf16[4,2,4,9,4,128]{5,4,3,2,1,0:T(4,128)(2,1)S(1)}, f32[4,8,1024]{2,1,0:T(8,128)S(1)}, f32[4,8,1024]{2,1,0:T(8,128)S(1)}, f32[8,128]{1,0:T(8,128)S(1)}) custom-call(bf16[4,2,4,9,4,128]{5,4,3,2,1,0:T(4,128)(2,1)S(1)} %bitcast.8, f32[4,8,1024]{2,1,0:T(8,128)S(1)} %get-tuple-element.43.x_ref, f32[4,1024]{1,0:T(4,128)S(1)} %get-tuple-element.44.e_ref, ...), custom_call_target="tpu_custom_call" | custom-call | tf_op jit(solution)/shard_map/pallas_call | solution.py:473
  41.4 13.4 %all_to_all.27 = bf16[32,9,4,128]{3,2,1,0:T(4,128)(2,1)S(1)} all-to-all(bf16[32,9,4,128]{3,2,1,0:T(4,128)(2,1)S(1)} %bitcast.14), channel_id=1, replica_groups=mesh['grp'=8,'tile'=4] {'grp','tile'}, dimensions={0} | all-to-all | bytes 589824 | tf_op jit(solution)/shard_map/all_to_all | solution.py:503
  54.8 0.1 shard_map.92
  54.9 0.6 collective-permute-start.2
  55.5 1.1 %shard_map.93.small_ref = f32[2,8,128]{2,1,0:T(8,128)S(1)} custom-call(f32[4,128]{1,0:T(4,128)S(1)} %get-tuple-element.49.moments_ref), custom_call_target="tpu_custom_call" | custom-call | tf_op jit(solution)/shard_map/pallas_call | solution.py:473
  56.6 0.0 collective-permute-done.2.other_ref
  56.6 2.3 %shard_map.94 = (f32[32,8,128]{2,1,0:T(8,128)S(1)}, f32[32,8,128]{2,1,0:T(8,128)S(1)}, f32[2,32,8,128]{3,2,1,0:T(8,128)S(1)}) custom-call(s32[32]{0:T(128)} %assign_hbm.3, s32[32,32]{1,0:T(8,128)} %ranks_hbm.3, bf16[16,256,256]{2,1,0:T(8,128)(2,1)S(1)} %get-tuple-element.34.head_ref, bf16[16,256,256]{2,1,0:T(8,128)(2,1)S(1)} %get-tuple-element.38.tail_ref, ...), custom_call_target="tpu_custom_call" | custom-call | tf_op jit(solution)/shard_map/pallas_call | solution.py:473
  59.0 0.3 collective-permute-start.3
  59.2 1.0 %shard_map.95 = (bf16[4,128]{1,0:T(4,128)(2,1)S(1)}, f32[8,128]{1,0:T(8,128)S(1)}) custom-call(f32[32,8,128]{2,1,0:T(8,128)S(1)} %get-tuple-element.50.keep_ref, f32[32,8,128]{2,1,0:T(8,128)S(1)} %get-tuple-element.51.send_ref, f32[2,32,8,128]{3,2,1,0:T(8,128)S(1)} %get-tuple-element.52.dens_ref, f32[4,128]{1,0:T(4,128)S(1)} %get-tuple-element.49.moments_ref, ...), custom_call_target="tpu_custom_call" | custom-call | tf_op jit(solution)/shard_map/pallas_call | solution.py:473
  60.3 0.1 collective-permute-done.3.recv_ref
  60.4 0.1 shard_map.96
  60.5 13.1 %all_to_all.28 = bf16[32,9,4,128]{3,2,1,0:T(4,128)(2,1)S(1)} all-to-all(bf16[32,9,4,128]{3,2,1,0:T(4,128)(2,1)S(1)} %bitcast.12), channel_id=1, replica_groups=mesh['grp'=8,'tile'=4] {'grp','tile'}, dimensions={0} | all-to-all | bytes 589824 | tf_op jit(solution)/shard_map/all_to_all | solution.py:503
  73.6 1.3 %shard_map.97 = (f32[32,1,128]{2,1,0:T(1,128)S(1)}, f32[4,8,1024]{2,1,0:T(8,128)}, f32[4,8,1024]{2,1,0:T(8,128)S(1)}, f32[4,8,1024]{2,1,0:T(8,128)S(1)}, f32[8,128]{1,0:T(8,128)S(1)}) custom-call(bf16[4,2,4,9,4,128]{5,4,3,2,1,0:T(4,128)(2,1)S(1)} %bitcast.13, f32[4,8,1024]{2,1,0:T(8,128)S(1)} %get-tuple-element.54.v_ref, ...), custom_call_target="tpu_custom_call" | custom-call | tf_op jit(solution)/shard_map/pallas_call | solution.py:473
  74.9 9.9 %all_to_all.29.recv_ref = f32[32,1,128]{2,1,0:T(1,128)S(1)} all-to-all(f32[32,1,128]{2,1,0:T(1,128)S(1)} %get-tuple-element.57), channel_id=1, replica_groups=mesh['grp'=8,'tile'=4] {'grp','tile'}, dimensions={0} | all-to-all | bytes 32768 | tf_op jit(solution)/shard_map/all_to_all | solution.py:583
  84.8 1.9 %shard_map.98 = (f32[4,8,1024]{2,1,0:T(8,128)}, f32[2,8,8]{2,1,0:T(8,128)}) custom-call(f32[32,1,128]{2,1,0:T(1,128)S(1)} %all_to_all.29.recv_ref, f32[4,8,1024]{2,1,0:T(8,128)S(1)} %get-tuple-element.58.q_ref, f32[4,8,1024]{2,1,0:T(8,128)S(1)} %get-tuple-element.59.b_ref, f32[8,128]{1,0:T(8,128)S(1)} %get-tuple-element.60.ray0_ref, ...), custom_call_target="tpu_custom_call" | custom-call | tf_op jit(solution)/shard_map/pallas_call | solution.py:473
Async XLA Ops:
  21.3 1.6 %collective-permute-start = (f32[32,8,128]{2,1,0:T(8,128)S(1)}, f32[32,8,128]{2,1,0:T(8,128)S(1)}, u32[]{:S(2)}, u32[]{:S(2)}) collective-permute-start(f32[32,8,128]{2,1,0:T(8,128)S(1)} %get-tuple-element.36.mine_ref), channel_id=1, source_target_pairs={{0,4},{4,0},{8,12},{12,8},{16,20},{20,16},{24,28},{28,24},{1,5},{5... | collective-permute-start | bytes 393224 | tf_op jit(solution)/shard_map/ppermute | solution.py:508
  25.2 1.4 %collective-permute-start.1 = (f32[32,8,128]{2,1,0:T(8,128)S(1)}, f32[32,8,128]{2,1,0:T(8,128)S(1)}, u32[]{:S(2)}, u32[]{:S(2)}) collective-permute-start(f32[32,8,128]{2,1,0:T(8,128)S(1)} %get-tuple-element.40.send_ref), channel_id=1, source_target_pairs={{0,4},{4,0},{8,12},{12,8},{16,20},{20,16},{24,28},{28,24},{1,5},{5... | collective-permute-start | bytes 393224 | tf_op jit(solution)/shard_map/ppermute | solution.py:559
  54.9 1.7 %collective-permute-start.2 = (f32[32,8,128]{2,1,0:T(8,128)S(1)}, f32[32,8,128]{2,1,0:T(8,128)S(1)}, u32[]{:S(2)}, u32[]{:S(2)}) collective-permute-start(f32[32,8,128]{2,1,0:T(8,128)S(1)} %get-tuple-element.48.mine_ref), channel_id=1, source_target_pairs={{0,4},{4,0},{8,12},{12,8},{16,20},{20,16},{24,28},{28,24},{1,5},{5... | collective-permute-start | bytes 393224 | tf_op jit(solution)/shard_map/ppermute | solution.py:508
  59.0 1.4 %collective-permute-start.3 = (f32[32,8,128]{2,1,0:T(8,128)S(1)}, f32[32,8,128]{2,1,0:T(8,128)S(1)}, u32[]{:S(2)}, u32[]{:S(2)}) collective-permute-start(f32[32,8,128]{2,1,0:T(8,128)S(1)} %get-tuple-element.51.send_ref), channel_id=1, source_target_pairs={{0,4},{4,0},{8,12},{12,8},{16,20},{20,16},{24,28},{28,24},{1,5},{5... | collective-permute-start | bytes 393224 | tf_op jit(solution)/shard_map/ppermute | solution.py:572

commit v9 on v8

--- a/solution.py
+++ b/solution.py
@@ -200,10 +200,14 @@
             lower = pltpu.roll(lower, (lanes + (t - 2) * v) % lanes, 1)
             factors = lower if factors is None else factors + lower
         left = jnp.concatenate(split2(factors[:, : tiles * v]), 0)
+        columns = []
         for k in range(local_k):
             sent = [mine_ref[g, t, 2 * k + i].astype(F4) for t in range(tiles) for i in range(2)]
-            both = mm(left, jnp.concatenate(sent, 0).astype(BF), NN)
-            dens_ref[g * local_k + k] = both[:v] + both[v:]
+            columns.append(jnp.concatenate(sent, 0).astype(BF))
+        both = mm(left, jnp.concatenate(columns, 1), NN)
+        both = both[:v] + both[v:]
+        for k in range(local_k):
+            dens_ref[g * local_k + k] = both[:, k * lanes : (k + 1) * lanes]
     moments_ref[...] = moments
 
 

time: 87 us -> 86.9 us (level)
  no operation moved by 1% of the time
where the time goes in v9:
time: 86.9 us; the launch traced here: 86.7 us
  blocking collectives  67.4 us (78%)
  Pallas kernels  16 us (18%)
  starting transfers between devices  1.87 us (2%)
    all_to_all x4, blocking collectives, exchange(): lax.all_to_all(sent, axes, 0, 0, tiled=True).reshape(shape + sent.shape[1:])  57.5 us
    pallas_call x14, Pallas kernels, call(): pl.pallas_call(body, out_shape=outs, in_specs=ins, out_specs=specs, scrat...  16 us
    all_to_all x1, blocking collectives, per_device(): got = lax.all_to_all(sent, axes, 0, 0, tiled=True)  9.89 us
  transfers between devices with their start and end apart: 4, of which 3 were waited for; matrix products, arithmetic and copies ran while one was open for 0% of the time, Pallas kernels for 4%

profile of v9, /device:TPU:0, one launch (start us, length us, event | category | flops | bytes accessed | tf_op | source)
XLA Modules:
  0.0 86.7 jit_solution(16378649660125480195)
XLA Ops:
  0.6 2.4 %shard_map.85 = (bf16[4,2,4,9,4,128]{5,4,3,2,1,0:T(4,128)(2,1)S(1)}, f32[4,8,1024]{2,1,0:T(8,128)S(1)}, f32[4,1024]{1,0:T(4,128)S(1)}, bf16[4,256,1024]{2,1,0:T(8,128)(2,1)S(1)}, bf16[16,256,256]{2,1,0:T(8,128)(2,1)S(1)}) custom-call(f32[4,8,1024]{2,1,0:T(8,128)} %x_hbm.1, f32[4,1024]{1,0:T(4,128)} %e_hbm.1, bf16[4,256,1024]{2,1,0:T(8,128)(2,1)} %c_hbm.1, ...), custom_call_target="tpu_custom_call" | custom-call | tf_op jit(solution)/shard_map/pallas_call | solution.py:477
  3.1 17.8 %all_to_all.25 = bf16[32,9,4,128]{3,2,1,0:T(4,128)(2,1)S(1)} all-to-all(bf16[32,9,4,128]{3,2,1,0:T(4,128)(2,1)S(1)} %bitcast.15), channel_id=1, replica_groups=mesh['grp'=8,'tile'=4] {'grp','tile'}, dimensions={0} | all-to-all | bytes 589824 | tf_op jit(solution)/shard_map/all_to_all | solution.py:507
  20.9 0.4 shard_map.86
  21.3 0.6 collective-permute-start
  21.9 0.7 shard_map.87.small_ref
  22.6 0.3 collective-permute-done.other_ref
  22.9 2.3 %shard_map.88 = (f32[32,8,128]{2,1,0:T(8,128)S(1)}, f32[32,8,128]{2,1,0:T(8,128)S(1)}, f32[2,32,8,128]{3,2,1,0:T(8,128)S(1)}, bf16[16,256,256]{2,1,0:T(8,128)(2,1)S(1)}) custom-call(s32[32]{0:T(128)} %assign_hbm.3, s32[32,32]{1,0:T(8,128)} %ranks_hbm.3, bf16[16,256,256]{2,1,0:T(8,128)(2,1)S(1)} %get-tuple-element.34.head_ref, ...), custom_call_target="tpu_custom_call" | custom-call | tf_op jit(solution)/shard_map/pallas_call | solution.py:477
  25.2 0.4 collective-permute-start.1
  25.6 0.7 shard_map.89
  26.3 0.3 collective-permute-done.1.recv_ref
  26.6 0.1 shard_map.90
  26.7 13.2 %all_to_all.26 = bf16[32,9,4,128]{3,2,1,0:T(4,128)(2,1)S(1)} all-to-all(bf16[32,9,4,128]{3,2,1,0:T(4,128)(2,1)S(1)} %bitcast.10), channel_id=1, replica_groups=mesh['grp'=8,'tile'=4] {'grp','tile'}, dimensions={0} | all-to-all | bytes 589824 | tf_op jit(solution)/shard_map/all_to_all | solution.py:507
  39.9 1.5 %shard_map.91 = (bf16[4,2,4,9,4,128]{5,4,3,2,1,0:T(4,128)(2,1)S(1)}, f32[4,8,1024]{2,1,0:T(8,128)S(1)}, f32[4,8,1024]{2,1,0:T(8,128)S(1)}, f32[8,128]{1,0:T(8,128)S(1)}) custom-call(bf16[4,2,4,9,4,128]{5,4,3,2,1,0:T(4,128)(2,1)S(1)} %bitcast.8, f32[4,8,1024]{2,1,0:T(8,128)S(1)} %get-tuple-element.43.x_ref, f32[4,1024]{1,0:T(4,128)S(1)} %get-tuple-element.44.e_ref, ...), custom_call_target="tpu_custom_call" | custom-call | tf_op jit(solution)/shard_map/pallas_call | solution.py:477
  41.4 13.4 %all_to_all.27 = bf16[32,9,4,128]{3,2,1,0:T(4,128)(2,1)S(1)} all-to-all(bf16[32,9,4,128]{3,2,1,0:T(4,128)(2,1)S(1)} %bitcast.14), channel_id=1, replica_groups=mesh['grp'=8,'tile'=4] {'grp','tile'}, dimensions={0} | all-to-all | bytes 589824 | tf_op jit(solution)/shard_map/all_to_all | solution.py:507
  54.8 0.1 shard_map.92
  54.9 0.6 collective-permute-start.2
  55.4 1.1 %shard_map.93.small_ref = f32[2,8,128]{2,1,0:T(8,128)S(1)} custom-call(f32[4,128]{1,0:T(4,128)S(1)} %get-tuple-element.49.moments_ref), custom_call_target="tpu_custom_call" | custom-call | tf_op jit(solution)/shard_map/pallas_call | solution.py:477
  56.6 0.0 collective-permute-done.2.other_ref
  56.6 2.3 %shard_map.94 = (f32[32,8,128]{2,1,0:T(8,128)S(1)}, f32[32,8,128]{2,1,0:T(8,128)S(1)}, f32[2,32,8,128]{3,2,1,0:T(8,128)S(1)}) custom-call(s32[32]{0:T(128)} %assign_hbm.3, s32[32,32]{1,0:T(8,128)} %ranks_hbm.3, bf16[16,256,256]{2,1,0:T(8,128)(2,1)S(1)} %get-tuple-element.34.head_ref, bf16[16,256,256]{2,1,0:T(8,128)(2,1)S(1)} %get-tuple-element.38.tail_ref, ...), custom_call_target="tpu_custom_call" | custom-call | tf_op jit(solution)/shard_map/pallas_call | solution.py:477
  58.9 0.3 collective-permute-start.3
  59.2 1.0 %shard_map.95 = (bf16[4,128]{1,0:T(4,128)(2,1)S(1)}, f32[8,128]{1,0:T(8,128)S(1)}) custom-call(f32[32,8,128]{2,1,0:T(8,128)S(1)} %get-tuple-element.50.keep_ref, f32[32,8,128]{2,1,0:T(8,128)S(1)} %get-tuple-element.51.send_ref, f32[2,32,8,128]{3,2,1,0:T(8,128)S(1)} %get-tuple-element.52.dens_ref, f32[4,128]{1,0:T(4,128)S(1)} %get-tuple-element.49.moments_ref, ...), custom_call_target="tpu_custom_call" | custom-call | tf_op jit(solution)/shard_map/pallas_call | solution.py:477
  60.2 0.1 collective-permute-done.3.recv_ref
  60.3 0.1 shard_map.96
  60.4 13.1 %all_to_all.28 = bf16[32,9,4,128]{3,2,1,0:T(4,128)(2,1)S(1)} all-to-all(bf16[32,9,4,128]{3,2,1,0:T(4,128)(2,1)S(1)} %bitcast.12), channel_id=1, replica_groups=mesh['grp'=8,'tile'=4] {'grp','tile'}, dimensions={0} | all-to-all | bytes 589824 | tf_op jit(solution)/shard_map/all_to_all | solution.py:507
  73.5 1.3 %shard_map.97 = (f32[32,1,128]{2,1,0:T(1,128)S(1)}, f32[4,8,1024]{2,1,0:T(8,128)}, f32[4,8,1024]{2,1,0:T(8,128)S(1)}, f32[4,8,1024]{2,1,0:T(8,128)S(1)}, f32[8,128]{1,0:T(8,128)S(1)}) custom-call(bf16[4,2,4,9,4,128]{5,4,3,2,1,0:T(4,128)(2,1)S(1)} %bitcast.13, f32[4,8,1024]{2,1,0:T(8,128)S(1)} %get-tuple-element.54.v_ref, ...), custom_call_target="tpu_custom_call" | custom-call | tf_op jit(solution)/shard_map/pallas_call | solution.py:477
  74.8 9.9 %all_to_all.29.recv_ref = f32[32,1,128]{2,1,0:T(1,128)S(1)} all-to-all(f32[32,1,128]{2,1,0:T(1,128)S(1)} %get-tuple-element.57), channel_id=1, replica_groups=mesh['grp'=8,'tile'=4] {'grp','tile'}, dimensions={0} | all-to-all | bytes 32768 | tf_op jit(solution)/shard_map/all_to_all | solution.py:587
  84.7 1.9 %shard_map.98 = (f32[4,8,1024]{2,1,0:T(8,128)}, f32[2,8,8]{2,1,0:T(8,128)}) custom-call(f32[32,1,128]{2,1,0:T(1,128)S(1)} %all_to_all.29.recv_ref, f32[4,8,1024]{2,1,0:T(8,128)S(1)} %get-tuple-element.58.q_ref, f32[4,8,1024]{2,1,0:T(8,128)S(1)} %get-tuple-element.59.b_ref, f32[8,128]{1,0:T(8,128)S(1)} %get-tuple-element.60.ray0_ref, ...), custom_call_target="tpu_custom_call" | custom-call | tf_op jit(solution)/shard_map/pallas_call | solution.py:477
Async XLA Ops:
  21.3 1.6 %collective-permute-start = (f32[32,8,128]{2,1,0:T(8,128)S(1)}, f32[32,8,128]{2,1,0:T(8,128)S(1)}, u32[]{:S(2)}, u32[]{:S(2)}) collective-permute-start(f32[32,8,128]{2,1,0:T(8,128)S(1)} %get-tuple-element.36.mine_ref), channel_id=1, source_target_pairs={{0,4},{4,0},{8,12},{12,8},{16,20},{20,16},{24,28},{28,24},{1,5},{5... | collective-permute-start | bytes 393224 | tf_op jit(solution)/shard_map/ppermute | solution.py:512
  25.2 1.4 %collective-permute-start.1 = (f32[32,8,128]{2,1,0:T(8,128)S(1)}, f32[32,8,128]{2,1,0:T(8,128)S(1)}, u32[]{:S(2)}, u32[]{:S(2)}) collective-permute-start(f32[32,8,128]{2,1,0:T(8,128)S(1)} %get-tuple-element.40.send_ref), channel_id=1, source_target_pairs={{0,4},{4,0},{8,12},{12,8},{16,20},{20,16},{24,28},{28,24},{1,5},{5... | collective-permute-start | bytes 393224 | tf_op jit(solution)/shard_map/ppermute | solution.py:563
  54.9 1.7 %collective-permute-start.2 = (f32[32,8,128]{2,1,0:T(8,128)S(1)}, f32[32,8,128]{2,1,0:T(8,128)S(1)}, u32[]{:S(2)}, u32[]{:S(2)}) collective-permute-start(f32[32,8,128]{2,1,0:T(8,128)S(1)} %get-tuple-element.48.mine_ref), channel_id=1, source_target_pairs={{0,4},{4,0},{8,12},{12,8},{16,20},{20,16},{24,28},{28,24},{1,5},{5... | collective-permute-start | bytes 393224 | tf_op jit(solution)/shard_map/ppermute | solution.py:512
  58.9 1.4 %collective-permute-start.3 = (f32[32,8,128]{2,1,0:T(8,128)S(1)}, f32[32,8,128]{2,1,0:T(8,128)S(1)}, u32[]{:S(2)}, u32[]{:S(2)}) collective-permute-start(f32[32,8,128]{2,1,0:T(8,128)S(1)} %get-tuple-element.51.send_ref), channel_id=1, source_target_pairs={{0,4},{4,0},{8,12},{12,8},{16,20},{20,16},{24,28},{28,24},{1,5},{5... | collective-permute-start | bytes 393224 | tf_op jit(solution)/shard_map/ppermute | solution.py:576
